TPU v7x, 256 devices: a whole 4x4x8 slice. The times are simulated.
256 devices in a mesh: comp: 64 (over x, y_lo, z), gy: 2 (over y_hi), gx: 2 (over core).
Axes of the slice: x: 4, y: 4 (y_hi: 2, y_lo: 2; y = y_hi * 2 + y_lo), z: 8, core: 2. Of those that a mesh axis runs over, the one named last changes fastest.
Arguments:
- flow_fields: float32 [4, 6, 2048, 384], P(None, None, ('comp', 'gy', 'gx')), may hold values from -6 to 6
- chlorophyll_lag: float32 [6, 2048, 384], P(None, ('comp', 'gy', 'gx')), may hold values from 0.1 to 3
- tracers: float32 [16, 6, 2048, 128], P(None, None, ('comp', 'gy', 'gx')), may hold values from -6 to 6
- forcing: float32 [4, 6, 2048, 128], P(None, None, ('comp', 'gy', 'gx')), may hold values from -6 to 6
- ocean_mask: int32 [512, 384], replicated, may hold values 0 or 1
- bottom: int32 [512, 384], replicated, may hold values from 1 to 6
- reaction: float32 [16, 16], replicated, may hold values from -1.5 to 0.1
Outputs:
- flow_out: float32 [4, 6, 2048, 384], P(None, None, ('comp', 'gy', 'gx'))
- light_out: float32 [6, 2048, 384], P(None, ('comp', 'gy', 'gx'))
- tracers_out: float32 [16, 6, 2048, 128], P(None, None, ('comp', 'gy', 'gx'))
- forcing_out: float32 [4, 6, 2048, 128], P(None, None, ('comp', 'gy', 'gx'))
All inputs are finite; a program needn't handle non-finite values.
Results may differ from a plain program's by a relative error of at most 0.0002.
Values sent between devices are 32-bit elements; how exact they have to be, the bound alone decides.
No kernel may reach another device: no remote copies, remote signals or barrier semaphores. Data moves between devices by JAX's collectives and lax.ppermute only.
A program may use at most 64 MiB of HBM per device.

v0:
```python
import jax
import jax.numpy as jnp
from jax import lax
from jax.experimental import pallas as pl
from jax.experimental.pallas import tpu as pltpu
from jax.sharding import PartitionSpec as P

AXES = ("comp", "gy", "gx")
SECTIONS = 4
DT = 0.1
F32 = jnp.float32
VMEM_LIMIT = 48 * 1024 * 1024


def place():
    gy = lax.axis_size("gy")
    gx = lax.axis_size("gx")
    total = lax.axis_size("comp") * gy * gx
    group = total // SECTIONS
    position = (lax.axis_index("comp") * gy + lax.axis_index("gy")) * gx + lax.axis_index("gx")
    moved = lax.rem(position + 1, total)
    return moved // group, lax.rem(moved, group), group


def lanes(rows):
    return lax.broadcasted_iota(jnp.int32, (rows, 128), 1)


def roll_lanes(x, by):
    by = by % 128
    return x if by == 0 else pltpu.roll(x, by, 1)


def swap(x):
    return pltpu.roll(x, 4, 0)


def upper_half():
    return lax.broadcasted_iota(jnp.int32, (8, 128), 0) < 4


def spread(flag):
    return jnp.where(flag, 1.0, 0.0).astype(F32)


def mask_kernel(ocean, bottom, out, ocean_rows, bottom_rows, sems):
    _, strip, group = place()
    starts = [jnp.maximum(strip - 1, 0), strip, jnp.minimum(strip + 1, group - 1)]
    copies = []
    for i, start in enumerate(starts):
        rows = pl.ds(pl.multiple_of(start * 8, 8), 8)
        copies.append(pltpu.make_async_copy(ocean.at[rows], ocean_rows.at[i], sems.at[i]))
        copies.append(pltpu.make_async_copy(bottom.at[rows], bottom_rows.at[i], sems.at[3 + i]))
    for copy in copies:
        copy.start()
    for copy in copies:
        copy.wait()
    inside = [(strip > 0).astype(jnp.int32), 1, (strip < group - 1).astype(jnp.int32)]
    for i in range(3):
        out[8 * i : 8 * i + 8] = jnp.where(ocean_rows[i] == 1, bottom_rows[i], 0) * inside[i]


def edge_tile(planes):
    lane = lanes(planes[0].shape[0])
    edges = jnp.zeros_like(planes[0])
    for a, x in enumerate(planes):
        edges = jnp.where(lane == a, roll_lanes(x, a + 1), edges)
        edges = jnp.where(lane == 64 + a, roll_lanes(x, 64 + a), edges)
    return edges


def edges_kernel(tracers, forcing, out):
    nt = tracers.shape[0]

    def level(l, carry):
        out[l] = edge_tile([tracers[a, l] for a in range(nt)] + [forcing[1, l]])
        return carry

    lax.fori_loop(0, tracers.shape[1], level, 0)


def open_edges(section, from_left, from_right, rows):
    lane = lanes(rows)
    return jnp.where(
        lane < 64, from_left * spread(section > 0), from_right * spread(section < 2)
    )


def rows_kernel(flow, pigment, tracers, forcing, from_left, from_right, to_next, to_prev, edges):
    section, _, _ = place()
    levels = pigment.shape[0]
    nt = tracers.shape[0]

    @pl.when(section == 3)
    def _():
        def level(l, carry):
            for f in range(5):
                for j in range(3):
                    cols = slice(128 * j, 128 * j + 128)
                    tile = flow[f, l, :, cols] if f < 4 else pigment[l, :, cols]
                    to_next[3 * f + j, l] = tile
                    to_prev[3 * f + j, l] = tile
            return carry

        lax.fori_loop(0, levels, level, 0)
        edges[...] = jnp.zeros_like(edges)

    @pl.when(section != 3)
    def _():
        half = upper_half()
        for l in range(levels):
            edges[l] = open_edges(section, from_left[l], from_right[l], 8)

        def put(plane, pair, even, odd):
            row, col = plane // 2, 3 * (plane % 2)
            to_next[row, col + pair] = jnp.where(half, swap(even), odd)
            to_prev[row, col + pair] = jnp.where(half, even, swap(odd))

        for pair in range(3):
            even, odd = 2 * pair, 2 * pair + 1
            for a in range(nt):
                put(a, pair, tracers[a, even], tracers[a, odd])
            put(nt, pair, forcing[0, even], forcing[0, odd])
            put(nt + 1, pair, forcing[1, even], forcing[1, odd])
            growth = [jnp.exp(0.1 * forcing[2, l] - 0.05 * forcing[3, l]) for l in (even, odd)]
            put(nt + 2, pair, growth[0], growth[1])
            put(nt + 3, pair, edges[even], edges[odd])
        for row in range(10, 15):
            for l in range(levels):
                to_next[row, l] = jnp.zeros((8, 128), F32)
                to_prev[row, l] = jnp.zeros((8, 128), F32)


def shifted(tiles):
    lane = lanes(tiles[0].shape[0])
    left = [roll_lanes(x, 127) for x in tiles]
    right = [roll_lanes(x, 1) for x in tiles]
    count = len(tiles)
    east = [
        jnp.where(lane == 127, left[j + 1] if j + 1 < count else 0.0, left[j]) for j in range(count)
    ]
    west = [jnp.where(lane == 0, right[j - 1] if j > 0 else 0.0, right[j]) for j in range(count)]
    return east, west


def substep(source, target, heat, wet_rows, tiles, read_at, write_at, heat_at, wet_at):
    levels = heat.shape[0]
    thirds = 3
    for tile in range(tiles):
        row = read_at + 8 * tile
        put = write_at + 8 * tile
        floors = [
            wet_rows[wet_at + 8 * tile : wet_at + 8 * tile + 8, 128 * j : 128 * j + 128]
            for j in range(thirds)
        ]

        def level(l, carry, row=row, put=put, tile=tile, floors=floors):
            slope_x, slope_y = carry

            def load(f, by):
                return [
                    source[f, l, row + by : row + by + 8, 128 * j : 128 * j + 128]
                    for j in range(thirds)
                ]

            centre = [load(f, 0) for f in range(4)]
            up = [load(f, -1) for f in range(4)]
            down = [load(f, 1) for f in range(4)]
            sides = [shifted(centre[f]) for f in range(4)]
            new_x, new_y = [], []
            for j in range(thirds):
                u, v, t, s = (centre[f][j] for f in range(4))
                un, vn, tn, sn = (up[f][j] for f in range(4))
                us, vs, ts, ss = (down[f][j] for f in range(4))
                ue, ve, te, se = (sides[f][0][j] for f in range(4))
                uw, vw, tw, sw = (sides[f][1][j] for f in range(4))
                px = slope_x[j] + ((ss - sn) - (ts - tn))
                py = slope_y[j] + ((se - sw) - (te - tw))
                new_x.append(px)
                new_y.append(py)
                is_wet = floors[j] > l
                a = 0.05 - 0.05 * us
                b = 0.05 + 0.05 * un
                c = 0.05 - 0.05 * ve
                d = 0.05 + 0.05 * vw
                cols = slice(128 * j, 128 * j + 128)
                h = heat[l, heat_at + 8 * tile : heat_at + 8 * tile + 8, cols]
                results = (
                    0.79 * u + 0.1 * v - 0.01 * px + 0.05 * ((un + us) + (ue + uw)),
                    0.79 * v - 0.1 * u - 0.01 * py + 0.05 * ((vn + vs) + (ve + vw)),
                    (0.8 * t + h) + ((ts * a + tn * b) + (te * c + tw * d)),
                    0.8 * s + ((ss * a + sn * b) + (se * c + sw * d)),
                )
                for f in range(4):
                    target[f, l, put : put + 8, cols] = jnp.where(is_wet, results[f], 0.0)
            return new_x, new_y

        zero = [jnp.zeros((8, 128), F32) for _ in range(thirds)]
        lax.fori_loop(0, levels, level, (zero, zero))


def fill_heat(load, heat):
    levels, rows = heat.shape[0], heat.shape[1]
    for tile in range(rows // 8):
        for j in range(3):
            optical = jnp.zeros((8, 128), F32)
            light = jnp.ones((8, 128), F32)
            for l in range(levels):
                optical = optical + (0.05 + 0.3 * load(l, tile, j))
                lower = jnp.exp(-optical)
                heat[l, 8 * tile : 8 * tile + 8, 128 * j : 128 * j + 128] = (5.0 * DT) * (
                    light - lower
                )
                light = lower


def extend(own, above, below, half):
    turned = swap(own)
    return jnp.concatenate([jnp.where(half, above, turned), jnp.where(half, turned, below)], axis=0)


def tracer_weights(u_up, u_down, v_east, v_west, growth, is_wet):
    wet = spread(is_wet)
    scale = wet * 0.05
    return (
        scale - scale * u_down,
        scale + scale * u_up,
        scale - scale * v_east,
        scale + scale * v_west,
        wet * 0.8,
        (wet * DT) * growth,
    )


def tracer_level(centre, up, down, edges, weights, reaction):
    nt = len(centre)
    lane = lanes(edges.shape[0])
    a, b, c, d, keep, grow = weights
    results = []
    for i in range(nt):
        east = jnp.where(lane == 127, roll_lanes(edges, 63 - i), roll_lanes(centre[i], 127))
        west = jnp.where(lane == 0, roll_lanes(edges, -i), roll_lanes(centre[i], 1))
        mixed = reaction[i, 0] * centre[0]
        for k in range(1, nt):
            mixed = mixed + reaction[i, k] * centre[k]
        results.append(
            (keep * centre[i] + grow * mixed)
            + ((down[i] * a + up[i] * b) + (east * c + west * d))
        )
    return results


def pigment_of(first, second):
    return 0.25 * (first * first + second * second)


def first_kernel(
    flow, pigment, tracers, forcing, edges, above, below, wet_rows, reaction,
    out_a, out_b, out_c, flow_next, tracers_next, buffers, heat, cells, winds,
):
    section, strip, group = place()
    levels = pigment.shape[0]
    nt = tracers.shape[0]
    low = spread(strip > 0)
    high = spread(strip < group - 1)

    @pl.when(section == 3)
    def _():
        def fill(l, carry):
            for f in range(4):
                for j in range(3):
                    cols = slice(128 * j, 128 * j + 128)
                    buffers[0, f, l, 8:16, cols] = above[3 * f + j, l] * low
                    buffers[0, f, l, 16:24, cols] = flow[f, l, :, cols]
                    buffers[0, f, l, 24:32, cols] = below[3 * f + j, l] * high
            return carry

        lax.fori_loop(0, levels, fill, 0)

        def load(l, tile, j):
            if tile == 1:
                return pigment[l, :, 128 * j : 128 * j + 128]
            return (above if tile == 0 else below)[12 + j, l]

        fill_heat(load, heat)
        for n in range(3):
            substep(buffers.at[n], buffers.at[n + 1], heat, wet_rows, 3, 8, 8, 0, 0)
        substep(buffers.at[3], flow_next, heat, wet_rows, 2, 12, 8, 4, 4)
        lane = lanes(8)
        outs = (out_a, out_b, out_c)
        sub = lax.broadcasted_iota(jnp.int32, (8, 128), 0)

        def mean(f, l, row, cols):
            total = buffers[1, f, l, row : row + 8, cols] + buffers[2, f, l, row : row + 8, cols]
            total = total + buffers[3, f, l, row : row + 8, cols]
            return 0.25 * (total + flow_next[f, l, row - 4 : row + 4, cols])

        edge_v = [jnp.zeros((8, 128), F32) for _ in range(3)]
        rows_above = [jnp.zeros((8, 128), F32) for _ in range(3)]
        rows_below = [jnp.zeros((8, 128), F32) for _ in range(3)]
        for l in range(levels):
            v_mean = []
            for j in range(3):
                cols = slice(128 * j, 128 * j + 128)
                outs[j][l] = mean(0, l, 16, cols)
                v_mean.append(mean(1, l, 16, cols))
                outs[j][6 + l] = v_mean[j]
                warm = flow_next[2, l, 12:20, cols]
                salt = flow_next[3, l, 12:20, cols]
                outs[j][12 + l] = jnp.exp(0.1 * warm - 0.05 * salt)
                first = mean(0, l, 15, cols)
                last = mean(0, l, 17, cols)
                rows_above[j] = jnp.where(sub == l, roll_rows(first, l), rows_above[j])
                rows_below[j] = jnp.where(sub == l, roll_rows(last, l + 1), rows_below[j])
            for j in range(3):
                if j > 0:
                    edge_v[j] = jnp.where(
                        lane == 2 * l, roll_lanes(v_mean[j - 1], 2 * l + 1), edge_v[j]
                    )
                if j < 2:
                    edge_v[j] = jnp.where(
                        lane == 2 * l + 1, roll_lanes(v_mean[j + 1], 2 * l + 1), edge_v[j]
                    )
        for j in range(3):
            outs[j][18] = edge_v[j]
            outs[j][19] = rows_above[j]
            outs[j][20] = rows_below[j]
            for i in range(21, 24):
                outs[j][i] = jnp.zeros((8, 128), F32)

    @pl.when(section != 3)
    def _():
        half = upper_half()

        def halo(message, plane, pair, odd, upward):
            tile = message[plane // 2, 3 * (plane % 2) + pair]
            return swap(tile) if odd != upward else tile

        def build(plane, own, l, masked):
            pair, odd = l // 2, l % 2 == 1
            up = halo(above, plane, pair, odd, False)
            down = halo(below, plane, pair, not odd, False)
            if masked:
                up, down = up * low, down * high
            return extend(own, up, down, half)

        for l in range(levels):
            for a in range(nt):
                cells[a, l, 8:24] = build(a, tracers[a, l], l, True)
            winds[0, l, 8:24] = build(nt, forcing[0, l], l, False)
            winds[1, l, 8:24] = build(nt + 1, forcing[1, l], l, False)
            growth = jnp.exp(0.1 * forcing[2, l] - 0.05 * forcing[3, l])
            winds[2, l, 8:24] = build(nt + 2, growth, l, False)
            winds[3, l, 8:24] = build(nt + 3, edges[l], l, False)
        col = pl.ds(pl.multiple_of(section * 128, 128), 128)
        floor = jnp.concatenate([wet_rows[4:12, col], wet_rows[12:20, col]], axis=0)
        lane = lanes(16)

        def level(l, carry):
            border = winds[3, l, 8:24]
            v = winds[1, l, 8:24]
            v_east = jnp.where(lane == 127, roll_lanes(border, 63 - nt), roll_lanes(v, 127))
            v_west = jnp.where(lane == 0, roll_lanes(border, -nt), roll_lanes(v, 1))
            weights = tracer_weights(
                winds[0, l, 7:23], winds[0, l, 9:25], v_east, v_west, winds[2, l, 8:24], floor > l
            )
            inside = lax.broadcasted_iota(jnp.int32, (16, 128), 0) * (section * 0 + 1)
            results = tracer_level(
                [cells[a, l, 8:24] for a in range(nt)],
                [cells[a, l, 7:23] for a in range(nt)],
                [cells[a, l, 9:25] for a in range(nt)],
                border, weights, reaction,
            )
            for a in range(nt):
                tracers_next[a, l] = results[a]
            edge = edge_tile(results)
            shade = pigment_of(results[0], results[1])
            shade = jnp.where((inside > 0) & (inside < 15), shade, 0.0)
            for out in (out_a, out_b, out_c):
                out[2 * l] = shade[:8]
                out[2 * l + 1] = shade[8:]
                out[12 + 2 * l] = edge[:8]
                out[13 + 2 * l] = edge[8:]
            return carry

        lax.fori_loop(0, levels, level, 0)


def roll_rows(x, by):
    by = by % 8
    return x if by == 0 else pltpu.roll(x, by, 0)


def second_kernel(
    from_a, from_b, from_c, flow_next, tracers_next, wet_rows, reaction,
    out_a, out_b, out_c, flow_out, tracers_out, buffers, heat, winds,
):
    section, _, _ = place()
    levels = heat.shape[0]
    nt = tracers_next.shape[0]

    @pl.when(section == 3)
    def _():
        shades = (from_c, from_b, from_a)

        def load(l, tile, j):
            return shades[j][2 * l + tile]

        fill_heat(load, heat)
        substep(flow_next, buffers.at[0], heat, wet_rows, 2, 8, 8, 0, 4)
        substep(buffers.at[0], buffers.at[1], heat, wet_rows, 2, 8, 8, 0, 4)
        substep(buffers.at[1], buffers.at[2], heat, wet_rows, 2, 8, 8, 0, 4)
        substep(buffers.at[2], flow_out, heat, wet_rows, 1, 12, 0, 4, 8)
        outs = (out_a, out_b, out_c)
        for l in range(levels):
            for j in range(3):
                cols = slice(128 * j, 128 * j + 128)
                for f in range(2):
                    total = buffers[0, f, l, 12:20, cols] + buffers[1, f, l, 12:20, cols]
                    total = total + buffers[2, f, l, 12:20, cols]
                    outs[j][6 * f + l] = 0.25 * (total + flow_out[f, l, :, cols])
                outs[j][12 + l] = flow_out[2, l, :, cols]
                outs[j][18 + l] = flow_out[3, l, :, cols]

        def clear(l, carry):
            for a in range(nt):
                tracers_out[a, l] = jnp.zeros((8, 128), F32)
            return carry

        lax.fori_loop(0, levels, clear, 0)

    @pl.when(section != 3)
    def _():
        def driven(i):
            return jnp.where(
                section == 0, from_a[i], jnp.where(section == 1, from_b[i], from_c[i])
            )

        for i in range(18):
            winds[i] = driven(i)
        edge_v = driven(18)
        rows_above = driven(19)
        rows_below = driven(20)
        lane = lanes(8)
        sub = lax.broadcasted_iota(jnp.int32, (8, 128), 0)
        for l in range(levels):
            u, v = winds[l], winds[6 + l]
            winds[18 + l] = jnp.where(sub == 0, roll_rows(rows_above, -l), roll_rows(u, 1))
            winds[24 + l] = jnp.where(sub == 7, roll_rows(rows_below, 7 - l), roll_rows(u, 7))
            winds[30 + l] = jnp.where(
                lane == 127, roll_lanes(edge_v, 126 - 2 * l), roll_lanes(v, 127)
            )
            winds[36 + l] = jnp.where(lane == 0, roll_lanes(edge_v, -2 * l), roll_lanes(v, 1))
            borders = [
                open_edges(section, from_a[12 + 2 * l + i], from_c[12 + 2 * l + i], 8)
                for i in range(2)
            ]
            half = upper_half()
            winds[42 + l] = swap(jnp.where(half, borders[1], borders[0]))
        col = pl.ds(pl.multiple_of(section * 128, 128), 128)
        floor = wet_rows[8:16, col]

        def level(l, carry):
            weights = tracer_weights(
                winds[18 + l], winds[24 + l], winds[30 + l], winds[36 + l], winds[12 + l], floor > l
            )
            results = tracer_level(
                [tracers_next[a, l, 4:12] for a in range(nt)],
                [tracers_next[a, l, 3:11] for a in range(nt)],
                [tracers_next[a, l, 5:13] for a in range(nt)],
                winds[42 + l], weights, reaction,
            )
            for a in range(nt):
                tracers_out[a, l] = results[a]
            shade = pigment_of(results[0], results[1])
            for out in (out_a, out_b, out_c):
                out[l] = shade
                for i in range(1, 4):
                    out[6 * i + l] = jnp.zeros((8, 128), F32)
            for f in range(4):
                flow_out[f, l] = jnp.zeros_like(flow_out[f, l])
            return carry

        lax.fori_loop(0, levels, level, 0)


def last_kernel(from_a, from_b, from_c, light_out, forcing_out):
    section, _, _ = place()
    levels = light_out.shape[0]
    is_dynamics = section == 3
    for l in range(levels):
        for j, shade in enumerate((from_c, from_b, from_a)):
            light_out[l, :, 128 * j : 128 * j + 128] = jnp.where(is_dynamics, shade[l], 0.0)
        for f in range(4):
            i = 6 * f + l
            picked = jnp.where(
                section == 0, from_a[i], jnp.where(section == 1, from_b[i], from_c[i])
            )
            forcing_out[f, l] = jnp.where(is_dynamics, 0.0, picked)


def call(kernel, shapes, operands, spaces, scratch=()):
    return pl.pallas_call(
        kernel,
        out_shape=[jax.ShapeDtypeStruct(shape, dtype) for shape, dtype in shapes],
        in_specs=[pl.BlockSpec(memory_space=space) for space in spaces],
        out_specs=[pl.BlockSpec(memory_space=pltpu.VMEM) for _ in shapes],
        scratch_shapes=list(scratch),
        compiler_params=pltpu.CompilerParams(vmem_limit_bytes=VMEM_LIMIT),
    )(*operands)


def route(target):
    total = lax.axis_size("comp") * lax.axis_size("gy") * lax.axis_size("gx")
    group = total // SECTIONS
    pairs = []
    for moved in range(total):
        section, strip = target(moved // group, moved % group, group)
        pairs.append(((moved - 1) % total, (section * group + strip - 1) % total))
    return pairs


def across(value, by):
    return lax.ppermute(value, AXES, route(lambda k, s, g: ((k + by) % SECTIONS, s)))


def along(value, by):
    return lax.ppermute(value, AXES, route(lambda k, s, g: (k, (s + by) % g)))


def on_device(flow_fields, chlorophyll_lag, tracers, forcing, ocean_mask, bottom, reaction):
    levels = chlorophyll_lag.shape[0]
    nt = tracers.shape[0]
    breadth = flow_fields.shape[3]
    vmem, smem, anywhere = pltpu.VMEM, pltpu.SMEM, pl.ANY
    (border,) = call(edges_kernel, [((levels, 8, 128), F32)], (tracers, forcing), (vmem, vmem))
    from_left = across(border, 1)
    from_right = across(border, -1)
    (wet_rows,) = call(
        mask_kernel,
        [((24, breadth), jnp.int32)],
        (ocean_mask, bottom),
        (anywhere, anywhere),
        (
            pltpu.VMEM((3, 8, breadth), jnp.int32),
            pltpu.VMEM((3, 8, breadth), jnp.int32),
            pltpu.SemaphoreType.DMA((6,)),
        ),
    )
    message = (15, levels, 8, 128)
    to_next, to_prev, edges = call(
        rows_kernel,
        [(message, F32), (message, F32), ((levels, 8, 128), F32)],
        (flow_fields, chlorophyll_lag, tracers, forcing, from_left, from_right),
        (vmem,) * 6,
    )
    above = along(to_next, 1)
    below = along(to_prev, -1)
    exchange = ((24, 8, 128), F32)
    sent = call(
        first_kernel,
        [
            exchange, exchange, exchange,
            ((4, levels, 32, breadth), F32), ((nt, levels, 16, 128), F32),
        ],
        (flow_fields, chlorophyll_lag, tracers, forcing, edges, above, below, wet_rows, reaction),
        (vmem,) * 8 + (smem,),
        (
            pltpu.VMEM((4, 4, levels, 40, breadth), F32),
            pltpu.VMEM((levels, 24, breadth), F32),
            pltpu.VMEM((nt, levels, 32, 128), F32),
            pltpu.VMEM((4, levels, 32, 128), F32),
        ),
    )
    from_b = across(sent[1], 2)
    from_a = across(sent[0], 1)
    from_c = across(sent[2], -1)
    last = call(
        second_kernel,
        [
            exchange, exchange, exchange,
            ((4, levels, 8, breadth), F32), ((nt, levels, 8, 128), F32),
        ],
        (from_a, from_b, from_c, sent[3], sent[4], wet_rows, reaction),
        (vmem,) * 6 + (smem,),
        (
            pltpu.VMEM((3, 4, levels, 32, breadth), F32),
            pltpu.VMEM((levels, 16, breadth), F32),
            pltpu.VMEM((48, 8, 128), F32),
        ),
    )
    final_b = across(last[1], 2)
    final_a = across(last[0], 1)
    final_c = across(last[2], -1)
    light_out, forcing_out = call(
        last_kernel,
        [((levels, 8, breadth), F32), ((4, levels, 8, 128), F32)],
        (final_a, final_b, final_c),
        (vmem,) * 3,
    )
    return last[3], light_out, last[4], forcing_out


def solution(mesh):
    rows = P(None, None, AXES, None)
    light = P(None, AXES, None)
    return jax.shard_map(
        on_device,
        mesh=mesh,
        in_specs=(rows, light, rows, rows, P(), P(), P()),
        out_specs=(rows, light, rows, rows),
        check_vma=False,
    )
```

profile of v0, /device:TPU:1, one launch (start us, length us, event | category | flops | bytes accessed | tf_op | source)
XLA Modules:
  0.0 57.8 jit_solution(15292516558181685725)
XLA Ops:
  0.6 0.0 copy-start
  0.6 1.0 %copy-done = f32[16,6,8,128]{3,2,1,0:T(8,128)S(1)} copy-done((f32[16,6,8,128]{3,2,1,0:T(8,128)S(1)}, f32[16,6,8,128]{3,2,1,0:T(8,128)}, u32[]{:S(2)}) %copy-start) | copy-done | bytes 393240
  1.6 0.9 %copy-done.4 = f32[4,6,8,128]{3,2,1,0:T(8,128)S(1)} copy-done((f32[4,6,8,128]{3,2,1,0:T(8,128)S(1)}, f32[4,6,8,128]{3,2,1,0:T(8,128)}, u32[]{:S(2)}) %copy-start.4) | copy-done | bytes 98328
  2.5 0.6 %shard_map.102 = f32[6,8,128]{2,1,0:T(8,128)S(1)} custom-call(f32[16,6,8,128]{3,2,1,0:T(8,128)S(1)} %copy-done, f32[4,6,8,128]{3,2,1,0:T(8,128)S(1)} %copy-done.4), custom_call_target="tpu_custom_call" | custom-call | tf_op jit(solution)/shard_map/pallas_call | solution.py:503
  3.2 0.0 copy-start.1
  3.2 3.4 %collective-permute-start.1 = (f32[6,8,128]{2,1,0:T(8,128)S(1)}, f32[6,8,128]{2,1,0:T(8,128)S(1)}, u32[]{:S(2)}, u32[]{:S(2)}) collective-permute-start(f32[6,8,128]{2,1,0:T(8,128)S(1)} %shard_map.102), channel_id=1, source_target_pairs={{255,191},{0,192},{1,193},{2,194},{3,195},{4,196},{5,197},{6,198},... | collective-permute-start | bytes 73736 | tf_op jit(solution)/shard_map/ppermute | solution.py:524
  6.6 0.9 %collective-permute-done.1.from_right = f32[6,8,128]{2,1,0:T(8,128)S(1)} collective-permute-done((f32[6,8,128]{2,1,0:T(8,128)S(1)}, f32[6,8,128]{2,1,0:T(8,128)S(1)}, u32[]{:S(2)}, u32[]{:S(2)}) %collective-permute-start.1) | collective-permute-done | bytes 24608 | tf_op jit(solution)/shard_map/ppermute | solution.py:524
  7.5 2.9 %collective-permute-done.from_left = f32[6,8,128]{2,1,0:T(8,128)S(1)} collective-permute-done((f32[6,8,128]{2,1,0:T(8,128)S(1)}, f32[6,8,128]{2,1,0:T(8,128)S(1)}, u32[]{:S(2)}, u32[]{:S(2)}) %collective-permute-start) | collective-permute-done | bytes 24608 | tf_op jit(solution)/shard_map/ppermute | solution.py:524
  10.5 1.0 %copy-done.2 = f32[4,6,8,384]{3,2,1,0:T(8,128)S(1)} copy-done((f32[4,6,8,384]{3,2,1,0:T(8,128)S(1)}, f32[4,6,8,384]{3,2,1,0:T(8,128)}, u32[]{:S(2)}) %copy-start.2) | copy-done | bytes 294936
  11.4 0.9 %copy-done.8 = f32[6,8,384]{2,1,0:T(8,128)S(1)} copy-done((f32[6,8,384]{2,1,0:T(8,128)S(1)}, f32[6,8,384]{2,1,0:T(8,128)}, u32[]{:S(2)}) %copy-start.8) | copy-done | bytes 73752
  12.3 0.1 shard_map.103
  12.4 5.0 %collective-permute-start.2 = (f32[15,6,8,128]{3,2,1,0:T(8,128)S(1)}, f32[15,6,8,128]{3,2,1,0:T(8,128)S(1)}, u32[]{:S(2)}, u32[]{:S(2)}) collective-permute-start(f32[15,6,8,128]{3,2,1,0:T(8,128)S(1)} %get-tuple-element.20), channel_id=1, source_target_pairs={{255,0},{0,1},{1,2},{2,3},{3,4},{4,5},{5,6},{6,7},{7,8},{8,9},{9,1... | collective-permute-start | bytes 1105928 | tf_op jit(solution)/shard_map/ppermute | solution.py:528
  17.3 0.0 collective-permute-start.3
  17.3 1.1 %copy-done.6 = s32[512,384]{1,0:T(8,128)S(1)} copy-done((s32[512,384]{1,0:T(8,128)S(1)}, s32[512,384]{1,0:T(8,128)}, u32[]{:S(2)}) %copy-start.6) | copy-done | bytes 786456
  18.5 1.1 %copy-done.7 = s32[512,384]{1,0:T(8,128)S(1)} copy-done((s32[512,384]{1,0:T(8,128)S(1)}, s32[512,384]{1,0:T(8,128)}, u32[]{:S(2)}) %copy-start.7) | copy-done | bytes 786456
  19.6 0.1 shard_map.104.wet_rows
  19.8 6.0 %collective-permute-done.2.above = f32[15,6,8,128]{3,2,1,0:T(8,128)S(1)} collective-permute-done((f32[15,6,8,128]{3,2,1,0:T(8,128)S(1)}, f32[15,6,8,128]{3,2,1,0:T(8,128)S(1)}, u32[]{:S(2)}, u32[]{:S(2)}) %collective-permute-start.2) | collective-permute-done | bytes 368672 | tf_op jit(solution)/shard_map/ppermute | solution.py:528
  25.7 4.0 %collective-permute-done.3.below = f32[15,6,8,128]{3,2,1,0:T(8,128)S(1)} collective-permute-done((f32[15,6,8,128]{3,2,1,0:T(8,128)S(1)}, f32[15,6,8,128]{3,2,1,0:T(8,128)S(1)}, u32[]{:S(2)}, u32[]{:S(2)}) %collective-permute-start.3) | collective-permute-done | bytes 368672 | tf_op jit(solution)/shard_map/ppermute | solution.py:528
  29.8 2.9 %shard_map.105 = (f32[24,8,128]{2,1,0:T(8,128)S(1)}, f32[24,8,128]{2,1,0:T(8,128)S(1)}, f32[24,8,128]{2,1,0:T(8,128)S(1)}, f32[4,6,32,384]{3,2,1,0:T(8,128)S(1)}, f32[16,6,16,128]{3,2,1,0:T(8,128)S(1)}) custom-call(f32[4,6,8,384]{3,2,1,0:T(8,128)S(1)} %copy-done.3, f32[6,8,384]{2,1,0:T(8,128)S(1)} %copy-done.9, f32[16,6,8,128]{3,2,1,0:T(8,128)S(1)} %copy-done.1, ...), custom_call_target="tpu_custom_call" | custom-call | tf_op jit(solution)/shard_map/pallas_call | solution.py:503
  32.7 0.1 collective-permute-start.4
  32.7 5.2 %collective-permute-start.5 = (f32[24,8,128]{2,1,0:T(8,128)S(1)}, f32[24,8,128]{2,1,0:T(8,128)S(1)}, u32[]{:S(2)}, u32[]{:S(2)}) collective-permute-start(f32[24,8,128]{2,1,0:T(8,128)S(1)} %get-tuple-element.23), channel_id=1, source_target_pairs={{255,127},{0,128},{1,129},{2,130},{3,131},{4,132},{5,133},{6,134},... | collective-permute-start | bytes 294920 | tf_op jit(solution)/shard_map/ppermute | solution.py:524
  37.9 0.0 collective-permute-start.6
  37.9 1.3 %collective-permute-done.4.from_a = f32[24,8,128]{2,1,0:T(8,128)S(1)} collective-permute-done((f32[24,8,128]{2,1,0:T(8,128)S(1)}, f32[24,8,128]{2,1,0:T(8,128)S(1)}, u32[]{:S(2)}, u32[]{:S(2)}) %collective-permute-start.4) | collective-permute-done | bytes 98336 | tf_op jit(solution)/shard_map/ppermute | solution.py:524
  39.2 3.6 %collective-permute-done.5.from_b = f32[24,8,128]{2,1,0:T(8,128)S(1)} collective-permute-done((f32[24,8,128]{2,1,0:T(8,128)S(1)}, f32[24,8,128]{2,1,0:T(8,128)S(1)}, u32[]{:S(2)}, u32[]{:S(2)}) %collective-permute-start.5) | collective-permute-done | bytes 98336 | tf_op jit(solution)/shard_map/ppermute | solution.py:524
  42.8 0.0 collective-permute-done.6.from_c
  42.8 2.5 %shard_map.106 = (f32[24,8,128]{2,1,0:T(8,128)S(1)}, f32[24,8,128]{2,1,0:T(8,128)S(1)}, f32[24,8,128]{2,1,0:T(8,128)S(1)}, f32[4,6,8,384]{3,2,1,0:T(8,128)}, f32[16,6,8,128]{3,2,1,0:T(8,128)}) custom-call(f32[24,8,128]{2,1,0:T(8,128)S(1)} %collective-permute-done.4.from_a, f32[24,8,128]{2,1,0:T(8,128)S(1)} %collective-permute-done.5.from_b, ...), custom_call_target="tpu_custom_call" | custom-call | tf_op jit(solution)/shard_map/pallas_call | solution.py:503
  45.3 0.0 collective-permute-start.7
  45.3 7.2 %collective-permute-start.8 = (f32[24,8,128]{2,1,0:T(8,128)S(1)}, f32[24,8,128]{2,1,0:T(8,128)S(1)}, u32[]{:S(2)}, u32[]{:S(2)}) collective-permute-start(f32[24,8,128]{2,1,0:T(8,128)S(1)} %get-tuple-element.29), channel_id=1, source_target_pairs={{255,127},{0,128},{1,129},{2,130},{3,131},{4,132},{5,133},{6,134},... | collective-permute-start | bytes 294920 | tf_op jit(solution)/shard_map/ppermute | solution.py:524
  52.5 0.0 collective-permute-start.9
  52.5 1.6 %collective-permute-done.7.from_a = f32[24,8,128]{2,1,0:T(8,128)S(1)} collective-permute-done((f32[24,8,128]{2,1,0:T(8,128)S(1)}, f32[24,8,128]{2,1,0:T(8,128)S(1)}, u32[]{:S(2)}, u32[]{:S(2)}) %collective-permute-start.7) | collective-permute-done | bytes 98336 | tf_op jit(solution)/shard_map/ppermute | solution.py:524
  54.2 3.0 %collective-permute-done.8.from_b = f32[24,8,128]{2,1,0:T(8,128)S(1)} collective-permute-done((f32[24,8,128]{2,1,0:T(8,128)S(1)}, f32[24,8,128]{2,1,0:T(8,128)S(1)}, u32[]{:S(2)}, u32[]{:S(2)}) %collective-permute-start.8) | collective-permute-done | bytes 98336 | tf_op jit(solution)/shard_map/ppermute | solution.py:524
  57.1 0.7 %shard_map.107 = (f32[6,8,384]{2,1,0:T(8,128)}, f32[4,6,8,128]{3,2,1,0:T(8,128)}) custom-call(f32[24,8,128]{2,1,0:T(8,128)S(1)} %collective-permute-done.7.from_a, f32[24,8,128]{2,1,0:T(8,128)S(1)} %collective-permute-done.8.from_b, f32[24,8,128]{2,1,0:T(8,128)S(1)} %collective-permute-done.9.from_c), custom_call_target="tpu_custom_call" | custom-call | tf_op jit(solution)/shard_map/pallas_call | solution.py:503
  (16 shorter events, 0.0 us)
Async XLA Ops:
  0.6 1.0 %copy-start = (f32[16,6,8,128]{3,2,1,0:T(8,128)S(1)}, f32[16,6,8,128]{3,2,1,0:T(8,128)}, u32[]{:S(2)}) copy-start(f32[16,6,8,128]{3,2,1,0:T(8,128)} %tracers.5) | copy-start | bytes 1179652
  1.6 0.9 %copy-start.4 = (f32[4,6,8,128]{3,2,1,0:T(8,128)S(1)}, f32[4,6,8,128]{3,2,1,0:T(8,128)}, u32[]{:S(2)}) copy-start(f32[4,6,8,128]{3,2,1,0:T(8,128)} %forcing.5) | copy-start | bytes 294916
  2.5 27.2 %copy-start.3 = (f32[4,6,8,384]{3,2,1,0:T(8,128)S(1)}, f32[4,6,8,384]{3,2,1,0:T(8,128)}, u32[]{:S(2)}) copy-start(f32[4,6,8,384]{3,2,1,0:T(8,128)} %flow.3) | copy-start | bytes 884740
  2.5 27.2 %copy-start.5 = (f32[4,6,8,128]{3,2,1,0:T(8,128)S(1)}, f32[4,6,8,128]{3,2,1,0:T(8,128)}, u32[]{:S(2)}) copy-start(f32[4,6,8,128]{3,2,1,0:T(8,128)} %forcing.5) | copy-start | bytes 294916
  2.5 27.2 %copy-start.9 = (f32[6,8,384]{2,1,0:T(8,128)S(1)}, f32[6,8,384]{2,1,0:T(8,128)}, u32[]{:S(2)}) copy-start(f32[6,8,384]{2,1,0:T(8,128)} %pigment.3) | copy-start | bytes 221188
  2.5 27.2 %copy-start.10 = (f32[16,16]{1,0:T(8,128)S(1)}, f32[16,16]{1,0:T(8,128)}, u32[]{:S(2)}) copy-start(f32[16,16]{1,0:T(8,128)} %reaction.3) | copy-start | bytes 3076
  3.2 26.6 %copy-start.1 = (f32[16,6,8,128]{3,2,1,0:T(8,128)S(1)}, f32[16,6,8,128]{3,2,1,0:T(8,128)}, u32[]{:S(2)}) copy-start(f32[16,6,8,128]{3,2,1,0:T(8,128)} %tracers.5) | copy-start | bytes 1179652
  3.2 4.3 %collective-permute-start.1 = (f32[6,8,128]{2,1,0:T(8,128)S(1)}, f32[6,8,128]{2,1,0:T(8,128)S(1)}, u32[]{:S(2)}, u32[]{:S(2)}) collective-permute-start(f32[6,8,128]{2,1,0:T(8,128)S(1)} %shard_map.102), channel_id=1, source_target_pairs={{255,191},{0,192},{1,193},{2,194},{3,195},{4,196},{5,197},{6,198},... | collective-permute-start | bytes 73736 | tf_op jit(solution)/shard_map/ppermute | solution.py:524
  6.6 3.9 %collective-permute-start = (f32[6,8,128]{2,1,0:T(8,128)S(1)}, f32[6,8,128]{2,1,0:T(8,128)S(1)}, u32[]{:S(2)}, u32[]{:S(2)}) collective-permute-start(f32[6,8,128]{2,1,0:T(8,128)S(1)} %shard_map.102), channel_id=1, source_target_pairs={{255,63},{0,64},{1,65},{2,66},{3,67},{4,68},{5,69},{6,70},{7,71},{... | collective-permute-start | bytes 73736 | tf_op jit(solution)/shard_map/ppermute | solution.py:524
  10.4 1.0 %copy-start.2 = (f32[4,6,8,384]{3,2,1,0:T(8,128)S(1)}, f32[4,6,8,384]{3,2,1,0:T(8,128)}, u32[]{:S(2)}) copy-start(f32[4,6,8,384]{3,2,1,0:T(8,128)} %flow.3) | copy-start | bytes 884740
  11.4 0.9 %copy-start.8 = (f32[6,8,384]{2,1,0:T(8,128)S(1)}, f32[6,8,384]{2,1,0:T(8,128)}, u32[]{:S(2)}) copy-start(f32[6,8,384]{2,1,0:T(8,128)} %pigment.3) | copy-start | bytes 221188
  12.4 13.4 %collective-permute-start.2 = (f32[15,6,8,128]{3,2,1,0:T(8,128)S(1)}, f32[15,6,8,128]{3,2,1,0:T(8,128)S(1)}, u32[]{:S(2)}, u32[]{:S(2)}) collective-permute-start(f32[15,6,8,128]{3,2,1,0:T(8,128)S(1)} %get-tuple-element.20), channel_id=1, source_target_pairs={{255,0},{0,1},{1,2},{2,3},{3,4},{4,5},{5,6},{6,7},{7,8},{8,9},{9,1... | collective-permute-start | bytes 1105928 | tf_op jit(solution)/shard_map/ppermute | solution.py:528
  17.3 12.4 %collective-permute-start.3 = (f32[15,6,8,128]{3,2,1,0:T(8,128)S(1)}, f32[15,6,8,128]{3,2,1,0:T(8,128)S(1)}, u32[]{:S(2)}, u32[]{:S(2)}) collective-permute-start(f32[15,6,8,128]{3,2,1,0:T(8,128)S(1)} %get-tuple-element.21), channel_id=1, source_target_pairs={{255,62},{0,255},{1,0},{2,1},{3,2},{4,3},{5,4},{6,5},{7,6},{8,7},{... | collective-permute-start | bytes 1105928 | tf_op jit(solution)/shard_map/ppermute | solution.py:528
  17.3 1.1 %copy-start.6 = (s32[512,384]{1,0:T(8,128)S(1)}, s32[512,384]{1,0:T(8,128)}, u32[]{:S(2)}) copy-start(s32[512,384]{1,0:T(8,128)} %ocean.1) | copy-start | bytes 2359300
  18.5 1.1 %copy-start.7 = (s32[512,384]{1,0:T(8,128)S(1)}, s32[512,384]{1,0:T(8,128)}, u32[]{:S(2)}) copy-start(s32[512,384]{1,0:T(8,128)} %bottom.1) | copy-start | bytes 2359300
  32.7 6.6 %collective-permute-start.4 = (f32[24,8,128]{2,1,0:T(8,128)S(1)}, f32[24,8,128]{2,1,0:T(8,128)S(1)}, u32[]{:S(2)}, u32[]{:S(2)}) collective-permute-start(f32[24,8,128]{2,1,0:T(8,128)S(1)} %get-tuple-element.22), channel_id=1, source_target_pairs={{255,63},{0,64},{1,65},{2,66},{3,67},{4,68},{5,69},{6,70},{7,71},{... | collective-permute-start | bytes 294920 | tf_op jit(solution)/shard_map/ppermute | solution.py:524
  32.7 10.0 %collective-permute-start.5 = (f32[24,8,128]{2,1,0:T(8,128)S(1)}, f32[24,8,128]{2,1,0:T(8,128)S(1)}, u32[]{:S(2)}, u32[]{:S(2)}) collective-permute-start(f32[24,8,128]{2,1,0:T(8,128)S(1)} %get-tuple-element.23), channel_id=1, source_target_pairs={{255,127},{0,128},{1,129},{2,130},{3,131},{4,132},{5,133},{6,134},... | collective-permute-start | bytes 294920 | tf_op jit(solution)/shard_map/ppermute | solution.py:524
  37.9 4.8 %collective-permute-start.6 = (f32[24,8,128]{2,1,0:T(8,128)S(1)}, f32[24,8,128]{2,1,0:T(8,128)S(1)}, u32[]{:S(2)}, u32[]{:S(2)}) collective-permute-start(f32[24,8,128]{2,1,0:T(8,128)S(1)} %get-tuple-element.24), channel_id=1, source_target_pairs={{255,191},{0,192},{1,193},{2,194},{3,195},{4,196},{5,197},{6,198},... | collective-permute-start | bytes 294920 | tf_op jit(solution)/shard_map/ppermute | solution.py:524
  45.3 8.9 %collective-permute-start.7 = (f32[24,8,128]{2,1,0:T(8,128)S(1)}, f32[24,8,128]{2,1,0:T(8,128)S(1)}, u32[]{:S(2)}, u32[]{:S(2)}) collective-permute-start(f32[24,8,128]{2,1,0:T(8,128)S(1)} %get-tuple-element.28), channel_id=1, source_target_pairs={{255,63},{0,64},{1,65},{2,66},{3,67},{4,68},{5,69},{6,70},{7,71},{... | collective-permute-start | bytes 294920 | tf_op jit(solution)/shard_map/ppermute | solution.py:524
  45.3 11.8 %collective-permute-start.8 = (f32[24,8,128]{2,1,0:T(8,128)S(1)}, f32[24,8,128]{2,1,0:T(8,128)S(1)}, u32[]{:S(2)}, u32[]{:S(2)}) collective-permute-start(f32[24,8,128]{2,1,0:T(8,128)S(1)} %get-tuple-element.29), channel_id=1, source_target_pairs={{255,127},{0,128},{1,129},{2,130},{3,131},{4,132},{5,133},{6,134},... | collective-permute-start | bytes 294920 | tf_op jit(solution)/shard_map/ppermute | solution.py:524
  52.5 4.6 %collective-permute-start.9 = (f32[24,8,128]{2,1,0:T(8,128)S(1)}, f32[24,8,128]{2,1,0:T(8,128)S(1)}, u32[]{:S(2)}, u32[]{:S(2)}) collective-permute-start(f32[24,8,128]{2,1,0:T(8,128)S(1)} %get-tuple-element.30), channel_id=1, source_target_pairs={{255,191},{0,192},{1,193},{2,194},{3,195},{4,196},{5,197},{6,198},... | collective-permute-start | bytes 294920 | tf_op jit(solution)/shard_map/ppermute | solution.py:524
where the time goes:
time: 58.1 us; the launch traced here: 57.8 us
  waiting for transfers between devices  23.3 us (40%)
  starting transfers between devices  20.8 us (36%)
  Pallas kernels  6.94 us (12%)
  local copies, waits for them, and re-layouts  6.02 us (10%)
  between operations  0.72 us (1%)
    ppermute x8, starting transfers between devices, across(): lax.ppermute(value, AXES, route(lambda k, s, g: ((k + by) % SECTIONS, s)))  15.9 us
    ppermute x8, waiting for transfers between devices, across(): lax.ppermute(value, AXES, route(lambda k, s, g: ((k + by) % SECTIONS, s)))  13.3 us
    ppermute x2, waiting for transfers between devices, along(): return lax.ppermute(value, AXES, route(lambda k, s, g: (k, (s + by) % g)))  9.98 us
    pallas_call x6, Pallas kernels, call(): pl.pallas_call(kernel, out_shape=[jax.ShapeDtypeStruct(shape, dtype) for...  6.94 us
    unnamed x22, local copies, waits for them, and re-layouts  6.02 us
    ppermute x2, starting transfers between devices, along(): return lax.ppermute(value, AXES, route(lambda k, s, g: (k, (s + by) % g)))  4.98 us
  transfers between devices with their start and end apart: 10, of which 8 were waited for; matrix products, arithmetic and copies ran while one was open for 0% of the time, Pallas kernels for 0%

commit v1 on v0

--- a/solution.py
+++ b/solution.py
@@ -9,6 +9,7 @@
 SECTIONS = 4
 DT = 0.1
 F32 = jnp.float32
+UNROLL = 2
 VMEM_LIMIT = 48 * 1024 * 1024
 
 
@@ -43,23 +44,6 @@
     return jnp.where(flag, 1.0, 0.0).astype(F32)
 
 
-def mask_kernel(ocean, bottom, out, ocean_rows, bottom_rows, sems):
-    _, strip, group = place()
-    starts = [jnp.maximum(strip - 1, 0), strip, jnp.minimum(strip + 1, group - 1)]
-    copies = []
-    for i, start in enumerate(starts):
-        rows = pl.ds(pl.multiple_of(start * 8, 8), 8)
-        copies.append(pltpu.make_async_copy(ocean.at[rows], ocean_rows.at[i], sems.at[i]))
-        copies.append(pltpu.make_async_copy(bottom.at[rows], bottom_rows.at[i], sems.at[3 + i]))
-    for copy in copies:
-        copy.start()
-    for copy in copies:
-        copy.wait()
-    inside = [(strip > 0).astype(jnp.int32), 1, (strip < group - 1).astype(jnp.int32)]
-    for i in range(3):
-        out[8 * i : 8 * i + 8] = jnp.where(ocean_rows[i] == 1, bottom_rows[i], 0) * inside[i]
-
-
 def edge_tile(planes):
     lane = lanes(planes[0].shape[0])
     edges = jnp.zeros_like(planes[0])
@@ -69,21 +53,69 @@
     return edges
 
 
-def edges_kernel(tracers, forcing, out):
+def load_kernel(
+    flow, pigment, tracers, forcing, ocean, bottom,
+    border, flow_in, pigment_in, tracers_in, forcing_in, wet_rows,
+    ocean_rows, bottom_rows, mask_sems, sems,
+):
+    section, strip, group = place()
+    levels = pigment.shape[0]
     nt = tracers.shape[0]
-
-    def level(l, carry):
-        out[l] = edge_tile([tracers[a, l] for a in range(nt)] + [forcing[1, l]])
-        return carry
-
-    lax.fori_loop(0, tracers.shape[1], level, 0)
+    starts = [jnp.maximum(strip - 1, 0), strip, jnp.minimum(strip + 1, group - 1)]
+    masks = []
+    for i, start in enumerate(starts):
+        rows = pl.ds(pl.multiple_of(start * 8, 8), 8)
+        masks.append(pltpu.make_async_copy(ocean.at[rows], ocean_rows.at[i], mask_sems.at[i]))
+        masks.append(pltpu.make_async_copy(bottom.at[rows], bottom_rows.at[i], mask_sems.at[3 + i]))
+
+    @pl.when(section == 3)
+    def _():
+        copies = []
+        for j in range(3):
+            cols = slice(128 * j, 128 * j + 128)
+            copies.append(
+                pltpu.make_async_copy(flow.at[:, :, :, cols], flow_in.at[:, :, j], sems.at[j])
+            )
+            copies.append(
+                pltpu.make_async_copy(pigment.at[:, :, cols], pigment_in.at[:, j], sems.at[3 + j])
+            )
+        for copy in copies + masks:
+            copy.start()
+        border[...] = jnp.zeros_like(border)
+        for copy in copies + masks:
+            copy.wait()
+
+    @pl.when(section != 3)
+    def _():
+        copies = []
+        for l in range(levels):
+            copies.append(
+                pltpu.make_async_copy(tracers.at[:, l], tracers_in.at[:, l], sems.at[l])
+            )
+            copies.append(
+                pltpu.make_async_copy(forcing.at[:, l], forcing_in.at[:, l], sems.at[levels + l])
+            )
+        for copy in copies + masks:
+            copy.start()
+        for l in range(levels):
+            copies[2 * l].wait()
+            copies[2 * l + 1].wait()
+            border[l] = edge_tile([tracers_in[a, l] for a in range(nt)] + [forcing_in[1, l]])
+        for copy in masks:
+            copy.wait()
+
+    inside = [(strip > 0).astype(jnp.int32), 1, (strip < group - 1).astype(jnp.int32)]
+    for i in range(3):
+        floor = jnp.where(ocean_rows[i] == 1, bottom_rows[i], 0) * inside[i]
+        for j in range(3):
+            wet_rows[j, 8 * i : 8 * i + 8] = floor[:, 128 * j : 128 * j + 128]
 
 
 def open_edges(section, from_left, from_right, rows):
     lane = lanes(rows)
-    return jnp.where(
-        lane < 64, from_left * spread(section > 0), from_right * spread(section < 2)
-    )
+    left = jnp.where(section > 0, from_left, 0.0)
+    right = jnp.where(section < 2, from_right, 0.0)
+    return jnp.where(lane < 64, left, right)
 
 
 def rows_kernel(flow, pigment, tracers, forcing, from_left, from_right, to_next, to_prev, edges):
@@ -96,8 +128,7 @@
         def level(l, carry):
             for f in range(5):
                 for j in range(3):
-                    cols = slice(128 * j, 128 * j + 128)
-                    tile = flow[f, l, :, cols] if f < 4 else pigment[l, :, cols]
+                    tile = flow[f, l, j] if f < 4 else pigment[l, j]
                     to_next[3 * f + j, l] = tile
                     to_prev[3 * f + j, l] = tile
             return carry
@@ -146,22 +177,17 @@
 def substep(source, target, heat, wet_rows, tiles, read_at, write_at, heat_at, wet_at):
     levels = heat.shape[0]
     thirds = 3
-    for tile in range(tiles):
-        row = read_at + 8 * tile
-        put = write_at + 8 * tile
-        floors = [
-            wet_rows[wet_at + 8 * tile : wet_at + 8 * tile + 8, 128 * j : 128 * j + 128]
-            for j in range(thirds)
-        ]
-
-        def level(l, carry, row=row, put=put, tile=tile, floors=floors):
-            slope_x, slope_y = carry
+    zero = jnp.zeros((8, 128), F32)
+
+    def level(l, carry):
+        slopes = []
+        for tile in range(tiles):
+            row = read_at + 8 * tile
+            put = write_at + 8 * tile
+            slope_x, slope_y = carry[tile]
 
             def load(f, by):
-                return [
-                    source[f, l, row + by : row + by + 8, 128 * j : 128 * j + 128]
-                    for j in range(thirds)
-                ]
+                return [source[f, l, j, row + by : row + by + 8] for j in range(thirds)]
 
             centre = [load(f, 0) for f in range(4)]
             up = [load(f, -1) for f in range(4)]
@@ -178,13 +204,12 @@
                 py = slope_y[j] + ((se - sw) - (te - tw))
                 new_x.append(px)
                 new_y.append(py)
-                is_wet = floors[j] > l
+                is_wet = wet_rows[j, wet_at + 8 * tile : wet_at + 8 * tile + 8] > l
                 a = 0.05 - 0.05 * us
                 b = 0.05 + 0.05 * un
                 c = 0.05 - 0.05 * ve
                 d = 0.05 + 0.05 * vw
-                cols = slice(128 * j, 128 * j + 128)
-                h = heat[l, heat_at + 8 * tile : heat_at + 8 * tile + 8, cols]
+                h = heat[l, j, heat_at + 8 * tile : heat_at + 8 * tile + 8]
                 results = (
                     0.79 * u + 0.1 * v - 0.01 * px + 0.05 * ((un + us) + (ue + uw)),
                     0.79 * v - 0.1 * u - 0.01 * py + 0.05 * ((vn + vs) + (ve + vw)),
@@ -192,15 +217,16 @@
                     0.8 * s + ((ss * a + sn * b) + (se * c + sw * d)),
                 )
                 for f in range(4):
-                    target[f, l, put : put + 8, cols] = jnp.where(is_wet, results[f], 0.0)
-            return new_x, new_y
-
-        zero = [jnp.zeros((8, 128), F32) for _ in range(thirds)]
-        lax.fori_loop(0, levels, level, (zero, zero))
+                    target[f, l, j, put : put + 8] = jnp.where(is_wet, results[f], 0.0)
+            slopes.append((new_x, new_y))
+        return slopes
+
+    start = [([zero] * thirds, [zero] * thirds) for _ in range(tiles)]
+    lax.fori_loop(0, levels, level, start, unroll=UNROLL)
 
 
 def fill_heat(load, heat):
-    levels, rows = heat.shape[0], heat.shape[1]
+    levels, rows = heat.shape[0], heat.shape[2]
     for tile in range(rows // 8):
         for j in range(3):
             optical = jnp.zeros((8, 128), F32)
@@ -208,9 +234,7 @@
             for l in range(levels):
                 optical = optical + (0.05 + 0.3 * load(l, tile, j))
                 lower = jnp.exp(-optical)
-                heat[l, 8 * tile : 8 * tile + 8, 128 * j : 128 * j + 128] = (5.0 * DT) * (
-                    light - lower
-                )
+                heat[l, j, 8 * tile : 8 * tile + 8] = (5.0 * DT) * (light - lower)
                 light = lower
 
 
@@ -256,7 +280,7 @@
 
 def first_kernel(
     flow, pigment, tracers, forcing, edges, above, below, wet_rows, reaction,
-    out_a, out_b, out_c, flow_next, tracers_next, buffers, heat, cells, winds,
+    out_a, out_b, out_c, flow_next, tracers_next, field_0, field_1, field_2, field_3, heat, cells, winds,
 ):
     section, strip, group = place()
     levels = pigment.shape[0]
@@ -269,31 +293,31 @@
         def fill(l, carry):
             for f in range(4):
                 for j in range(3):
-                    cols = slice(128 * j, 128 * j + 128)
-                    buffers[0, f, l, 8:16, cols] = above[3 * f + j, l] * low
-                    buffers[0, f, l, 16:24, cols] = flow[f, l, :, cols]
-                    buffers[0, f, l, 24:32, cols] = below[3 * f + j, l] * high
+                    field_0[f, l, j, 8:16] = above[3 * f + j, l] * low
+                    field_0[f, l, j, 16:24] = flow[f, l, j]
+                    field_0[f, l, j, 24:32] = below[3 * f + j, l] * high
             return carry
 
         lax.fori_loop(0, levels, fill, 0)
 
         def load(l, tile, j):
             if tile == 1:
-                return pigment[l, :, 128 * j : 128 * j + 128]
+                return pigment[l, j]
             return (above if tile == 0 else below)[12 + j, l]
 
         fill_heat(load, heat)
-        for n in range(3):
-            substep(buffers.at[n], buffers.at[n + 1], heat, wet_rows, 3, 8, 8, 0, 0)
-        substep(buffers.at[3], flow_next, heat, wet_rows, 2, 12, 8, 4, 4)
+        substep(field_0, field_1, heat, wet_rows, 3, 8, 8, 0, 0)
+        substep(field_1, field_2, heat, wet_rows, 3, 8, 8, 0, 0)
+        substep(field_2, field_3, heat, wet_rows, 3, 8, 8, 0, 0)
+        substep(field_3, flow_next, heat, wet_rows, 2, 12, 8, 4, 4)
         lane = lanes(8)
         outs = (out_a, out_b, out_c)
         sub = lax.broadcasted_iota(jnp.int32, (8, 128), 0)
 
-        def mean(f, l, row, cols):
-            total = buffers[1, f, l, row : row + 8, cols] + buffers[2, f, l, row : row + 8, cols]
-            total = total + buffers[3, f, l, row : row + 8, cols]
-            return 0.25 * (total + flow_next[f, l, row - 4 : row + 4, cols])
+        def mean(f, l, row, j):
+            total = field_1[f, l, j, row : row + 8] + field_2[f, l, j, row : row + 8]
+            total = total + field_3[f, l, j, row : row + 8]
+            return 0.25 * (total + flow_next[f, l, j, row - 4 : row + 4])
 
         edge_v = [jnp.zeros((8, 128), F32) for _ in range(3)]
         rows_above = [jnp.zeros((8, 128), F32) for _ in range(3)]
@@ -301,15 +325,14 @@
         for l in range(levels):
             v_mean = []
             for j in range(3):
-                cols = slice(128 * j, 128 * j + 128)
-                outs[j][l] = mean(0, l, 16, cols)
-                v_mean.append(mean(1, l, 16, cols))
+                outs[j][l] = mean(0, l, 16, j)
+                v_mean.append(mean(1, l, 16, j))
                 outs[j][6 + l] = v_mean[j]
-                warm = flow_next[2, l, 12:20, cols]
-                salt = flow_next[3, l, 12:20, cols]
+                warm = flow_next[2, l, j, 12:20]
+                salt = flow_next[3, l, j, 12:20]
                 outs[j][12 + l] = jnp.exp(0.1 * warm - 0.05 * salt)
-                first = mean(0, l, 15, cols)
-                last = mean(0, l, 17, cols)
+                first = mean(0, l, 15, j)
+                last = mean(0, l, 17, j)
                 rows_above[j] = jnp.where(sub == l, roll_rows(first, l), rows_above[j])
                 rows_below[j] = jnp.where(sub == l, roll_rows(last, l + 1), rows_below[j])
             for j in range(3):
@@ -352,9 +375,9 @@
             growth = jnp.exp(0.1 * forcing[2, l] - 0.05 * forcing[3, l])
             winds[2, l, 8:24] = build(nt + 2, growth, l, False)
             winds[3, l, 8:24] = build(nt + 3, edges[l], l, False)
-        col = pl.ds(pl.multiple_of(section * 128, 128), 128)
-        floor = jnp.concatenate([wet_rows[4:12, col], wet_rows[12:20, col]], axis=0)
+        floor = wet_rows[section, 4:20]
         lane = lanes(16)
+        inside = lax.broadcasted_iota(jnp.int32, (16, 128), 0)
 
         def level(l, carry):
             border = winds[3, l, 8:24]
@@ -364,7 +387,6 @@
             weights = tracer_weights(
                 winds[0, l, 7:23], winds[0, l, 9:25], v_east, v_west, winds[2, l, 8:24], floor > l
             )
-            inside = lax.broadcasted_iota(jnp.int32, (16, 128), 0) * (section * 0 + 1)
             results = tracer_level(
                 [cells[a, l, 8:24] for a in range(nt)],
                 [cells[a, l, 7:23] for a in range(nt)],
@@ -393,7 +415,7 @@
 
 def second_kernel(
     from_a, from_b, from_c, flow_next, tracers_next, wet_rows, reaction,
-    out_a, out_b, out_c, flow_out, tracers_out, buffers, heat, winds,
+    out_a, out_b, out_c, flow_last, tracers_last, field_0, field_1, field_2, heat, winds,
 ):
     section, _, _ = place()
     levels = heat.shape[0]
@@ -407,27 +429,19 @@
             return shades[j][2 * l + tile]
 
         fill_heat(load, heat)
-        substep(flow_next, buffers.at[0], heat, wet_rows, 2, 8, 8, 0, 4)
-        substep(buffers.at[0], buffers.at[1], heat, wet_rows, 2, 8, 8, 0, 4)
-        substep(buffers.at[1], buffers.at[2], heat, wet_rows, 2, 8, 8, 0, 4)
-        substep(buffers.at[2], flow_out, heat, wet_rows, 1, 12, 0, 4, 8)
+        substep(flow_next, field_0, heat, wet_rows, 2, 8, 8, 0, 4)
+        substep(field_0, field_1, heat, wet_rows, 2, 8, 8, 0, 4)
+        substep(field_1, field_2, heat, wet_rows, 2, 8, 8, 0, 4)
+        substep(field_2, flow_last, heat, wet_rows, 1, 12, 0, 4, 8)
         outs = (out_a, out_b, out_c)
         for l in range(levels):
             for j in range(3):
-                cols = slice(128 * j, 128 * j + 128)
                 for f in range(2):
-                    total = buffers[0, f, l, 12:20, cols] + buffers[1, f, l, 12:20, cols]
-                    total = total + buffers[2, f, l, 12:20, cols]
-                    outs[j][6 * f + l] = 0.25 * (total + flow_out[f, l, :, cols])
-                outs[j][12 + l] = flow_out[2, l, :, cols]
-                outs[j][18 + l] = flow_out[3, l, :, cols]
-
-        def clear(l, carry):
-            for a in range(nt):
-                tracers_out[a, l] = jnp.zeros((8, 128), F32)
-            return carry
-
-        lax.fori_loop(0, levels, clear, 0)
+                    total = field_0[f, l, j, 12:20] + field_1[f, l, j, 12:20]
+                    total = total + field_2[f, l, j, 12:20]
+                    outs[j][6 * f + l] = 0.25 * (total + flow_last[f, l, j])
+                outs[j][12 + l] = flow_last[2, l, j]
+                outs[j][18 + l] = flow_last[3, l, j]
 
     @pl.when(section != 3)
     def _():
@@ -457,8 +471,7 @@
             ]
             half = upper_half()
             winds[42 + l] = swap(jnp.where(half, borders[1], borders[0]))
-        col = pl.ds(pl.multiple_of(section * 128, 128), 128)
-        floor = wet_rows[8:16, col]
+        floor = wet_rows[section, 8:16]
 
         def level(l, carry):
             weights = tracer_weights(
@@ -471,17 +484,38 @@
                 winds[42 + l], weights, reaction,
             )
             for a in range(nt):
-                tracers_out[a, l] = results[a]
+                tracers_last[a, l] = results[a]
             shade = pigment_of(results[0], results[1])
             for out in (out_a, out_b, out_c):
                 out[l] = shade
                 for i in range(1, 4):
                     out[6 * i + l] = jnp.zeros((8, 128), F32)
-            for f in range(4):
-                flow_out[f, l] = jnp.zeros_like(flow_out[f, l])
             return carry
 
         lax.fori_loop(0, levels, level, 0)
+
+
+def store_kernel(flow_last, tracers_last, flow_out, tracers_out, blank, sems):
+    section, _, _ = place()
+    blank[...] = jnp.zeros_like(blank)
+
+    def put(flow_of, tracers_from):
+        copies = [pltpu.make_async_copy(tracers_from, tracers_out, sems.at[3])]
+        for j in range(3):
+            target = flow_out.at[:, :, :, 128 * j : 128 * j + 128]
+            copies.append(pltpu.make_async_copy(flow_of(j), target, sems.at[j]))
+        for copy in copies:
+            copy.start()
+        for copy in copies:
+            copy.wait()
+
+    @pl.when(section == 3)
+    def _():
+        put(lambda j: flow_last.at[:, :, j], blank)
+
+    @pl.when(section != 3)
+    def _():
+        put(lambda j: blank.at[0:4], tracers_last)
 
 
 def last_kernel(from_a, from_b, from_c, light_out, forcing_out):
@@ -499,12 +533,16 @@
             forcing_out[f, l] = jnp.where(is_dynamics, 0.0, picked)
 
 
-def call(kernel, shapes, operands, spaces, scratch=()):
+def call(kernel, shapes, operands, spaces, scratch=(), out_space=pltpu.VMEM):
+    operands = [
+        pltpu.with_memory_space_constraint(x, pltpu.HBM) if space == pltpu.HBM else x
+        for x, space in zip(operands, spaces)
+    ]
     return pl.pallas_call(
         kernel,
         out_shape=[jax.ShapeDtypeStruct(shape, dtype) for shape, dtype in shapes],
         in_specs=[pl.BlockSpec(memory_space=space) for space in spaces],
-        out_specs=[pl.BlockSpec(memory_space=pltpu.VMEM) for _ in shapes],
+        out_specs=[pl.BlockSpec(memory_space=out_space) for _ in shapes],
         scratch_shapes=list(scratch),
         compiler_params=pltpu.CompilerParams(vmem_limit_bytes=VMEM_LIMIT),
     )(*operands)
@@ -532,26 +570,29 @@
     levels = chlorophyll_lag.shape[0]
     nt = tracers.shape[0]
     breadth = flow_fields.shape[3]
-    vmem, smem, anywhere = pltpu.VMEM, pltpu.SMEM, pl.ANY
-    (border,) = call(edges_kernel, [((levels, 8, 128), F32)], (tracers, forcing), (vmem, vmem))
-    from_left = across(border, 1)
-    from_right = across(border, -1)
-    (wet_rows,) = call(
-        mask_kernel,
-        [((24, breadth), jnp.int32)],
-        (ocean_mask, bottom),
-        (anywhere, anywhere),
+    vmem, smem, hbm = pltpu.VMEM, pltpu.SMEM, pltpu.HBM
+    border, flow, pigment, tracers, forcing, wet_rows = call(
+        load_kernel,
+        [
+            ((levels, 8, 128), F32), ((4, levels, 3, 8, 128), F32), ((levels, 3, 8, 128), F32),
+            (tracers.shape, F32), (forcing.shape, F32), ((3, 24, 128), jnp.int32),
+        ],
+        (flow_fields, chlorophyll_lag, tracers, forcing, ocean_mask, bottom),
+        (hbm,) * 6,
         (
             pltpu.VMEM((3, 8, breadth), jnp.int32),
             pltpu.VMEM((3, 8, breadth), jnp.int32),
             pltpu.SemaphoreType.DMA((6,)),
+            pltpu.SemaphoreType.DMA((2 * levels,)),
         ),
     )
+    from_left = across(border, 1)
+    from_right = across(border, -1)
     message = (15, levels, 8, 128)
     to_next, to_prev, edges = call(
         rows_kernel,
         [(message, F32), (message, F32), ((levels, 8, 128), F32)],
-        (flow_fields, chlorophyll_lag, tracers, forcing, from_left, from_right),
+        (flow, pigment, tracers, forcing, from_left, from_right),
         (vmem,) * 6,
     )
     above = along(to_next, 1)
@@ -561,13 +602,13 @@
         first_kernel,
         [
             exchange, exchange, exchange,
-            ((4, levels, 32, breadth), F32), ((nt, levels, 16, 128), F32),
+            ((4, levels, 3, 32, 128), F32), ((nt, levels, 16, 128), F32),
         ],
-        (flow_fields, chlorophyll_lag, tracers, forcing, edges, above, below, wet_rows, reaction),
+        (flow, pigment, tracers, forcing, edges, above, below, wet_rows, reaction),
         (vmem,) * 8 + (smem,),
         (
-            pltpu.VMEM((4, 4, levels, 40, breadth), F32),
-            pltpu.VMEM((levels, 24, breadth), F32),
+            *[pltpu.VMEM((4, levels, 3, 40, 128), F32) for _ in range(4)],
+            pltpu.VMEM((levels, 3, 24, 128), F32),
             pltpu.VMEM((nt, levels, 32, 128), F32),
             pltpu.VMEM((4, levels, 32, 128), F32),
         ),
@@ -579,26 +620,34 @@
         second_kernel,
         [
             exchange, exchange, exchange,
-            ((4, levels, 8, breadth), F32), ((nt, levels, 8, 128), F32),
+            ((4, levels, 3, 8, 128), F32), ((nt, levels, 8, 128), F32),
         ],
         (from_a, from_b, from_c, sent[3], sent[4], wet_rows, reaction),
         (vmem,) * 6 + (smem,),
         (
-            pltpu.VMEM((3, 4, levels, 32, breadth), F32),
-            pltpu.VMEM((levels, 16, breadth), F32),
+            *[pltpu.VMEM((4, levels, 3, 32, 128), F32) for _ in range(3)],
+            pltpu.VMEM((levels, 3, 16, 128), F32),
             pltpu.VMEM((48, 8, 128), F32),
         ),
     )
     final_b = across(last[1], 2)
     final_a = across(last[0], 1)
     final_c = across(last[2], -1)
+    flow_out, tracers_out = call(
+        store_kernel,
+        [(flow_fields.shape, F32), (tracers.shape, F32)],
+        (last[3], last[4]),
+        (vmem, vmem),
+        (pltpu.VMEM(tracers.shape, F32), pltpu.SemaphoreType.DMA((4,))),
+        hbm,
+    )
     light_out, forcing_out = call(
         last_kernel,
         [((levels, 8, breadth), F32), ((4, levels, 8, 128), F32)],
         (final_a, final_b, final_c),
         (vmem,) * 3,
     )
-    return last[3], light_out, last[4], forcing_out
+    return flow_out, light_out, tracers_out, forcing_out
 
 
 def solution(mesh):

time: 58.1 us -> 49 us (0.84)
  the two profiles are of different devices: /device:TPU:1 before, /device:TPU:6 now
where the time goes in v1:
time: 49 us; the launch traced here: 48.7 us
  waiting for transfers between devices  22.5 us (46%)
  starting transfers between devices  16 us (33%)
  Pallas kernels  9.44 us (19%)
  between operations  0.71 us (1%)
    ppermute x8, waiting for transfers between devices, across(): lax.ppermute(value, AXES, route(lambda k, s, g: ((k + by) % SECTIONS, s)))  14.6 us
    ppermute x8, starting transfers between devices, across(): lax.ppermute(value, AXES, route(lambda k, s, g: ((k + by) % SECTIONS, s)))  9.59 us
    pallas_call x6, Pallas kernels, call(): pl.pallas_call(kernel, out_shape=[jax.ShapeDtypeStruct(shape, dtype) for...  9.44 us
    ppermute x2, waiting for transfers between devices, along(): return lax.ppermute(value, AXES, route(lambda k, s, g: (k, (s + by) % g)))  7.82 us
    ppermute x2, starting transfers between devices, along(): return lax.ppermute(value, AXES, route(lambda k, s, g: (k, (s + by) % g)))  6.44 us
  transfers between devices with their start and end apart: 10, of which 8 were waited for; matrix products, arithmetic and copies ran while one was open for 0% of the time, Pallas kernels for 2%

profile of v1, /device:TPU:6, one launch (start us, length us, event | category | flops | bytes accessed | tf_op | source)
XLA Modules:
  0.0 48.7 jit_solution(2089933191040702881)
XLA Ops:
  0.6 0.0 copy-start
  0.6 1.3 %shard_map.102 = (f32[6,8,128]{2,1,0:T(8,128)S(1)}, f32[4,6,3,8,128]{4,3,2,1,0:T(8,128)S(1)}, f32[6,3,8,128]{3,2,1,0:T(8,128)S(1)}, f32[16,6,8,128]{3,2,1,0:T(8,...) custom-call(f32[4,6,8,384]{3,2,1,0:T(8,128)} %flow.1, f32[6,8,384]{2,1,0:T(8,128)} %pigment.1, ...), custom_call_target="tpu_custom_call" | custom-call | tf_op jit(solution)/shard_map/pallas_call | solution.py:541
  1.9 1.3 %collective-permute-start.1 = (f32[6,8,128]{2,1,0:T(8,128)S(1)}, f32[6,8,128]{2,1,0:T(8,128)S(1)}, u32[]{:S(2)}, u32[]{:S(2)}) collective-permute-start(f32[6,8,128]{2,1,0:T(8,128)S(1)} %get-tuple-element.31), channel_id=1, source_target_pairs={{255,191},{0,192},{1,193},{2,194},{3,195},{4,196},{5,197},{6,198},... | collective-permute-start | bytes 73736 | tf_op jit(solution)/shard_map/ppermute | solution.py:562
  3.2 2.0 %collective-permute-start = (f32[6,8,128]{2,1,0:T(8,128)S(1)}, f32[6,8,128]{2,1,0:T(8,128)S(1)}, u32[]{:S(2)}, u32[]{:S(2)}) collective-permute-start(f32[6,8,128]{2,1,0:T(8,128)S(1)} %get-tuple-element.31), channel_id=1, source_target_pairs={{255,63},{0,64},{1,65},{2,66},{3,67},{4,68},{5,69},{6,70},{7,71},{... | collective-permute-start | bytes 73736 | tf_op jit(solution)/shard_map/ppermute | solution.py:562
  5.3 1.8 %collective-permute-done.1.from_right = f32[6,8,128]{2,1,0:T(8,128)S(1)} collective-permute-done((f32[6,8,128]{2,1,0:T(8,128)S(1)}, f32[6,8,128]{2,1,0:T(8,128)S(1)}, u32[]{:S(2)}, u32[]{:S(2)}) %collective-permute-start.1) | collective-permute-done | bytes 24608 | tf_op jit(solution)/shard_map/ppermute | solution.py:562
  7.1 0.0 collective-permute-done.from_left
  7.1 0.1 shard_map.103
  7.1 0.1 collective-permute-start.2
  7.2 6.4 %collective-permute-start.3 = (f32[15,6,8,128]{3,2,1,0:T(8,128)S(1)}, f32[15,6,8,128]{3,2,1,0:T(8,128)S(1)}, u32[]{:S(2)}, u32[]{:S(2)}) collective-permute-start(f32[15,6,8,128]{3,2,1,0:T(8,128)S(1)} %get-tuple-element.34), channel_id=1, source_target_pairs={{255,62},{0,255},{1,0},{2,1},{3,2},{4,3},{5,4},{6,5},{7,6},{8,7},{... | collective-permute-start | bytes 1105928 | tf_op jit(solution)/shard_map/ppermute | solution.py:566
  13.6 7.8 %collective-permute-done.2.above = f32[15,6,8,128]{3,2,1,0:T(8,128)S(1)} collective-permute-done((f32[15,6,8,128]{3,2,1,0:T(8,128)S(1)}, f32[15,6,8,128]{3,2,1,0:T(8,128)S(1)}, u32[]{:S(2)}, u32[]{:S(2)}) %collective-permute-start.2) | collective-permute-done | bytes 368672 | tf_op jit(solution)/shard_map/ppermute | solution.py:566
  21.4 0.0 collective-permute-done.3.below
  21.4 0.0 copy-done
  21.4 3.7 %shard_map.104 = (f32[24,8,128]{2,1,0:T(8,128)S(1)}, f32[24,8,128]{2,1,0:T(8,128)S(1)}, f32[24,8,128]{2,1,0:T(8,128)S(1)}, f32[4,6,3,32,128]{4,3,2,1,0:T(8,128)S(1)}, f32[16,6,16,128]{3,2,1,0:T(8,128)S(1)}) custom-call(f32[4,6,3,8,128]{4,3,2,1,0:T(8,128)S(1)} %get-tuple-element.27.flow, f32[6,3,8,128]{3,2,1,0:T(8,128)S(1)} %get-tuple-element.28.pigment, ...), custom_call_target="tpu_custom_call" | custom-call | tf_op jit(solution)/shard_map/pallas_call | solution.py:541
  25.1 3.2 %collective-permute-start.4 = (f32[24,8,128]{2,1,0:T(8,128)S(1)}, f32[24,8,128]{2,1,0:T(8,128)S(1)}, u32[]{:S(2)}, u32[]{:S(2)}) collective-permute-start(f32[24,8,128]{2,1,0:T(8,128)S(1)} %get-tuple-element.36), channel_id=1, source_target_pairs={{255,63},{0,64},{1,65},{2,66},{3,67},{4,68},{5,69},{6,70},{7,71},{... | collective-permute-start | bytes 294920 | tf_op jit(solution)/shard_map/ppermute | solution.py:562
  28.3 0.2 collective-permute-start.5
  28.5 0.8 %collective-permute-start.6 = (f32[24,8,128]{2,1,0:T(8,128)S(1)}, f32[24,8,128]{2,1,0:T(8,128)S(1)}, u32[]{:S(2)}, u32[]{:S(2)}) collective-permute-start(f32[24,8,128]{2,1,0:T(8,128)S(1)} %get-tuple-element.38), channel_id=1, source_target_pairs={{255,191},{0,192},{1,193},{2,194},{3,195},{4,196},{5,197},{6,198},... | collective-permute-start | bytes 294920 | tf_op jit(solution)/shard_map/ppermute | solution.py:562
  29.3 4.2 %collective-permute-done.4.from_a = f32[24,8,128]{2,1,0:T(8,128)S(1)} collective-permute-done((f32[24,8,128]{2,1,0:T(8,128)S(1)}, f32[24,8,128]{2,1,0:T(8,128)S(1)}, u32[]{:S(2)}, u32[]{:S(2)}) %collective-permute-start.4) | collective-permute-done | bytes 98336 | tf_op jit(solution)/shard_map/ppermute | solution.py:562
  33.4 2.0 %collective-permute-done.5.from_b = f32[24,8,128]{2,1,0:T(8,128)S(1)} collective-permute-done((f32[24,8,128]{2,1,0:T(8,128)S(1)}, f32[24,8,128]{2,1,0:T(8,128)S(1)}, u32[]{:S(2)}, u32[]{:S(2)}) %collective-permute-start.5) | collective-permute-done | bytes 98336 | tf_op jit(solution)/shard_map/ppermute | solution.py:562
  35.5 1.4 %collective-permute-done.6.from_c = f32[24,8,128]{2,1,0:T(8,128)S(1)} collective-permute-done((f32[24,8,128]{2,1,0:T(8,128)S(1)}, f32[24,8,128]{2,1,0:T(8,128)S(1)}, u32[]{:S(2)}, u32[]{:S(2)}) %collective-permute-start.6) | collective-permute-done | bytes 98336 | tf_op jit(solution)/shard_map/ppermute | solution.py:562
  36.9 2.8 %shard_map.105 = (f32[24,8,128]{2,1,0:T(8,128)S(1)}, f32[24,8,128]{2,1,0:T(8,128)S(1)}, f32[24,8,128]{2,1,0:T(8,128)S(1)}, f32[4,6,3,8,128]{4,3,2,1,0:T(8,128)S(1)}, f32[16,6,8,128]{3,2,1,0:T(8,128)S(1)}) custom-call(f32[24,8,128]{2,1,0:T(8,128)S(1)} %collective-permute-done.4.from_a, f32[24,8,128]{2,1,0:T(8,128)S(1)} %collective-permute-done.5.from_b, ...), custom_call_target="tpu_custom_call" | custom-call | tf_op jit(solution)/shard_map/pallas_call | solution.py:541
  39.7 0.1 collective-permute-start.7
  39.8 0.1 collective-permute-start.8
  39.9 1.9 %collective-permute-start.9 = (f32[24,8,128]{2,1,0:T(8,128)S(1)}, f32[24,8,128]{2,1,0:T(8,128)S(1)}, u32[]{:S(2)}, u32[]{:S(2)}) collective-permute-start(f32[24,8,128]{2,1,0:T(8,128)S(1)} %get-tuple-element.46), channel_id=1, source_target_pairs={{255,191},{0,192},{1,193},{2,194},{3,195},{4,196},{5,197},{6,198},... | collective-permute-start | bytes 294920 | tf_op jit(solution)/shard_map/ppermute | solution.py:562
  41.8 0.9 %shard_map.106 = (f32[4,6,8,384]{3,2,1,0:T(8,128)}, f32[16,6,8,128]{3,2,1,0:T(8,128)}) custom-call(f32[4,6,3,8,128]{4,3,2,1,0:T(8,128)S(1)} %get-tuple-element.41.flow_last, f32[16,6,8,128]{3,2,1,0:T(8,128)S(1)} %get-tuple-element.42.tracers_last), custom_call_target="tpu_custom_call" | custom-call | tf_op jit(solution)/shard_map/pallas_call | solution.py:541
  42.7 2.6 %collective-permute-done.7.from_a = f32[24,8,128]{2,1,0:T(8,128)S(1)} collective-permute-done((f32[24,8,128]{2,1,0:T(8,128)S(1)}, f32[24,8,128]{2,1,0:T(8,128)S(1)}, u32[]{:S(2)}, u32[]{:S(2)}) %collective-permute-start.7) | collective-permute-done | bytes 98336 | tf_op jit(solution)/shard_map/ppermute | solution.py:562
  45.3 1.0 %collective-permute-done.8.from_b = f32[24,8,128]{2,1,0:T(8,128)S(1)} collective-permute-done((f32[24,8,128]{2,1,0:T(8,128)S(1)}, f32[24,8,128]{2,1,0:T(8,128)S(1)}, u32[]{:S(2)}, u32[]{:S(2)}) %collective-permute-start.8) | collective-permute-done | bytes 98336 | tf_op jit(solution)/shard_map/ppermute | solution.py:562
  46.3 1.7 %collective-permute-done.9.from_c = f32[24,8,128]{2,1,0:T(8,128)S(1)} collective-permute-done((f32[24,8,128]{2,1,0:T(8,128)S(1)}, f32[24,8,128]{2,1,0:T(8,128)S(1)}, u32[]{:S(2)}, u32[]{:S(2)}) %collective-permute-start.9) | collective-permute-done | bytes 98336 | tf_op jit(solution)/shard_map/ppermute | solution.py:562
  48.0 0.7 %shard_map.107 = (f32[6,8,384]{2,1,0:T(8,128)}, f32[4,6,8,128]{3,2,1,0:T(8,128)}) custom-call(f32[24,8,128]{2,1,0:T(8,128)S(1)} %collective-permute-done.7.from_a, f32[24,8,128]{2,1,0:T(8,128)S(1)} %collective-permute-done.8.from_b, f32[24,8,128]{2,1,0:T(8,128)S(1)} %collective-permute-done.9.from_c), custom_call_target="tpu_custom_call" | custom-call | tf_op jit(solution)/shard_map/pallas_call | solution.py:541
Async XLA Ops:
  0.6 20.8 %copy-start = (f32[16,16]{1,0:T(8,128)S(1)}, f32[16,16]{1,0:T(8,128)}, u32[]{:S(2)}) copy-start(f32[16,16]{1,0:T(8,128)} %reaction.3) | copy-start | bytes 3076
  1.9 5.1 %collective-permute-start.1 = (f32[6,8,128]{2,1,0:T(8,128)S(1)}, f32[6,8,128]{2,1,0:T(8,128)S(1)}, u32[]{:S(2)}, u32[]{:S(2)}) collective-permute-start(f32[6,8,128]{2,1,0:T(8,128)S(1)} %get-tuple-element.31), channel_id=1, source_target_pairs={{255,191},{0,192},{1,193},{2,194},{3,195},{4,196},{5,197},{6,198},... | collective-permute-start | bytes 73736 | tf_op jit(solution)/shard_map/ppermute | solution.py:562
  3.2 3.8 %collective-permute-start = (f32[6,8,128]{2,1,0:T(8,128)S(1)}, f32[6,8,128]{2,1,0:T(8,128)S(1)}, u32[]{:S(2)}, u32[]{:S(2)}) collective-permute-start(f32[6,8,128]{2,1,0:T(8,128)S(1)} %get-tuple-element.31), channel_id=1, source_target_pairs={{255,63},{0,64},{1,65},{2,66},{3,67},{4,68},{5,69},{6,70},{7,71},{... | collective-permute-start | bytes 73736 | tf_op jit(solution)/shard_map/ppermute | solution.py:562
  7.1 14.3 %collective-permute-start.2 = (f32[15,6,8,128]{3,2,1,0:T(8,128)S(1)}, f32[15,6,8,128]{3,2,1,0:T(8,128)S(1)}, u32[]{:S(2)}, u32[]{:S(2)}) collective-permute-start(f32[15,6,8,128]{3,2,1,0:T(8,128)S(1)} %get-tuple-element.33), channel_id=1, source_target_pairs={{255,0},{0,1},{1,2},{2,3},{3,4},{4,5},{5,6},{6,7},{7,8},{8,9},{9,1... | collective-permute-start | bytes 1105928 | tf_op jit(solution)/shard_map/ppermute | solution.py:566
  7.2 14.2 %collective-permute-start.3 = (f32[15,6,8,128]{3,2,1,0:T(8,128)S(1)}, f32[15,6,8,128]{3,2,1,0:T(8,128)S(1)}, u32[]{:S(2)}, u32[]{:S(2)}) collective-permute-start(f32[15,6,8,128]{3,2,1,0:T(8,128)S(1)} %get-tuple-element.34), channel_id=1, source_target_pairs={{255,62},{0,255},{1,0},{2,1},{3,2},{4,3},{5,4},{6,5},{7,6},{8,7},{... | collective-permute-start | bytes 1105928 | tf_op jit(solution)/shard_map/ppermute | solution.py:566
  25.1 8.4 %collective-permute-start.4 = (f32[24,8,128]{2,1,0:T(8,128)S(1)}, f32[24,8,128]{2,1,0:T(8,128)S(1)}, u32[]{:S(2)}, u32[]{:S(2)}) collective-permute-start(f32[24,8,128]{2,1,0:T(8,128)S(1)} %get-tuple-element.36), channel_id=1, source_target_pairs={{255,63},{0,64},{1,65},{2,66},{3,67},{4,68},{5,69},{6,70},{7,71},{... | collective-permute-start | bytes 294920 | tf_op jit(solution)/shard_map/ppermute | solution.py:562
  28.3 7.1 %collective-permute-start.5 = (f32[24,8,128]{2,1,0:T(8,128)S(1)}, f32[24,8,128]{2,1,0:T(8,128)S(1)}, u32[]{:S(2)}, u32[]{:S(2)}) collective-permute-start(f32[24,8,128]{2,1,0:T(8,128)S(1)} %get-tuple-element.37), channel_id=1, source_target_pairs={{255,127},{0,128},{1,129},{2,130},{3,131},{4,132},{5,133},{6,134},... | collective-permute-start | bytes 294920 | tf_op jit(solution)/shard_map/ppermute | solution.py:562
  28.5 8.4 %collective-permute-start.6 = (f32[24,8,128]{2,1,0:T(8,128)S(1)}, f32[24,8,128]{2,1,0:T(8,128)S(1)}, u32[]{:S(2)}, u32[]{:S(2)}) collective-permute-start(f32[24,8,128]{2,1,0:T(8,128)S(1)} %get-tuple-element.38), channel_id=1, source_target_pairs={{255,191},{0,192},{1,193},{2,194},{3,195},{4,196},{5,197},{6,198},... | collective-permute-start | bytes 294920 | tf_op jit(solution)/shard_map/ppermute | solution.py:562
  39.7 5.6 %collective-permute-start.7 = (f32[24,8,128]{2,1,0:T(8,128)S(1)}, f32[24,8,128]{2,1,0:T(8,128)S(1)}, u32[]{:S(2)}, u32[]{:S(2)}) collective-permute-start(f32[24,8,128]{2,1,0:T(8,128)S(1)} %get-tuple-element.44), channel_id=1, source_target_pairs={{255,63},{0,64},{1,65},{2,66},{3,67},{4,68},{5,69},{6,70},{7,71},{... | collective-permute-start | bytes 294920 | tf_op jit(solution)/shard_map/ppermute | solution.py:562
  39.8 6.5 %collective-permute-start.8 = (f32[24,8,128]{2,1,0:T(8,128)S(1)}, f32[24,8,128]{2,1,0:T(8,128)S(1)}, u32[]{:S(2)}, u32[]{:S(2)}) collective-permute-start(f32[24,8,128]{2,1,0:T(8,128)S(1)} %get-tuple-element.45), channel_id=1, source_target_pairs={{255,127},{0,128},{1,129},{2,130},{3,131},{4,132},{5,133},{6,134},... | collective-permute-start | bytes 294920 | tf_op jit(solution)/shard_map/ppermute | solution.py:562
  39.9 8.1 %collective-permute-start.9 = (f32[24,8,128]{2,1,0:T(8,128)S(1)}, f32[24,8,128]{2,1,0:T(8,128)S(1)}, u32[]{:S(2)}, u32[]{:S(2)}) collective-permute-start(f32[24,8,128]{2,1,0:T(8,128)S(1)} %get-tuple-element.46), channel_id=1, source_target_pairs={{255,191},{0,192},{1,193},{2,194},{3,195},{4,196},{5,197},{6,198},... | collective-permute-start | bytes 294920 | tf_op jit(solution)/shard_map/ppermute | solution.py:562

commit v2 on v1

--- a/solution.py
+++ b/solution.py
@@ -45,22 +45,44 @@
 
 
 def edge_tile(planes):
-    lane = lanes(planes[0].shape[0])
+    pair = lanes(planes[0].shape[0]) // 2
     edges = jnp.zeros_like(planes[0])
     for a, x in enumerate(planes):
-        edges = jnp.where(lane == a, roll_lanes(x, a + 1), edges)
-        edges = jnp.where(lane == 64 + a, roll_lanes(x, 64 + a), edges)
+        edges = jnp.where(pair == a, roll_lanes(x, 2 * a + 1), edges)
     return edges
+
+
+def pack_rows(tracers, forcing, to_next, to_prev):
+    half = upper_half()
+    nt, levels = tracers.shape[0], tracers.shape[1]
+
+    def put(plane, pair, even, odd):
+        row, col = plane // 2, 3 * (plane % 2)
+        to_next[row, col + pair] = jnp.where(half, swap(even), odd)
+        to_prev[row, col + pair] = jnp.where(half, even, swap(odd))
+
+    for pair in range(levels // 2):
+        even, odd = 2 * pair, 2 * pair + 1
+        for a in range(nt):
+            put(a, pair, tracers[a, even], tracers[a, odd])
+        put(nt, pair, forcing[0, even], forcing[0, odd])
+        put(nt + 1, pair, forcing[1, even], forcing[1, odd])
+        growth = [jnp.exp(0.1 * forcing[2, l] - 0.05 * forcing[3, l]) for l in (even, odd)]
+        put(nt + 2, pair, growth[0], growth[1])
+        put(nt + 3, pair, jnp.zeros((8, 128), F32), jnp.zeros((8, 128), F32))
+    for row in range(10, 15):
+        for l in range(levels):
+            to_next[row, l] = jnp.zeros((8, 128), F32)
+            to_prev[row, l] = jnp.zeros((8, 128), F32)
 
 
 def load_kernel(
     flow, pigment, tracers, forcing, ocean, bottom,
-    border, flow_in, pigment_in, tracers_in, forcing_in, wet_rows,
+    to_next, to_prev, flow_in, pigment_in, tracers_in, forcing_in, wet_rows,
     ocean_rows, bottom_rows, mask_sems, sems,
 ):
     section, strip, group = place()
     levels = pigment.shape[0]
-    nt = tracers.shape[0]
     starts = [jnp.maximum(strip - 1, 0), strip, jnp.minimum(strip + 1, group - 1)]
     masks = []
     for i, start in enumerate(starts):
@@ -81,9 +103,18 @@
             )
         for copy in copies + masks:
             copy.start()
-        border[...] = jnp.zeros_like(border)
         for copy in copies + masks:
             copy.wait()
+
+        def level(l, carry):
+            for f in range(5):
+                for j in range(3):
+                    tile = flow_in[f, l, j] if f < 4 else pigment_in[l, j]
+                    to_next[3 * f + j, l] = tile
+                    to_prev[3 * f + j, l] = tile
+            return carry
+
+        lax.fori_loop(0, levels, level, 0)
 
     @pl.when(section != 3)
     def _():
@@ -97,12 +128,9 @@
             )
         for copy in copies + masks:
             copy.start()
-        for l in range(levels):
-            copies[2 * l].wait()
-            copies[2 * l + 1].wait()
-            border[l] = edge_tile([tracers_in[a, l] for a in range(nt)] + [forcing_in[1, l]])
-        for copy in masks:
+        for copy in copies + masks:
             copy.wait()
+        pack_rows(tracers_in, forcing_in, to_next, to_prev)
 
     inside = [(strip > 0).astype(jnp.int32), 1, (strip < group - 1).astype(jnp.int32)]
     for i in range(3):
@@ -111,55 +139,11 @@
             wet_rows[j, 8 * i : 8 * i + 8] = floor[:, 128 * j : 128 * j + 128]
 
 
-def open_edges(section, from_left, from_right, rows):
-    lane = lanes(rows)
-    left = jnp.where(section > 0, from_left, 0.0)
-    right = jnp.where(section < 2, from_right, 0.0)
-    return jnp.where(lane < 64, left, right)
-
-
-def rows_kernel(flow, pigment, tracers, forcing, from_left, from_right, to_next, to_prev, edges):
-    section, _, _ = place()
-    levels = pigment.shape[0]
-    nt = tracers.shape[0]
-
-    @pl.when(section == 3)
-    def _():
-        def level(l, carry):
-            for f in range(5):
-                for j in range(3):
-                    tile = flow[f, l, j] if f < 4 else pigment[l, j]
-                    to_next[3 * f + j, l] = tile
-                    to_prev[3 * f + j, l] = tile
-            return carry
-
-        lax.fori_loop(0, levels, level, 0)
-        edges[...] = jnp.zeros_like(edges)
-
-    @pl.when(section != 3)
-    def _():
-        half = upper_half()
-        for l in range(levels):
-            edges[l] = open_edges(section, from_left[l], from_right[l], 8)
-
-        def put(plane, pair, even, odd):
-            row, col = plane // 2, 3 * (plane % 2)
-            to_next[row, col + pair] = jnp.where(half, swap(even), odd)
-            to_prev[row, col + pair] = jnp.where(half, even, swap(odd))
-
-        for pair in range(3):
-            even, odd = 2 * pair, 2 * pair + 1
-            for a in range(nt):
-                put(a, pair, tracers[a, even], tracers[a, odd])
-            put(nt, pair, forcing[0, even], forcing[0, odd])
-            put(nt + 1, pair, forcing[1, even], forcing[1, odd])
-            growth = [jnp.exp(0.1 * forcing[2, l] - 0.05 * forcing[3, l]) for l in (even, odd)]
-            put(nt + 2, pair, growth[0], growth[1])
-            put(nt + 3, pair, edges[even], edges[odd])
-        for row in range(10, 15):
-            for l in range(levels):
-                to_next[row, l] = jnp.zeros((8, 128), F32)
-                to_prev[row, l] = jnp.zeros((8, 128), F32)
+def side_columns(section, from_left, from_right):
+    even = lanes(from_left.shape[0]) % 2 == 0
+    east = jnp.where(section < 2, roll_lanes(from_right, -1), 0.0)
+    west = jnp.where(section > 0, roll_lanes(from_left, 1), 0.0)
+    return jnp.where(even, east, west)
 
 
 def shifted(tiles):
@@ -175,7 +159,7 @@
 
 
 def substep(source, target, heat, wet_rows, tiles, read_at, write_at, heat_at, wet_at):
-    levels = heat.shape[0]
+    levels = target.shape[1]
     thirds = 3
     zero = jnp.zeros((8, 128), F32)
 
@@ -187,7 +171,7 @@
             slope_x, slope_y = carry[tile]
 
             def load(f, by):
-                return [source[f, l, j, row + by : row + by + 8] for j in range(thirds)]
+                return [source[f][l, j, row + by : row + by + 8] for j in range(thirds)]
 
             centre = [load(f, 0) for f in range(4)]
             up = [load(f, -1) for f in range(4)]
@@ -209,11 +193,13 @@
                 b = 0.05 + 0.05 * un
                 c = 0.05 - 0.05 * ve
                 d = 0.05 + 0.05 * vw
-                h = heat[l, j, heat_at + 8 * tile : heat_at + 8 * tile + 8]
+                kept = 0.8 * t
+                if heat is not None:
+                    kept = kept + heat[l, j, heat_at + 8 * tile : heat_at + 8 * tile + 8]
                 results = (
                     0.79 * u + 0.1 * v - 0.01 * px + 0.05 * ((un + us) + (ue + uw)),
                     0.79 * v - 0.1 * u - 0.01 * py + 0.05 * ((vn + vs) + (ve + vw)),
-                    (0.8 * t + h) + ((ts * a + tn * b) + (te * c + tw * d)),
+                    kept + ((ts * a + tn * b) + (te * c + tw * d)),
                     0.8 * s + ((ss * a + sn * b) + (se * c + sw * d)),
                 )
                 for f in range(4):
@@ -256,14 +242,15 @@
     )
 
 
-def tracer_level(centre, up, down, edges, weights, reaction):
+def tracer_level(centre, up, down, sides, weights, reaction):
     nt = len(centre)
-    lane = lanes(edges.shape[0])
+    lane = lanes(centre[0].shape[0])
     a, b, c, d, keep, grow = weights
     results = []
     for i in range(nt):
-        east = jnp.where(lane == 127, roll_lanes(edges, 63 - i), roll_lanes(centre[i], 127))
-        west = jnp.where(lane == 0, roll_lanes(edges, -i), roll_lanes(centre[i], 1))
+        side = 0.0 if sides is None else roll_lanes(sides, -2 * i - 1)
+        east = jnp.where(lane == 127, side, roll_lanes(centre[i], 127))
+        west = jnp.where(lane == 0, side, roll_lanes(centre[i], 1))
         mixed = reaction[i, 0] * centre[0]
         for k in range(1, nt):
             mixed = mixed + reaction[i, k] * centre[k]
@@ -278,13 +265,56 @@
     return 0.25 * (first * first + second * second)
 
 
+def gather_kernel(tracers, forcing, above, below, cells, winds, border):
+    section, strip, group = place()
+    nt, levels = tracers.shape[0], tracers.shape[1]
+    low = spread(strip > 0)
+    high = spread(strip < group - 1)
+
+    @pl.when(section == 3)
+    def _():
+        border[...] = jnp.zeros_like(border)
+
+    @pl.when(section != 3)
+    def _():
+        half = upper_half()
+
+        def halo(message, plane, pair, odd, upward):
+            tile = message[plane // 2, 3 * (plane % 2) + pair]
+            return swap(tile) if odd != upward else tile
+
+        def build(plane, own, l, masked):
+            pair, odd = l // 2, l % 2 == 1
+            up = halo(above, plane, pair, odd, False)
+            down = halo(below, plane, pair, not odd, False)
+            if masked:
+                up, down = up * low, down * high
+            return extend(own, up, down, half)
+
+        lane = lanes(16)
+        for l in range(levels):
+            v = build(nt + 1, forcing[1, l], l, False)
+            scale = 0.05 + jnp.where(lane == 0, -0.05, 0.05) * v
+            products = []
+            for a in range(nt):
+                cell = build(a, tracers[a, l], l, True)
+                cells[a, l, 8:24] = cell
+                products.append(scale * cell)
+            winds[0, l, 8:24] = build(nt, forcing[0, l], l, False)
+            winds[1, l, 8:24] = v
+            growth = jnp.exp(0.1 * forcing[2, l] - 0.05 * forcing[3, l])
+            winds[2, l, 8:24] = build(nt + 2, growth, l, False)
+            border[l] = edge_tile(products)
+
+
 def first_kernel(
-    flow, pigment, tracers, forcing, edges, above, below, wet_rows, reaction,
-    out_a, out_b, out_c, flow_next, tracers_next, field_0, field_1, field_2, field_3, heat, cells, winds,
+    flow, pigment, above, below, cells, winds, wet_rows, reaction,
+    send_a, send_b, send_c, flow_next, partial,
+    field_0, field_1, field_2, field_3, heat,
 ):
     section, strip, group = place()
     levels = pigment.shape[0]
-    nt = tracers.shape[0]
+    nt = cells.shape[0]
     low = spread(strip > 0)
     high = spread(strip < group - 1)
 
@@ -306,12 +336,12 @@
             return (above if tile == 0 else below)[12 + j, l]
 
         fill_heat(load, heat)
-        substep(field_0, field_1, heat, wet_rows, 3, 8, 8, 0, 0)
-        substep(field_1, field_2, heat, wet_rows, 3, 8, 8, 0, 0)
-        substep(field_2, field_3, heat, wet_rows, 3, 8, 8, 0, 0)
-        substep(field_3, flow_next, heat, wet_rows, 2, 12, 8, 4, 4)
+        substep(planes(field_0), field_1, heat, wet_rows, 3, 8, 8, 0, 0)
+        substep(planes(field_1), field_2, heat, wet_rows, 3, 8, 8, 0, 0)
+        substep(planes(field_2), field_3, heat, wet_rows, 3, 8, 8, 0, 0)
+        substep(planes(field_3), flow_next, heat, wet_rows, 2, 12, 8, 4, 4)
         lane = lanes(8)
-        outs = (out_a, out_b, out_c)
+        outs = (send_a, send_b, send_c)
         sub = lax.broadcasted_iota(jnp.int32, (8, 128), 0)
 
         def mean(f, l, row, j):
@@ -348,64 +378,73 @@
             outs[j][18] = edge_v[j]
             outs[j][19] = rows_above[j]
             outs[j][20] = rows_below[j]
-            for i in range(21, 24):
-                outs[j][i] = jnp.zeros((8, 128), F32)
 
     @pl.when(section != 3)
     def _():
-        half = upper_half()
-
-        def halo(message, plane, pair, odd, upward):
-            tile = message[plane // 2, 3 * (plane % 2) + pair]
-            return swap(tile) if odd != upward else tile
-
-        def build(plane, own, l, masked):
-            pair, odd = l // 2, l % 2 == 1
-            up = halo(above, plane, pair, odd, False)
-            down = halo(below, plane, pair, not odd, False)
-            if masked:
-                up, down = up * low, down * high
-            return extend(own, up, down, half)
-
-        for l in range(levels):
-            for a in range(nt):
-                cells[a, l, 8:24] = build(a, tracers[a, l], l, True)
-            winds[0, l, 8:24] = build(nt, forcing[0, l], l, False)
-            winds[1, l, 8:24] = build(nt + 1, forcing[1, l], l, False)
-            growth = jnp.exp(0.1 * forcing[2, l] - 0.05 * forcing[3, l])
-            winds[2, l, 8:24] = build(nt + 2, growth, l, False)
-            winds[3, l, 8:24] = build(nt + 3, edges[l], l, False)
         floor = wet_rows[section, 4:20]
-        lane = lanes(16)
-        inside = lax.broadcasted_iota(jnp.int32, (16, 128), 0)
 
         def level(l, carry):
-            border = winds[3, l, 8:24]
             v = winds[1, l, 8:24]
-            v_east = jnp.where(lane == 127, roll_lanes(border, 63 - nt), roll_lanes(v, 127))
-            v_west = jnp.where(lane == 0, roll_lanes(border, -nt), roll_lanes(v, 1))
             weights = tracer_weights(
-                winds[0, l, 7:23], winds[0, l, 9:25], v_east, v_west, winds[2, l, 8:24], floor > l
+                winds[0, l, 7:23], winds[0, l, 9:25], roll_lanes(v, 127), roll_lanes(v, 1),
+                winds[2, l, 8:24], floor > l,
             )
             results = tracer_level(
                 [cells[a, l, 8:24] for a in range(nt)],
                 [cells[a, l, 7:23] for a in range(nt)],
                 [cells[a, l, 9:25] for a in range(nt)],
-                border, weights, reaction,
+                None, weights, reaction,
             )
             for a in range(nt):
-                tracers_next[a, l] = results[a]
-            edge = edge_tile(results)
-            shade = pigment_of(results[0], results[1])
-            shade = jnp.where((inside > 0) & (inside < 15), shade, 0.0)
-            for out in (out_a, out_b, out_c):
+                partial[a, l] = results[a]
+            return carry
+
+        lax.fori_loop(0, levels, level, 0)
+
+
+def sides_kernel(
+    from_left, from_right, send_a, send_b, send_c, partial, wet_rows,
+    out_a, out_b, out_c, tracers_next,
+):
+    section, _, _ = place()
+    nt, levels = partial.shape[0], partial.shape[1]
+    outs = (out_a, out_b, out_c)
+
+    @pl.when(section == 3)
+    def _():
+        for out, send in zip(outs, (send_a, send_b, send_c)):
+            out[...] = send[...]
+
+    @pl.when(section != 3)
+    def _():
+        floor = wet_rows[section, 4:20]
+        lane = lanes(16)
+        rim = (lane == 0) | (lane == 127)
+        row = lax.broadcasted_iota(jnp.int32, (16, 128), 0)
+        inside = (row > 0) & (row < 15)
+
+        def level(l, carry):
+            sides = side_columns(section, from_left[l], from_right[l])
+            wet_rim = rim & (floor > l)
+            shades = []
+            for a in range(nt):
+                side = jnp.where(wet_rim, roll_lanes(sides, -2 * a - 1), 0.0)
+                cell = partial[a, l] + side
+                tracers_next[a, l] = cell
+                if a < 2:
+                    shades.append(cell)
+            edge = edge_tile([tracers_next[a, l, 4:12] for a in range(nt)])
+            shade = jnp.where(inside, pigment_of(shades[0], shades[1]), 0.0)
+            for out in outs:
                 out[2 * l] = shade[:8]
                 out[2 * l + 1] = shade[8:]
-                out[12 + 2 * l] = edge[:8]
-                out[13 + 2 * l] = edge[8:]
+                out[12 + l] = edge
             return carry
 
-        lax.fori_loop(0, levels, level, 0)
+        lax.fori_loop(0, levels, level, 0, unroll=2)
+        for out in outs:
+            for i in range(18, 21):
+                out[i] = jnp.zeros((8, 128), F32)
 
 
 def roll_rows(x, by):
@@ -413,9 +452,21 @@
     return x if by == 0 else pltpu.roll(x, by, 0)
 
 
+def planes(buffer):
+    return [buffer.at[f] for f in range(4)]
+
+
+def early_kernel(flow_next, wet_rows, early):
+    section, _, _ = place()
+
+    @pl.when(section == 3)
+    def _():
+        substep(planes(flow_next), early, None, wet_rows, 2, 8, 8, 0, 4)
+
+
 def second_kernel(
-    from_a, from_b, from_c, flow_next, tracers_next, wet_rows, reaction,
-    out_a, out_b, out_c, flow_last, tracers_last, field_0, field_1, field_2, heat, winds,
+    from_a, from_b, from_c, early, tracers_next, wet_rows, reaction,
+    out_a, out_b, out_c, flow_last, tracers_last, warm, field_1, field_2, heat, winds,
 ):
     section, _, _ = place()
     levels = heat.shape[0]
@@ -429,15 +480,24 @@
             return shades[j][2 * l + tile]
 
         fill_heat(load, heat)
-        substep(flow_next, field_0, heat, wet_rows, 2, 8, 8, 0, 4)
-        substep(field_0, field_1, heat, wet_rows, 2, 8, 8, 0, 4)
-        substep(field_1, field_2, heat, wet_rows, 2, 8, 8, 0, 4)
-        substep(field_2, flow_last, heat, wet_rows, 1, 12, 0, 4, 8)
+
+        def warm_up(l, carry):
+            for j in range(3):
+                heated = jnp.where(wet_rows[j, 4:20] > l, heat[l, j], 0.0)
+                warm[l, j, 8:24] = early[2, l, j, 8:24] + heated
+            return carry
+
+        lax.fori_loop(0, levels, warm_up, 0)
+        first = planes(early)
+        first[2] = warm
+        substep(first, field_1, heat, wet_rows, 2, 8, 8, 0, 4)
+        substep(planes(field_1), field_2, heat, wet_rows, 2, 8, 8, 0, 4)
+        substep(planes(field_2), flow_last, heat, wet_rows, 1, 12, 0, 4, 8)
         outs = (out_a, out_b, out_c)
         for l in range(levels):
             for j in range(3):
                 for f in range(2):
-                    total = field_0[f, l, j, 12:20] + field_1[f, l, j, 12:20]
+                    total = early[f, l, j, 12:20] + field_1[f, l, j, 12:20]
                     total = total + field_2[f, l, j, 12:20]
                     outs[j][6 * f + l] = 0.25 * (total + flow_last[f, l, j])
                 outs[j][12 + l] = flow_last[2, l, j]
@@ -465,12 +525,7 @@
                 lane == 127, roll_lanes(edge_v, 126 - 2 * l), roll_lanes(v, 127)
             )
             winds[36 + l] = jnp.where(lane == 0, roll_lanes(edge_v, -2 * l), roll_lanes(v, 1))
-            borders = [
-                open_edges(section, from_a[12 + 2 * l + i], from_c[12 + 2 * l + i], 8)
-                for i in range(2)
-            ]
-            half = upper_half()
-            winds[42 + l] = swap(jnp.where(half, borders[1], borders[0]))
+            winds[42 + l] = side_columns(section, from_a[12 + l], from_c[12 + l])
         floor = wet_rows[section, 8:16]
 
         def level(l, carry):
@@ -562,8 +617,19 @@
     return lax.ppermute(value, AXES, route(lambda k, s, g: ((k + by) % SECTIONS, s)))
 
 
+def opposite(value):
+    def target(k, s, g):
+        if k % 2 == 1:
+            return (k + 2) % SECTIONS, s
+        if s in (0, g - 1):
+            return k, g - 1 - s
+        return k, s + 1 if s % 2 == 1 else s - 1
+
+    return lax.ppermute(value, AXES, route(target))
+
+
 def along(value, by):
-    return lax.ppermute(value, AXES, route(lambda k, s, g: (k, (s + by) % g)))
+    return lax.ppermute(value, AXES, route(lambda k, s, g: divmod((k * g + s + by) % (SECTIONS * g), g)))
 
 
 def on_device(flow_fields, chlorophyll_lag, tracers, forcing, ocean_mask, bottom, reaction):
@@ -571,10 +637,12 @@
     nt = tracers.shape[0]
     breadth = flow_fields.shape[3]
     vmem, smem, hbm = pltpu.VMEM, pltpu.SMEM, pltpu.HBM
-    border, flow, pigment, tracers, forcing, wet_rows = call(
+    message = (15, levels, 8, 128)
+    to_next, to_prev, flow, pigment, tracers, forcing, wet_rows = call(
         load_kernel,
         [
-            ((levels, 8, 128), F32), ((4, levels, 3, 8, 128), F32), ((levels, 3, 8, 128), F32),
+            (message, F32), (message, F32),
+            ((4, levels, 3, 8, 128), F32), ((levels, 3, 8, 128), F32),
             (tracers.shape, F32), (forcing.shape, F32), ((3, 24, 128), jnp.int32),
         ],
         (flow_fields, chlorophyll_lag, tracers, forcing, ocean_mask, bottom),
@@ -586,51 +654,62 @@
             pltpu.SemaphoreType.DMA((2 * levels,)),
         ),
     )
+    above = along(to_next, 1)
+    below = along(to_prev, -1)
+    cells, winds, border = call(
+        gather_kernel,
+        [((nt, levels, 32, 128), F32), ((3, levels, 32, 128), F32), ((levels, 16, 128), F32)],
+        (tracers, forcing, above, below),
+        (vmem,) * 4,
+    )
     from_left = across(border, 1)
     from_right = across(border, -1)
-    message = (15, levels, 8, 128)
-    to_next, to_prev, edges = call(
-        rows_kernel,
-        [(message, F32), (message, F32), ((levels, 8, 128), F32)],
-        (flow, pigment, tracers, forcing, from_left, from_right),
-        (vmem,) * 6,
-    )
-    above = along(to_next, 1)
-    below = along(to_prev, -1)
-    exchange = ((24, 8, 128), F32)
-    sent = call(
+    exchange = ((21, 8, 128), F32)
+    *sends, flow_next, partial = call(
         first_kernel,
         [
             exchange, exchange, exchange,
             ((4, levels, 3, 32, 128), F32), ((nt, levels, 16, 128), F32),
         ],
-        (flow, pigment, tracers, forcing, edges, above, below, wet_rows, reaction),
-        (vmem,) * 8 + (smem,),
+        (flow, pigment, above, below, cells, winds, wet_rows, reaction),
+        (vmem,) * 7 + (smem,),
         (
             *[pltpu.VMEM((4, levels, 3, 40, 128), F32) for _ in range(4)],
             pltpu.VMEM((levels, 3, 24, 128), F32),
-            pltpu.VMEM((nt, levels, 32, 128), F32),
-            pltpu.VMEM((4, levels, 32, 128), F32),
         ),
     )
-    from_b = across(sent[1], 2)
+    *sent, tracers_next = call(
+        sides_kernel,
+        [exchange, exchange, exchange, ((nt, levels, 16, 128), F32)],
+        (from_left, from_right, *sends, partial, wet_rows),
+        (vmem,) * 7,
+    )
+    from_b = opposite(sent[1])
     from_a = across(sent[0], 1)
     from_c = across(sent[2], -1)
+    (early,) = call(
+        early_kernel,
+        [((4, levels, 3, 32, 128), F32)],
+        (flow_next, wet_rows),
+        (vmem, vmem),
+    )
+    exchange = ((24, 8, 128), F32)
     last = call(
         second_kernel,
         [
             exchange, exchange, exchange,
             ((4, levels, 3, 8, 128), F32), ((nt, levels, 8, 128), F32),
         ],
-        (from_a, from_b, from_c, sent[3], sent[4], wet_rows, reaction),
+        (from_a, from_b, from_c, early, tracers_next, wet_rows, reaction),
         (vmem,) * 6 + (smem,),
         (
-            *[pltpu.VMEM((4, levels, 3, 32, 128), F32) for _ in range(3)],
+            pltpu.VMEM((levels, 3, 32, 128), F32),
+            *[pltpu.VMEM((4, levels, 3, 32, 128), F32) for _ in range(2)],
             pltpu.VMEM((levels, 3, 16, 128), F32),
             pltpu.VMEM((48, 8, 128), F32),
         ),
     )
-    final_b = across(last[1], 2)
+    final_b = opposite(last[1])
     final_a = across(last[0], 1)
     final_c = across(last[2], -1)
     flow_out, tracers_out = call(

time: 49 us -> 44.8 us (0.914)
  waiting for transfers between devices: 22.5 us -> 18.3 us
    ppermute x8 -> x6, waiting for transfers between devices: 14.6 us -> 4.74 us  [across(): lax.ppermute(value, AXES, route(lambda k, s, g: ((k + by) % SECTIONS, s)))]
    ppermute x2 -> x4, waiting for transfers between devices: 7.82 us -> 13.6 us  [the longest x2 7.78 us: along(): lax.ppermute(value, AXES, route(lambda k, s, g: divmod((k * g + s + by) %...]
    ppermute x2 -> x4, starting transfers between devices: 6.44 us -> 8.81 us  [the longest x2 8.17 us: along(): lax.ppermute(value, AXES, route(lambda k, s, g: divmod((k * g + s + by) %...]
    ppermute x8 -> x6, starting transfers between devices: 9.59 us -> 7.35 us  [across(): lax.ppermute(value, AXES, route(lambda k, s, g: ((k + by) % SECTIONS, s)))]
    pallas_call x6 -> x8, Pallas kernels: 9.44 us -> 9.48 us  [call(): pl.pallas_call(kernel, out_shape=[jax.ShapeDtypeStruct(shape, dtype) for...]
  transfers between devices with their start and end apart: 10 -> 10, of which waited for: 8 -> 7; matrix products, arithmetic and copies ran while one was open for 0% -> 0% of each run, Pallas kernels for 2% -> 11%
where the time goes in v2:
time: 44.8 us; the launch traced here: 44.7 us
  waiting for transfers between devices  18.3 us (41%)
  starting transfers between devices  16.2 us (36%)
  Pallas kernels  9.48 us (21%)
  between operations  0.72 us (2%)
    pallas_call x8, Pallas kernels, call(): pl.pallas_call(kernel, out_shape=[jax.ShapeDtypeStruct(shape, dtype) for...  9.48 us
    ppermute x2, starting transfers between devices, along(): lax.ppermute(value, AXES, route(lambda k, s, g: divmod((k * g + s + by) %...  8.17 us
    ppermute x2, waiting for transfers between devices, along(): lax.ppermute(value, AXES, route(lambda k, s, g: divmod((k * g + s + by) %...  7.78 us
    ppermute x6, starting transfers between devices, across(): lax.ppermute(value, AXES, route(lambda k, s, g: ((k + by) % SECTIONS, s)))  7.35 us
    ppermute x2, waiting for transfers between devices, opposite(): return lax.ppermute(value, AXES, route(target))  5.78 us
    ppermute x6, waiting for transfers between devices, across(): lax.ppermute(value, AXES, route(lambda k, s, g: ((k + by) % SECTIONS, s)))  4.74 us
  transfers between devices with their start and end apart: 10, of which 7 were waited for; matrix products, arithmetic and copies ran while one was open for 0% of the time, Pallas kernels for 11%

profile of v2, /device:TPU:6, one launch (start us, length us, event | category | flops | bytes accessed | tf_op | source)
XLA Modules:
  0.0 44.7 jit_solution(542195760205685737)
XLA Ops:
  0.6 1.4 %shard_map.102 = (f32[15,6,8,128]{3,2,1,0:T(8,128)S(1)}, f32[15,6,8,128]{3,2,1,0:T(8,128)S(1)}, f32[4,6,3,8,128]{4,3,2,1,0:T(8,128)S(1)}, f32[6,3,8,128]{3,2,1,0...) custom-call(f32[4,6,8,384]{3,2,1,0:T(8,128)} %flow.1, ...), custom_call_target="tpu_custom_call" | custom-call | tf_op jit(solution)/shard_map/pallas_call | solution.py:596
  2.0 0.0 copy-start
  2.0 0.1 collective-permute-start
  2.1 8.1 %collective-permute-start.1 = (f32[15,6,8,128]{3,2,1,0:T(8,128)S(1)}, f32[15,6,8,128]{3,2,1,0:T(8,128)S(1)}, u32[]{:S(2)}, u32[]{:S(2)}) collective-permute-start(f32[15,6,8,128]{3,2,1,0:T(8,128)S(1)} %get-tuple-element.35), channel_id=1, source_target_pairs={{255,254},{0,255},{1,0},{2,1},{3,2},{4,3},{5,4},{6,5},{7,6},{8,7},... | collective-permute-start | bytes 1105928 | tf_op jit(solution)/shard_map/ppermute | solution.py:632
  10.2 7.8 %collective-permute-done.above = f32[15,6,8,128]{3,2,1,0:T(8,128)S(1)} collective-permute-done((f32[15,6,8,128]{3,2,1,0:T(8,128)S(1)}, f32[15,6,8,128]{3,2,1,0:T(8,128)S(1)}, u32[]{:S(2)}, u32[]{:S(2)}) %collective-permute-start) | collective-permute-done | bytes 368672 | tf_op jit(solution)/shard_map/ppermute | solution.py:632
  18.0 0.0 collective-permute-done.1.below
  18.0 1.2 %collective-permute-start.3 = (f32[6,16,128]{2,1,0:T(8,128)S(1)}, f32[6,16,128]{2,1,0:T(8,128)S(1)}, u32[]{:S(2)}, u32[]{:S(2)}) collective-permute-start(f32[6,16,128]{2,1,0:T(8,128)S(1)} %get-tuple-element.36), channel_id=1, source_target_pairs={{255,191},{0,192},{1,193},{2,194},{3,195},{4,196},{5,197},{6,198},... | collective-permute-start | bytes 147464 | tf_op jit(solution)/shard_map/ppermute | solution.py:617
  19.2 2.1 %collective-permute-start.2 = (f32[6,16,128]{2,1,0:T(8,128)S(1)}, f32[6,16,128]{2,1,0:T(8,128)S(1)}, u32[]{:S(2)}, u32[]{:S(2)}) collective-permute-start(f32[6,16,128]{2,1,0:T(8,128)S(1)} %get-tuple-element.36), channel_id=1, source_target_pairs={{255,63},{0,64},{1,65},{2,66},{3,67},{4,68},{5,69},{6,70},{7,71},{... | collective-permute-start | bytes 147464 | tf_op jit(solution)/shard_map/ppermute | solution.py:617
  21.3 0.0 copy-done
  21.3 3.6 %shard_map.104 = (f32[21,8,128]{2,1,0:T(8,128)S(1)}, f32[21,8,128]{2,1,0:T(8,128)S(1)}, f32[21,8,128]{2,1,0:T(8,128)S(1)}, f32[4,6,3,32,128]{4,3,2,1,0:T(8,128)S(1)}, f32[16,6,16,128]{3,2,1,0:T(8,128)S(1)}) custom-call(f32[4,6,3,8,128]{4,3,2,1,0:T(8,128)S(1)} %get-tuple-element.37.flow, f32[6,3,8,128]{3,2,1,0:T(8,128)S(1)} %get-tuple-element.38.pigment, ...), custom_call_target="tpu_custom_call" | custom-call | tf_op jit(solution)/shard_map/pallas_call | solution.py:596
  24.9 0.0 collective-permute-done.3.from_right
  25.0 0.0 collective-permute-done.2.from_left
  25.0 2.6 %collective-permute-start.4 = (f32[21,8,128]{2,1,0:T(8,128)S(1)}, f32[21,8,128]{2,1,0:T(8,128)S(1)}, u32[]{:S(2)}, u32[]{:S(2)}) collective-permute-start(f32[21,8,128]{2,1,0:T(8,128)S(1)} %get-tuple-element.46), channel_id=1, source_target_pairs={{255,63},{0,64},{1,65},{2,66},{3,67},{4,68},{5,69},{6,70},{7,71},{... | collective-permute-start | bytes 258056 | tf_op jit(solution)/shard_map/ppermute | solution.py:617
  27.6 0.0 collective-permute-start.5
  27.6 0.0 collective-permute-start.6
  27.6 0.5 %shard_map.106.early = f32[4,6,3,32,128]{4,3,2,1,0:T(8,128)S(1)} custom-call(f32[4,6,3,32,128]{4,3,2,1,0:T(8,128)S(1)} %get-tuple-element.49.flow_next, s32[3,24,128]{2,1,0:T(8,128)S(1)} %get-tuple-element.41.wet_rows), custom_call_target="tpu_custom_call" | custom-call | tf_op jit(solution)/shard_map/pallas_call | solution.py:596
  28.1 1.5 %collective-permute-done.4.from_a = f32[21,8,128]{2,1,0:T(8,128)S(1)} collective-permute-done((f32[21,8,128]{2,1,0:T(8,128)S(1)}, f32[21,8,128]{2,1,0:T(8,128)S(1)}, u32[]{:S(2)}, u32[]{:S(2)}) %collective-permute-start.4) | collective-permute-done | bytes 86048 | tf_op jit(solution)/shard_map/ppermute | solution.py:617
  29.7 4.0 %collective-permute-done.5.from_b = f32[21,8,128]{2,1,0:T(8,128)S(1)} collective-permute-done((f32[21,8,128]{2,1,0:T(8,128)S(1)}, f32[21,8,128]{2,1,0:T(8,128)S(1)}, u32[]{:S(2)}, u32[]{:S(2)}) %collective-permute-start.5) | collective-permute-done | bytes 86048 | tf_op jit(solution)/shard_map/ppermute | solution.py:628
  33.7 0.5 %collective-permute-done.6.from_c = f32[21,8,128]{2,1,0:T(8,128)S(1)} collective-permute-done((f32[21,8,128]{2,1,0:T(8,128)S(1)}, f32[21,8,128]{2,1,0:T(8,128)S(1)}, u32[]{:S(2)}, u32[]{:S(2)}) %collective-permute-start.6) | collective-permute-done | bytes 86048 | tf_op jit(solution)/shard_map/ppermute | solution.py:617
  34.2 2.3 %shard_map.107 = (f32[24,8,128]{2,1,0:T(8,128)S(1)}, f32[24,8,128]{2,1,0:T(8,128)S(1)}, f32[24,8,128]{2,1,0:T(8,128)S(1)}, f32[4,6,3,8,128]{4,3,2,1,0:T(8,128)S(1)}, f32[16,6,8,128]{3,2,1,0:T(8,128)S(1)}) custom-call(f32[21,8,128]{2,1,0:T(8,128)S(1)} %collective-permute-done.4.from_a, f32[21,8,128]{2,1,0:T(8,128)S(1)} %collective-permute-done.5.from_b, ...), custom_call_target="tpu_custom_call" | custom-call | tf_op jit(solution)/shard_map/pallas_call | solution.py:596
  36.5 0.3 collective-permute-start.7
  36.8 0.6 %collective-permute-start.8 = (f32[24,8,128]{2,1,0:T(8,128)S(1)}, f32[24,8,128]{2,1,0:T(8,128)S(1)}, u32[]{:S(2)}, u32[]{:S(2)}) collective-permute-start(f32[24,8,128]{2,1,0:T(8,128)S(1)} %get-tuple-element.55), channel_id=1, source_target_pairs={{255,62},{0,1},{1,0},{2,3},{3,2},{4,5},{5,4},{6,7},{7,6},{8,9},{9,... | collective-permute-start | bytes 294920 | tf_op jit(solution)/shard_map/ppermute | solution.py:628
  37.5 1.2 %collective-permute-start.9 = (f32[24,8,128]{2,1,0:T(8,128)S(1)}, f32[24,8,128]{2,1,0:T(8,128)S(1)}, u32[]{:S(2)}, u32[]{:S(2)}) collective-permute-start(f32[24,8,128]{2,1,0:T(8,128)S(1)} %get-tuple-element.56), channel_id=1, source_target_pairs={{255,191},{0,192},{1,193},{2,194},{3,195},{4,196},{5,197},{6,198},... | collective-permute-start | bytes 294920 | tf_op jit(solution)/shard_map/ppermute | solution.py:617
  38.6 0.9 %shard_map.108 = (f32[4,6,8,384]{3,2,1,0:T(8,128)}, f32[16,6,8,128]{3,2,1,0:T(8,128)}) custom-call(f32[4,6,3,8,128]{4,3,2,1,0:T(8,128)S(1)} %get-tuple-element.51.flow_last, f32[16,6,8,128]{3,2,1,0:T(8,128)S(1)} %get-tuple-element.52.tracers_last), custom_call_target="tpu_custom_call" | custom-call | tf_op jit(solution)/shard_map/pallas_call | solution.py:596
  39.5 1.7 %collective-permute-done.7.from_a = f32[24,8,128]{2,1,0:T(8,128)S(1)} collective-permute-done((f32[24,8,128]{2,1,0:T(8,128)S(1)}, f32[24,8,128]{2,1,0:T(8,128)S(1)}, u32[]{:S(2)}, u32[]{:S(2)}) %collective-permute-start.7) | collective-permute-done | bytes 98336 | tf_op jit(solution)/shard_map/ppermute | solution.py:617
  41.2 1.8 %collective-permute-done.8.from_b = f32[24,8,128]{2,1,0:T(8,128)S(1)} collective-permute-done((f32[24,8,128]{2,1,0:T(8,128)S(1)}, f32[24,8,128]{2,1,0:T(8,128)S(1)}, u32[]{:S(2)}, u32[]{:S(2)}) %collective-permute-start.8) | collective-permute-done | bytes 98336 | tf_op jit(solution)/shard_map/ppermute | solution.py:628
  43.0 1.0 %collective-permute-done.9.from_c = f32[24,8,128]{2,1,0:T(8,128)S(1)} collective-permute-done((f32[24,8,128]{2,1,0:T(8,128)S(1)}, f32[24,8,128]{2,1,0:T(8,128)S(1)}, u32[]{:S(2)}, u32[]{:S(2)}) %collective-permute-start.9) | collective-permute-done | bytes 98336 | tf_op jit(solution)/shard_map/ppermute | solution.py:617
  44.0 0.7 %shard_map.109 = (f32[6,8,384]{2,1,0:T(8,128)}, f32[4,6,8,128]{3,2,1,0:T(8,128)}) custom-call(f32[24,8,128]{2,1,0:T(8,128)S(1)} %collective-permute-done.7.from_a, f32[24,8,128]{2,1,0:T(8,128)S(1)} %collective-permute-done.8.from_b, f32[24,8,128]{2,1,0:T(8,128)S(1)} %collective-permute-done.9.from_c), custom_call_target="tpu_custom_call" | custom-call | tf_op jit(solution)/shard_map/pallas_call | solution.py:596
  (2 shorter events, 0.1 us)
Async XLA Ops:
  2.0 19.3 %copy-start = (f32[16,16]{1,0:T(8,128)S(1)}, f32[16,16]{1,0:T(8,128)}, u32[]{:S(2)}) copy-start(f32[16,16]{1,0:T(8,128)} %reaction.3) | copy-start | bytes 3076
  2.0 16.0 %collective-permute-start = (f32[15,6,8,128]{3,2,1,0:T(8,128)S(1)}, f32[15,6,8,128]{3,2,1,0:T(8,128)S(1)}, u32[]{:S(2)}, u32[]{:S(2)}) collective-permute-start(f32[15,6,8,128]{3,2,1,0:T(8,128)S(1)} %get-tuple-element.34), channel_id=1, source_target_pairs={{255,0},{0,1},{1,2},{2,3},{3,4},{4,5},{5,6},{6,7},{7,8},{8,9},{9,1... | collective-permute-start | bytes 1105928 | tf_op jit(solution)/shard_map/ppermute | solution.py:632
  2.1 15.9 %collective-permute-start.1 = (f32[15,6,8,128]{3,2,1,0:T(8,128)S(1)}, f32[15,6,8,128]{3,2,1,0:T(8,128)S(1)}, u32[]{:S(2)}, u32[]{:S(2)}) collective-permute-start(f32[15,6,8,128]{3,2,1,0:T(8,128)S(1)} %get-tuple-element.35), channel_id=1, source_target_pairs={{255,254},{0,255},{1,0},{2,1},{3,2},{4,3},{5,4},{6,5},{7,6},{8,7},... | collective-permute-start | bytes 1105928 | tf_op jit(solution)/shard_map/ppermute | solution.py:632
  18.0 7.0 %collective-permute-start.3 = (f32[6,16,128]{2,1,0:T(8,128)S(1)}, f32[6,16,128]{2,1,0:T(8,128)S(1)}, u32[]{:S(2)}, u32[]{:S(2)}) collective-permute-start(f32[6,16,128]{2,1,0:T(8,128)S(1)} %get-tuple-element.36), channel_id=1, source_target_pairs={{255,191},{0,192},{1,193},{2,194},{3,195},{4,196},{5,197},{6,198},... | collective-permute-start | bytes 147464 | tf_op jit(solution)/shard_map/ppermute | solution.py:617
  19.2 5.8 %collective-permute-start.2 = (f32[6,16,128]{2,1,0:T(8,128)S(1)}, f32[6,16,128]{2,1,0:T(8,128)S(1)}, u32[]{:S(2)}, u32[]{:S(2)}) collective-permute-start(f32[6,16,128]{2,1,0:T(8,128)S(1)} %get-tuple-element.36), channel_id=1, source_target_pairs={{255,63},{0,64},{1,65},{2,66},{3,67},{4,68},{5,69},{6,70},{7,71},{... | collective-permute-start | bytes 147464 | tf_op jit(solution)/shard_map/ppermute | solution.py:617
  25.0 4.7 %collective-permute-start.4 = (f32[21,8,128]{2,1,0:T(8,128)S(1)}, f32[21,8,128]{2,1,0:T(8,128)S(1)}, u32[]{:S(2)}, u32[]{:S(2)}) collective-permute-start(f32[21,8,128]{2,1,0:T(8,128)S(1)} %get-tuple-element.46), channel_id=1, source_target_pairs={{255,63},{0,64},{1,65},{2,66},{3,67},{4,68},{5,69},{6,70},{7,71},{... | collective-permute-start | bytes 258056 | tf_op jit(solution)/shard_map/ppermute | solution.py:617
  27.6 6.1 %collective-permute-start.5 = (f32[21,8,128]{2,1,0:T(8,128)S(1)}, f32[21,8,128]{2,1,0:T(8,128)S(1)}, u32[]{:S(2)}, u32[]{:S(2)}) collective-permute-start(f32[21,8,128]{2,1,0:T(8,128)S(1)} %get-tuple-element.47), channel_id=1, source_target_pairs={{255,62},{0,1},{1,0},{2,3},{3,2},{4,5},{5,4},{6,7},{7,6},{8,9},{9,... | collective-permute-start | bytes 258056 | tf_op jit(solution)/shard_map/ppermute | solution.py:628
  27.6 6.6 %collective-permute-start.6 = (f32[21,8,128]{2,1,0:T(8,128)S(1)}, f32[21,8,128]{2,1,0:T(8,128)S(1)}, u32[]{:S(2)}, u32[]{:S(2)}) collective-permute-start(f32[21,8,128]{2,1,0:T(8,128)S(1)} %get-tuple-element.48), channel_id=1, source_target_pairs={{255,191},{0,192},{1,193},{2,194},{3,195},{4,196},{5,197},{6,198},... | collective-permute-start | bytes 258056 | tf_op jit(solution)/shard_map/ppermute | solution.py:617
  36.5 4.7 %collective-permute-start.7 = (f32[24,8,128]{2,1,0:T(8,128)S(1)}, f32[24,8,128]{2,1,0:T(8,128)S(1)}, u32[]{:S(2)}, u32[]{:S(2)}) collective-permute-start(f32[24,8,128]{2,1,0:T(8,128)S(1)} %get-tuple-element.54), channel_id=1, source_target_pairs={{255,63},{0,64},{1,65},{2,66},{3,67},{4,68},{5,69},{6,70},{7,71},{... | collective-permute-start | bytes 294920 | tf_op jit(solution)/shard_map/ppermute | solution.py:617
  36.8 6.2 %collective-permute-start.8 = (f32[24,8,128]{2,1,0:T(8,128)S(1)}, f32[24,8,128]{2,1,0:T(8,128)S(1)}, u32[]{:S(2)}, u32[]{:S(2)}) collective-permute-start(f32[24,8,128]{2,1,0:T(8,128)S(1)} %get-tuple-element.55), channel_id=1, source_target_pairs={{255,62},{0,1},{1,0},{2,3},{3,2},{4,5},{5,4},{6,7},{7,6},{8,9},{9,... | collective-permute-start | bytes 294920 | tf_op jit(solution)/shard_map/ppermute | solution.py:628
  37.5 6.5 %collective-permute-start.9 = (f32[24,8,128]{2,1,0:T(8,128)S(1)}, f32[24,8,128]{2,1,0:T(8,128)S(1)}, u32[]{:S(2)}, u32[]{:S(2)}) collective-permute-start(f32[24,8,128]{2,1,0:T(8,128)S(1)} %get-tuple-element.56), channel_id=1, source_target_pairs={{255,191},{0,192},{1,193},{2,194},{3,195},{4,196},{5,197},{6,198},... | collective-permute-start | bytes 294920 | tf_op jit(solution)/shard_map/ppermute | solution.py:617

commit v3 on v2

--- a/solution.py
+++ b/solution.py
@@ -7,6 +7,7 @@
 
 AXES = ("comp", "gy", "gx")
 SECTIONS = 4
+SHARED = 10
 DT = 0.1
 F32 = jnp.float32
 UNROLL = 2
@@ -52,7 +53,7 @@
     return edges
 
 
-def pack_rows(tracers, forcing, to_next, to_prev):
+def pack_rows(tracers, forcing, to_next, to_prev, copies):
     half = upper_half()
     nt, levels = tracers.shape[0], tracers.shape[1]
 
@@ -63,6 +64,8 @@
 
     for pair in range(levels // 2):
         even, odd = 2 * pair, 2 * pair + 1
+        for copy in copies[4 * pair : 4 * pair + 4]:
+            copy.wait()
         for a in range(nt):
             put(a, pair, tracers[a, even], tracers[a, odd])
         put(nt, pair, forcing[0, even], forcing[0, odd])
@@ -70,68 +73,75 @@
         growth = [jnp.exp(0.1 * forcing[2, l] - 0.05 * forcing[3, l]) for l in (even, odd)]
         put(nt + 2, pair, growth[0], growth[1])
         put(nt + 3, pair, jnp.zeros((8, 128), F32), jnp.zeros((8, 128), F32))
-    for row in range(10, 15):
+
+
+def load_kernel(
+    flow, pigment, tracers, forcing,
+    to_next, to_prev, more_next, more_prev, flow_in, pigment_in, tracers_in, forcing_in, sems,
+):
+    section, _, _ = place()
+    levels = pigment.shape[0]
+
+    @pl.when(section == 3)
+    def _():
+        copies = []
+        for j in range(3):
+            cols = slice(128 * j, 128 * j + 128)
+            copies.append(
+                pltpu.make_async_copy(flow.at[:, :, :, cols], flow_in.at[:, :, j], sems.at[j])
+            )
+            copies.append(
+                pltpu.make_async_copy(pigment.at[:, :, cols], pigment_in.at[:, j], sems.at[3 + j])
+            )
+        for copy in copies:
+            copy.start()
+        for copy in copies:
+            copy.wait()
+
+        def level(l, carry):
+            for f in range(5):
+                for j in range(3):
+                    tile = flow_in[f, l, j] if f < 4 else pigment_in[l, j]
+                    row = 3 * f + j
+                    if row < SHARED:
+                        to_next[row, l] = tile
+                        to_prev[row, l] = tile
+                    else:
+                        more_next[row - SHARED, l] = tile
+                        more_prev[row - SHARED, l] = tile
+            return carry
+
+        lax.fori_loop(0, levels, level, 0)
+
+    @pl.when(section != 3)
+    def _():
+        copies = []
         for l in range(levels):
-            to_next[row, l] = jnp.zeros((8, 128), F32)
-            to_prev[row, l] = jnp.zeros((8, 128), F32)
-
-
-def load_kernel(
-    flow, pigment, tracers, forcing, ocean, bottom,
-    to_next, to_prev, flow_in, pigment_in, tracers_in, forcing_in, wet_rows,
-    ocean_rows, bottom_rows, mask_sems, sems,
-):
-    section, strip, group = place()
-    levels = pigment.shape[0]
+            copies.append(
+                pltpu.make_async_copy(tracers.at[:, l], tracers_in.at[:, l], sems.at[l])
+            )
+            copies.append(
+                pltpu.make_async_copy(forcing.at[:, l], forcing_in.at[:, l], sems.at[levels + l])
+            )
+        for copy in copies:
+            copy.start()
+        pack_rows(tracers_in, forcing_in, to_next, to_prev, copies)
+        more_next[...] = jnp.zeros_like(more_next)
+        more_prev[...] = jnp.zeros_like(more_prev)
+
+
+def mask_kernel(ocean, bottom, wet_rows, ocean_rows, bottom_rows, mask_sems):
+    _, strip, group = place()
     starts = [jnp.maximum(strip - 1, 0), strip, jnp.minimum(strip + 1, group - 1)]
     masks = []
     for i, start in enumerate(starts):
         rows = pl.ds(pl.multiple_of(start * 8, 8), 8)
         masks.append(pltpu.make_async_copy(ocean.at[rows], ocean_rows.at[i], mask_sems.at[i]))
         masks.append(pltpu.make_async_copy(bottom.at[rows], bottom_rows.at[i], mask_sems.at[3 + i]))
-
-    @pl.when(section == 3)
-    def _():
-        copies = []
-        for j in range(3):
-            cols = slice(128 * j, 128 * j + 128)
-            copies.append(
-                pltpu.make_async_copy(flow.at[:, :, :, cols], flow_in.at[:, :, j], sems.at[j])
-            )
-            copies.append(
-                pltpu.make_async_copy(pigment.at[:, :, cols], pigment_in.at[:, j], sems.at[3 + j])
-            )
-        for copy in copies + masks:
-            copy.start()
-        for copy in copies + masks:
-            copy.wait()
-
-        def level(l, carry):
-            for f in range(5):
-                for j in range(3):
-                    tile = flow_in[f, l, j] if f < 4 else pigment_in[l, j]
-                    to_next[3 * f + j, l] = tile
-                    to_prev[3 * f + j, l] = tile
-            return carry
-
-        lax.fori_loop(0, levels, level, 0)
-
-    @pl.when(section != 3)
-    def _():
-        copies = []
-        for l in range(levels):
-            copies.append(
-                pltpu.make_async_copy(tracers.at[:, l], tracers_in.at[:, l], sems.at[l])
-            )
-            copies.append(
-                pltpu.make_async_copy(forcing.at[:, l], forcing_in.at[:, l], sems.at[levels + l])
-            )
-        for copy in copies + masks:
-            copy.start()
-        for copy in copies + masks:
-            copy.wait()
-        pack_rows(tracers_in, forcing_in, to_next, to_prev)
-
+    for copy in masks:
+        copy.start()
+    for copy in masks:
+        copy.wait()
     inside = [(strip > 0).astype(jnp.int32), 1, (strip < group - 1).astype(jnp.int32)]
     for i in range(3):
         floor = jnp.where(ocean_rows[i] == 1, bottom_rows[i], 0) * inside[i]
@@ -265,7 +275,7 @@
     return 0.25 * (first * first + second * second)
 
 
-def gather_kernel(tracers, forcing, above, below, cells, winds, border):
+def gather_kernel(tracers, forcing, above, below, wet_rows, cells, winds, border):
     section, strip, group = place()
     nt, levels = tracers.shape[0], tracers.shape[1]
     low = spread(strip > 0)
@@ -308,8 +318,8 @@
 
 
 def first_kernel(
-    flow, pigment, above, below, cells, winds, wet_rows, reaction,
-    send_a, send_b, send_c, flow_next, partial,
+    flow, pigment, above, below, more_above, more_below, cells, winds, wet_rows, reaction,
+    send_a, send_b, send_c, flow_next, partial, rim_edges, rim_wet,
     field_0, field_1, field_2, field_3, heat,
 ):
     section, strip, group = place()
@@ -320,12 +330,18 @@
 
     @pl.when(section == 3)
     def _():
+        def over(row, l):
+            return above[row, l] if row < SHARED else more_above[row - SHARED, l]
+
+        def under(row, l):
+            return below[row, l] if row < SHARED else more_below[row - SHARED, l]
+
         def fill(l, carry):
             for f in range(4):
                 for j in range(3):
-                    field_0[f, l, j, 8:16] = above[3 * f + j, l] * low
+                    field_0[f, l, j, 8:16] = over(3 * f + j, l) * low
                     field_0[f, l, j, 16:24] = flow[f, l, j]
-                    field_0[f, l, j, 24:32] = below[3 * f + j, l] * high
+                    field_0[f, l, j, 24:32] = under(3 * f + j, l) * high
             return carry
 
         lax.fori_loop(0, levels, fill, 0)
@@ -333,7 +349,7 @@
         def load(l, tile, j):
             if tile == 1:
                 return pigment[l, j]
-            return (above if tile == 0 else below)[12 + j, l]
+            return (over if tile == 0 else under)(12 + j, l)
 
         fill_heat(load, heat)
         substep(planes(field_0), field_1, heat, wet_rows, 3, 8, 8, 0, 0)
@@ -397,17 +413,22 @@
             )
             for a in range(nt):
                 partial[a, l] = results[a]
+            rim_edges[l] = edge_tile([partial[a, l, 4:12] for a in range(nt)])
+            wet = spread(wet_rows[section, 8:16] > l)
+            first = jnp.broadcast_to(wet[:, :1], (8, 128))
+            last = jnp.broadcast_to(wet[:, 127:], (8, 128))
+            rim_wet[l] = jnp.where(lanes(8) % 2 == 0, last, first)
             return carry
 
         lax.fori_loop(0, levels, level, 0)
 
 
 def sides_kernel(
-    from_left, from_right, send_a, send_b, send_c, partial, wet_rows,
-    out_a, out_b, out_c, tracers_next,
+    from_left, from_right, send_a, send_b, send_c, partial, rim_edges, rim_wet, wet_rows,
+    out_a, out_b, out_c,
 ):
     section, _, _ = place()
-    nt, levels = partial.shape[0], partial.shape[1]
+    levels = partial.shape[1]
     outs = (out_a, out_b, out_c)
 
     @pl.when(section == 3)
@@ -422,26 +443,20 @@
         rim = (lane == 0) | (lane == 127)
         row = lax.broadcasted_iota(jnp.int32, (16, 128), 0)
         inside = (row > 0) & (row < 15)
-
-        def level(l, carry):
+        for l in range(levels):
             sides = side_columns(section, from_left[l], from_right[l])
             wet_rim = rim & (floor > l)
-            shades = []
-            for a in range(nt):
-                side = jnp.where(wet_rim, roll_lanes(sides, -2 * a - 1), 0.0)
-                cell = partial[a, l] + side
-                tracers_next[a, l] = cell
-                if a < 2:
-                    shades.append(cell)
-            edge = edge_tile([tracers_next[a, l, 4:12] for a in range(nt)])
-            shade = jnp.where(inside, pigment_of(shades[0], shades[1]), 0.0)
+            pair = [
+                partial[a, l] + jnp.where(wet_rim, roll_lanes(sides, -2 * a - 1), 0.0)
+                for a in range(2)
+            ]
+            own = side_columns(section, from_left[l, 4:12], from_right[l, 4:12])
+            edge = rim_edges[l] + jnp.where(rim_wet[l] > 0.0, own, 0.0)
+            shade = jnp.where(inside, pigment_of(pair[0], pair[1]), 0.0)
             for out in outs:
                 out[2 * l] = shade[:8]
                 out[2 * l + 1] = shade[8:]
                 out[12 + l] = edge
-            return carry
-
-        lax.fori_loop(0, levels, level, 0, unroll=2)
         for out in outs:
             for i in range(18, 21):
                 out[i] = jnp.zeros((8, 128), F32)
@@ -456,8 +471,25 @@
     return [buffer.at[f] for f in range(4)]
 
 
-def early_kernel(flow_next, wet_rows, early):
+def early_kernel(flow_next, wet_rows, partial, from_left, from_right, early, tracers_next):
     section, _, _ = place()
+    nt, levels = partial.shape[0], partial.shape[1]
+
+    @pl.when(section != 3)
+    def _():
+        floor = wet_rows[section, 4:20]
+        lane = lanes(16)
+        rim = (lane == 0) | (lane == 127)
+
+        def level(l, carry):
+            sides = side_columns(section, from_left[l], from_right[l])
+            wet_rim = rim & (floor > l)
+            for a in range(nt):
+                side = jnp.where(wet_rim, roll_lanes(sides, -2 * a - 1), 0.0)
+                tracers_next[a, l] = partial[a, l] + side
+            return carry
+
+        lax.fori_loop(0, levels, level, 0, unroll=2)
 
     @pl.when(section == 3)
     def _():
@@ -465,7 +497,7 @@
 
 
 def second_kernel(
-    from_a, from_b, from_c, early, tracers_next, wet_rows, reaction,
+    from_b, from_a, from_c, early, tracers_next, wet_rows, reaction,
     out_a, out_b, out_c, flow_last, tracers_last, warm, field_1, field_2, heat, winds,
 ):
     section, _, _ = place()
@@ -573,7 +605,7 @@
         put(lambda j: blank.at[0:4], tracers_last)
 
 
-def last_kernel(from_a, from_b, from_c, light_out, forcing_out):
+def last_kernel(from_b, from_a, from_c, light_out, forcing_out):
     section, _, _ = place()
     levels = light_out.shape[0]
     is_dynamics = section == 3
@@ -617,13 +649,29 @@
     return lax.ppermute(value, AXES, route(lambda k, s, g: ((k + by) % SECTIONS, s)))
 
 
+def partner(strip, group):
+    if strip in (0, group - 1):
+        return group - 1 - strip
+    return strip + 1 if strip % 2 == 1 else strip - 1
+
+
 def opposite(value):
     def target(k, s, g):
-        if k % 2 == 1:
-            return (k + 2) % SECTIONS, s
-        if s in (0, g - 1):
-            return k, g - 1 - s
-        return k, s + 1 if s % 2 == 1 else s - 1
+        return ((k + 2) % SECTIONS, s) if k % 2 == 1 else (k, partner(s, g))
+
+    return lax.ppermute(value, AXES, route(target))
+
+
+def along_dynamics(value, by):
+    def target(k, s, g):
+        return (k, (s + by) % g) if k == 3 else (k, partner(s, g))
+
+    return lax.ppermute(value, AXES, route(target))
+
+
+def beside(value, by):
+    def target(k, s, g):
+        return ((k + by) % 3, s) if k < 3 else (k, partner(s, g))
 
     return lax.ppermute(value, AXES, route(target))
 
@@ -637,61 +685,74 @@
     nt = tracers.shape[0]
     breadth = flow_fields.shape[3]
     vmem, smem, hbm = pltpu.VMEM, pltpu.SMEM, pltpu.HBM
-    message = (15, levels, 8, 128)
-    to_next, to_prev, flow, pigment, tracers, forcing, wet_rows = call(
+    message = (SHARED, levels, 8, 128)
+    more = (15 - SHARED, levels, 8, 128)
+    to_next, to_prev, more_next, more_prev, flow, pigment, tracers, forcing = call(
         load_kernel,
         [
-            (message, F32), (message, F32),
+            (message, F32), (message, F32), (more, F32), (more, F32),
             ((4, levels, 3, 8, 128), F32), ((levels, 3, 8, 128), F32),
-            (tracers.shape, F32), (forcing.shape, F32), ((3, 24, 128), jnp.int32),
+            (tracers.shape, F32), (forcing.shape, F32),
         ],
-        (flow_fields, chlorophyll_lag, tracers, forcing, ocean_mask, bottom),
-        (hbm,) * 6,
+        (flow_fields, chlorophyll_lag, tracers, forcing),
+        (hbm,) * 4,
+        (pltpu.SemaphoreType.DMA((2 * levels,)),),
+    )
+    above = along(to_next, 1)
+    below = along(to_prev, -1)
+    more_above = along_dynamics(more_next, 1)
+    more_below = along_dynamics(more_prev, -1)
+    (wet_rows,) = call(
+        mask_kernel,
+        [((3, 24, 128), jnp.int32)],
+        (ocean_mask, bottom),
+        (hbm,) * 2,
         (
             pltpu.VMEM((3, 8, breadth), jnp.int32),
             pltpu.VMEM((3, 8, breadth), jnp.int32),
             pltpu.SemaphoreType.DMA((6,)),
-            pltpu.SemaphoreType.DMA((2 * levels,)),
         ),
     )
-    above = along(to_next, 1)
-    below = along(to_prev, -1)
     cells, winds, border = call(
         gather_kernel,
         [((nt, levels, 32, 128), F32), ((3, levels, 32, 128), F32), ((levels, 16, 128), F32)],
-        (tracers, forcing, above, below),
-        (vmem,) * 4,
-    )
-    from_left = across(border, 1)
-    from_right = across(border, -1)
+        (tracers, forcing, above, below, wet_rows),
+        (vmem,) * 5,
+    )
+    from_left = beside(border, 1)
+    from_right = beside(border, -1)
     exchange = ((21, 8, 128), F32)
-    *sends, flow_next, partial = call(
+    *sends, flow_next, partial, rim_edges, rim_wet = call(
         first_kernel,
         [
             exchange, exchange, exchange,
             ((4, levels, 3, 32, 128), F32), ((nt, levels, 16, 128), F32),
+            ((levels, 8, 128), F32), ((levels, 8, 128), F32),
         ],
-        (flow, pigment, above, below, cells, winds, wet_rows, reaction),
-        (vmem,) * 7 + (smem,),
+        (
+            flow, pigment, above, below, more_above, more_below, cells, winds, wet_rows,
+            reaction,
+        ),
+        (vmem,) * 9 + (smem,),
         (
             *[pltpu.VMEM((4, levels, 3, 40, 128), F32) for _ in range(4)],
             pltpu.VMEM((levels, 3, 24, 128), F32),
         ),
     )
-    *sent, tracers_next = call(
+    sent = call(
         sides_kernel,
-        [exchange, exchange, exchange, ((nt, levels, 16, 128), F32)],
-        (from_left, from_right, *sends, partial, wet_rows),
-        (vmem,) * 7,
+        [exchange, exchange, exchange],
+        (from_left, from_right, *sends, partial, rim_edges, rim_wet, wet_rows),
+        (vmem,) * 9,
     )
     from_b = opposite(sent[1])
     from_a = across(sent[0], 1)
     from_c = across(sent[2], -1)
-    (early,) = call(
+    early, tracers_next = call(
         early_kernel,
-        [((4, levels, 3, 32, 128), F32)],
-        (flow_next, wet_rows),
-        (vmem, vmem),
+        [((4, levels, 3, 32, 128), F32), ((nt, levels, 16, 128), F32)],
+        (flow_next, wet_rows, partial, from_left, from_right),
+        (vmem,) * 5,
     )
     exchange = ((24, 8, 128), F32)
     last = call(
@@ -700,7 +761,7 @@
             exchange, exchange, exchange,
             ((4, levels, 3, 8, 128), F32), ((nt, levels, 8, 128), F32),
         ],
-        (from_a, from_b, from_c, early, tracers_next, wet_rows, reaction),
+        (from_b, from_a, from_c, early, tracers_next, wet_rows, reaction),
         (vmem,) * 6 + (smem,),
         (
             pltpu.VMEM((levels, 3, 32, 128), F32),
@@ -723,7 +784,7 @@
     light_out, forcing_out = call(
         last_kernel,
         [((levels, 8, breadth), F32), ((4, levels, 8, 128), F32)],
-        (final_a, final_b, final_c),
+        (final_b, final_a, final_c),
         (vmem,) * 3,
     )
     return flow_out, light_out, tracers_out, forcing_out

time: 44.8 us -> 42.2 us (0.942)
  waiting for transfers between devices: 18.3 us -> 10.8 us
  starting transfers between devices: 16.2 us -> 20 us
  Pallas kernels: 9.48 us -> 10.2 us
    ppermute x2, waiting for transfers between devices: 7.78 us -> 0.01 us  [along(): lax.ppermute(value, AXES, route(lambda k, s, g: divmod((k * g + s + by) %...]
    ppermute x0 -> x4, starting transfers between devices: none -> 6.54 us  [the longest x2 5.96 us: along_dynamics(): return lax.ppermute(value, AXES, route(target))]
    ppermute x6 -> x4, starting transfers between devices: 7.35 us -> 4.12 us  [across(): lax.ppermute(value, AXES, route(lambda k, s, g: ((k + by) % SECTIONS, s)))]
    ppermute x6 -> x4, waiting for transfers between devices: 4.74 us -> 2.35 us  [across(): lax.ppermute(value, AXES, route(lambda k, s, g: ((k + by) % SECTIONS, s)))]
    ppermute x2, waiting for transfers between devices: 5.78 us -> 7.38 us  [opposite(): return lax.ppermute(value, AXES, route(target))]
    ppermute x0 -> x4, waiting for transfers between devices: none -> 1.06 us  [the longest x2 1.05 us: along_dynamics(): return lax.ppermute(value, AXES, route(target))]
    pallas_call x8 -> x9, Pallas kernels: 9.48 us -> 10.2 us  [call(): pl.pallas_call(kernel, out_shape=[jax.ShapeDtypeStruct(shape, dtype) for...]
    ppermute x2, starting transfers between devices: 0.64 us -> 1.2 us  [opposite(): return lax.ppermute(value, AXES, route(target))]
  transfers between devices with their start and end apart: 10 -> 12, of which waited for: 7 -> 5; matrix products, arithmetic and copies ran while one was open for 0% -> 0% of each run, Pallas kernels for 11% -> 14%
where the time goes in v3:
time: 42.2 us; the launch traced here: 41.8 us
  starting transfers between devices  20 us (47%)
  waiting for transfers between devices  10.8 us (26%)
  Pallas kernels  10.2 us (24%)
  between operations  0.77 us (2%)
    pallas_call x9, Pallas kernels, call(): pl.pallas_call(kernel, out_shape=[jax.ShapeDtypeStruct(shape, dtype) for...  10.2 us
    ppermute x2, starting transfers between devices, along(): lax.ppermute(value, AXES, route(lambda k, s, g: divmod((k * g + s + by) %...  8.17 us
    ppermute x2, waiting for transfers between devices, opposite(): return lax.ppermute(value, AXES, route(target))  7.38 us
    ppermute x2, starting transfers between devices, along_dynamics(): return lax.ppermute(value, AXES, route(target))  5.96 us
    ppermute x4, starting transfers between devices, across(): lax.ppermute(value, AXES, route(lambda k, s, g: ((k + by) % SECTIONS, s)))  4.12 us
    ppermute x4, waiting for transfers between devices, across(): lax.ppermute(value, AXES, route(lambda k, s, g: ((k + by) % SECTIONS, s)))  2.35 us
    ppermute x2, starting transfers between devices, opposite(): return lax.ppermute(value, AXES, route(target))  1.2 us
    ppermute x2, waiting for transfers between devices, along_dynamics(): return lax.ppermute(value, AXES, route(target))  1.05 us
  transfers between devices with their start and end apart: 12, of which 5 were waited for; matrix products, arithmetic and copies ran while one was open for 0% of the time, Pallas kernels for 14%

profile of v3, /device:TPU:6, one launch (start us, length us, event | category | flops | bytes accessed | tf_op | source)
XLA Modules:
  0.0 41.8 jit_solution(4089727171461705652)
XLA Ops:
  0.6 1.2 %shard_map.102 = (f32[10,6,8,128]{3,2,1,0:T(8,128)S(1)}, f32[10,6,8,128]{3,2,1,0:T(8,128)S(1)}, f32[5,6,8,128]{3,2,1,0:T(8,128)S(1)}, f32[5,6,8,128]{3,2,1,0:T(8...) custom-call(f32[4,6,8,384]{3,2,1,0:T(8,128)} %flow.1, ...), custom_call_target="tpu_custom_call" | custom-call | tf_op jit(solution)/shard_map/pallas_call | solution.py:628
  1.9 0.1 collective-permute-start
  1.9 8.1 %collective-permute-start.1 = (f32[10,6,8,128]{3,2,1,0:T(8,128)S(1)}, f32[10,6,8,128]{3,2,1,0:T(8,128)S(1)}, u32[]{:S(2)}, u32[]{:S(2)}) collective-permute-start(f32[10,6,8,128]{3,2,1,0:T(8,128)S(1)} %get-tuple-element.39), channel_id=1, source_target_pairs={{255,254},{0,255},{1,0},{2,1},{3,2},{4,3},{5,4},{6,5},{7,6},{8,7},... | collective-permute-start | bytes 737288 | tf_op jit(solution)/shard_map/ppermute | solution.py:680
  10.0 0.0 collective-permute-start.4
  10.0 6.0 %collective-permute-start.5 = (f32[5,6,8,128]{3,2,1,0:T(8,128)S(1)}, f32[5,6,8,128]{3,2,1,0:T(8,128)S(1)}, u32[]{:S(2)}, u32[]{:S(2)}) collective-permute-start(f32[5,6,8,128]{3,2,1,0:T(8,128)S(1)} %get-tuple-element.44), channel_id=1, source_target_pairs={{255,62},{0,1},{1,0},{2,3},{3,2},{4,5},{5,4},{6,7},{7,6},{8,9},{9,... | collective-permute-start | bytes 368648 | tf_op jit(solution)/shard_map/ppermute | solution.py:669
  16.0 0.8 %shard_map.103.wet_rows = s32[3,24,128]{2,1,0:T(8,128)S(1)} custom-call(s32[512,384]{1,0:T(8,128)} %ocean.1, s32[512,384]{1,0:T(8,128)} %bottom.1), custom_call_target="tpu_custom_call" | custom-call | tf_op jit(solution)/shard_map/pallas_call | solution.py:628
  16.9 0.0 collective-permute-done.above
  16.9 0.0 collective-permute-done.1.below
  16.9 0.1 collective-permute-start.3
  17.0 0.5 %collective-permute-start.2 = (f32[6,16,128]{2,1,0:T(8,128)S(1)}, f32[6,16,128]{2,1,0:T(8,128)S(1)}, u32[]{:S(2)}, u32[]{:S(2)}) collective-permute-start(f32[6,16,128]{2,1,0:T(8,128)S(1)} %get-tuple-element.40), channel_id=1, source_target_pairs={{255,63},{0,64},{1,65},{2,66},{3,67},{4,68},{5,69},{6,70},{7,71},{... | collective-permute-start | bytes 147464 | tf_op jit(solution)/shard_map/ppermute | solution.py:676
  17.5 1.0 %collective-permute-done.4.more_above = f32[5,6,8,128]{3,2,1,0:T(8,128)S(1)} collective-permute-done((f32[5,6,8,128]{3,2,1,0:T(8,128)S(1)}, f32[5,6,8,128]{3,2,1,0:T(8,128)S(1)}, u32[]{:S(2)}, u32[]{:S(2)}) %collective-permute-start.4) | collective-permute-done | bytes 122912 | tf_op jit(solution)/shard_map/ppermute | solution.py:669
  18.6 0.0 collective-permute-done.5.more_below
  18.6 0.0 copy-done
  18.6 3.6 %shard_map.105 = (f32[21,8,128]{2,1,0:T(8,128)S(1)}, f32[21,8,128]{2,1,0:T(8,128)S(1)}, f32[21,8,128]{2,1,0:T(8,128)S(1)}, f32[4,6,3,32,128]{4,3,2,1,0:T(8,128)S...) custom-call(f32[4,6,3,8,128]{4,3,2,1,0:T(8,128)S(1)} %get-tuple-element.41.flow, ...), custom_call_target="tpu_custom_call" | custom-call | tf_op jit(solution)/shard_map/pallas_call | solution.py:628
  22.2 0.0 collective-permute-done.3.from_right
  22.2 0.0 collective-permute-done.2.from_left
  22.3 1.1 %collective-permute-start.6 = (f32[21,8,128]{2,1,0:T(8,128)S(1)}, f32[21,8,128]{2,1,0:T(8,128)S(1)}, u32[]{:S(2)}, u32[]{:S(2)}) collective-permute-start(f32[21,8,128]{2,1,0:T(8,128)S(1)} %get-tuple-element.53), channel_id=1, source_target_pairs={{255,62},{0,1},{1,0},{2,3},{3,2},{4,5},{5,4},{6,7},{7,6},{8,9},{9,... | collective-permute-start | bytes 258056 | tf_op jit(solution)/shard_map/ppermute | solution.py:662
  23.4 1.6 %collective-permute-start.7 = (f32[21,8,128]{2,1,0:T(8,128)S(1)}, f32[21,8,128]{2,1,0:T(8,128)S(1)}, u32[]{:S(2)}, u32[]{:S(2)}) collective-permute-start(f32[21,8,128]{2,1,0:T(8,128)S(1)} %get-tuple-element.54), channel_id=1, source_target_pairs={{255,63},{0,64},{1,65},{2,66},{3,67},{4,68},{5,69},{6,70},{7,71},{... | collective-permute-start | bytes 258056 | tf_op jit(solution)/shard_map/ppermute | solution.py:649
  25.0 0.4 collective-permute-start.8
  25.4 0.6 %shard_map.107 = (f32[4,6,3,32,128]{4,3,2,1,0:T(8,128)S(1)}, f32[16,6,16,128]{3,2,1,0:T(8,128)S(1)}) custom-call(f32[4,6,3,32,128]{4,3,2,1,0:T(8,128)S(1)} %get-tuple-element.56.flow_next, s32[3,24,128]{2,1,0:T(8,128)S(1)} %shard_map.103.wet_rows, f32[16,6,16,128]{3,2,1,0:T(8,128)S(1)} %get-tuple-element.50.partial, ...), custom_call_target="tpu_custom_call" | custom-call | tf_op jit(solution)/shard_map/pallas_call | solution.py:628
  26.0 3.3 %collective-permute-done.6.from_b = f32[21,8,128]{2,1,0:T(8,128)S(1)} collective-permute-done((f32[21,8,128]{2,1,0:T(8,128)S(1)}, f32[21,8,128]{2,1,0:T(8,128)S(1)}, u32[]{:S(2)}, u32[]{:S(2)}) %collective-permute-start.6) | collective-permute-done | bytes 86048 | tf_op jit(solution)/shard_map/ppermute | solution.py:662
  29.3 0.0 collective-permute-done.7.from_a
  29.3 1.7 %collective-permute-done.8.from_c = f32[21,8,128]{2,1,0:T(8,128)S(1)} collective-permute-done((f32[21,8,128]{2,1,0:T(8,128)S(1)}, f32[21,8,128]{2,1,0:T(8,128)S(1)}, u32[]{:S(2)}, u32[]{:S(2)}) %collective-permute-start.8) | collective-permute-done | bytes 86048 | tf_op jit(solution)/shard_map/ppermute | solution.py:649
  31.0 2.3 %shard_map.108 = (f32[24,8,128]{2,1,0:T(8,128)S(1)}, f32[24,8,128]{2,1,0:T(8,128)S(1)}, f32[24,8,128]{2,1,0:T(8,128)S(1)}, f32[4,6,3,8,128]{4,3,2,1,0:T(8,128)S(1)}, f32[16,6,8,128]{3,2,1,0:T(8,128)S(1)}) custom-call(f32[21,8,128]{2,1,0:T(8,128)S(1)} %collective-permute-done.6.from_b, f32[21,8,128]{2,1,0:T(8,128)S(1)} %collective-permute-done.7.from_a, ...), custom_call_target="tpu_custom_call" | custom-call | tf_op jit(solution)/shard_map/pallas_call | solution.py:628
  33.3 0.1 collective-permute-start.9
  33.4 0.1 collective-permute-start.10
  33.5 2.0 %collective-permute-start.11 = (f32[24,8,128]{2,1,0:T(8,128)S(1)}, f32[24,8,128]{2,1,0:T(8,128)S(1)}, u32[]{:S(2)}, u32[]{:S(2)}) collective-permute-start(f32[24,8,128]{2,1,0:T(8,128)S(1)} %get-tuple-element.64), channel_id=1, source_target_pairs={{255,191},{0,192},{1,193},{2,194},{3,195},{4,196},{5,197},{6,198},... | collective-permute-start | bytes 294920 | tf_op jit(solution)/shard_map/ppermute | solution.py:649
  35.5 0.9 %shard_map.109 = (f32[4,6,8,384]{3,2,1,0:T(8,128)}, f32[16,6,8,128]{3,2,1,0:T(8,128)}) custom-call(f32[4,6,3,8,128]{4,3,2,1,0:T(8,128)S(1)} %get-tuple-element.59.flow_last, f32[16,6,8,128]{3,2,1,0:T(8,128)S(1)} %get-tuple-element.60.tracers_last), custom_call_target="tpu_custom_call" | custom-call | tf_op jit(solution)/shard_map/pallas_call | solution.py:628
  36.4 4.1 %collective-permute-done.9.from_b = f32[24,8,128]{2,1,0:T(8,128)S(1)} collective-permute-done((f32[24,8,128]{2,1,0:T(8,128)S(1)}, f32[24,8,128]{2,1,0:T(8,128)S(1)}, u32[]{:S(2)}, u32[]{:S(2)}) %collective-permute-start.9) | collective-permute-done | bytes 98336 | tf_op jit(solution)/shard_map/ppermute | solution.py:662
  40.5 0.0 collective-permute-done.10.from_a
  40.5 0.6 %collective-permute-done.11.from_c = f32[24,8,128]{2,1,0:T(8,128)S(1)} collective-permute-done((f32[24,8,128]{2,1,0:T(8,128)S(1)}, f32[24,8,128]{2,1,0:T(8,128)S(1)}, u32[]{:S(2)}, u32[]{:S(2)}) %collective-permute-start.11) | collective-permute-done | bytes 98336 | tf_op jit(solution)/shard_map/ppermute | solution.py:649
  41.1 0.7 %shard_map.110 = (f32[6,8,384]{2,1,0:T(8,128)}, f32[4,6,8,128]{3,2,1,0:T(8,128)}) custom-call(f32[24,8,128]{2,1,0:T(8,128)S(1)} %collective-permute-done.9.from_b, f32[24,8,128]{2,1,0:T(8,128)S(1)} %collective-permute-done.10.from_a, f32[24,8,128]{2,1,0:T(8,128)S(1)} %collective-permute-done.11.from_c), custom_call_target="tpu_custom_call" | custom-call | tf_op jit(solution)/shard_map/pallas_call | solution.py:628
  (3 shorter events, 0.1 us)
Async XLA Ops:
  1.9 15.0 %collective-permute-start = (f32[10,6,8,128]{3,2,1,0:T(8,128)S(1)}, f32[10,6,8,128]{3,2,1,0:T(8,128)S(1)}, u32[]{:S(2)}, u32[]{:S(2)}) collective-permute-start(f32[10,6,8,128]{3,2,1,0:T(8,128)S(1)} %get-tuple-element.38), channel_id=1, source_target_pairs={{255,0},{0,1},{1,2},{2,3},{3,4},{4,5},{5,6},{6,7},{7,8},{8,9},{9,1... | collective-permute-start | bytes 737288 | tf_op jit(solution)/shard_map/ppermute | solution.py:680
  1.9 14.9 %collective-permute-start.1 = (f32[10,6,8,128]{3,2,1,0:T(8,128)S(1)}, f32[10,6,8,128]{3,2,1,0:T(8,128)S(1)}, u32[]{:S(2)}, u32[]{:S(2)}) collective-permute-start(f32[10,6,8,128]{3,2,1,0:T(8,128)S(1)} %get-tuple-element.39), channel_id=1, source_target_pairs={{255,254},{0,255},{1,0},{2,1},{3,2},{4,3},{5,4},{6,5},{7,6},{8,7},... | collective-permute-start | bytes 737288 | tf_op jit(solution)/shard_map/ppermute | solution.py:680
  10.0 8.5 %collective-permute-start.4 = (f32[5,6,8,128]{3,2,1,0:T(8,128)S(1)}, f32[5,6,8,128]{3,2,1,0:T(8,128)S(1)}, u32[]{:S(2)}, u32[]{:S(2)}) collective-permute-start(f32[5,6,8,128]{3,2,1,0:T(8,128)S(1)} %get-tuple-element.43), channel_id=1, source_target_pairs={{255,62},{0,1},{1,0},{2,3},{3,2},{4,5},{5,4},{6,7},{7,6},{8,9},{9,... | collective-permute-start | bytes 368648 | tf_op jit(solution)/shard_map/ppermute | solution.py:669
  10.0 8.5 %copy-start = (f32[16,16]{1,0:T(8,128)S(1)}, f32[16,16]{1,0:T(8,128)}, u32[]{:S(2)}) copy-start(f32[16,16]{1,0:T(8,128)} %reaction.3) | copy-start | bytes 3076
  10.0 8.5 %collective-permute-start.5 = (f32[5,6,8,128]{3,2,1,0:T(8,128)S(1)}, f32[5,6,8,128]{3,2,1,0:T(8,128)S(1)}, u32[]{:S(2)}, u32[]{:S(2)}) collective-permute-start(f32[5,6,8,128]{3,2,1,0:T(8,128)S(1)} %get-tuple-element.44), channel_id=1, source_target_pairs={{255,62},{0,1},{1,0},{2,3},{3,2},{4,5},{5,4},{6,7},{7,6},{8,9},{9,... | collective-permute-start | bytes 368648 | tf_op jit(solution)/shard_map/ppermute | solution.py:669
  16.9 5.3 %collective-permute-start.3 = (f32[6,16,128]{2,1,0:T(8,128)S(1)}, f32[6,16,128]{2,1,0:T(8,128)S(1)}, u32[]{:S(2)}, u32[]{:S(2)}) collective-permute-start(f32[6,16,128]{2,1,0:T(8,128)S(1)} %get-tuple-element.40), channel_id=1, source_target_pairs={{255,127},{0,128},{1,129},{2,130},{3,131},{4,132},{5,133},{6,134},... | collective-permute-start | bytes 147464 | tf_op jit(solution)/shard_map/ppermute | solution.py:676
  17.0 5.2 %collective-permute-start.2 = (f32[6,16,128]{2,1,0:T(8,128)S(1)}, f32[6,16,128]{2,1,0:T(8,128)S(1)}, u32[]{:S(2)}, u32[]{:S(2)}) collective-permute-start(f32[6,16,128]{2,1,0:T(8,128)S(1)} %get-tuple-element.40), channel_id=1, source_target_pairs={{255,63},{0,64},{1,65},{2,66},{3,67},{4,68},{5,69},{6,70},{7,71},{... | collective-permute-start | bytes 147464 | tf_op jit(solution)/shard_map/ppermute | solution.py:676
  22.3 7.0 %collective-permute-start.6 = (f32[21,8,128]{2,1,0:T(8,128)S(1)}, f32[21,8,128]{2,1,0:T(8,128)S(1)}, u32[]{:S(2)}, u32[]{:S(2)}) collective-permute-start(f32[21,8,128]{2,1,0:T(8,128)S(1)} %get-tuple-element.53), channel_id=1, source_target_pairs={{255,62},{0,1},{1,0},{2,3},{3,2},{4,5},{5,4},{6,7},{7,6},{8,9},{9,... | collective-permute-start | bytes 258056 | tf_op jit(solution)/shard_map/ppermute | solution.py:662
  23.4 5.9 %collective-permute-start.7 = (f32[21,8,128]{2,1,0:T(8,128)S(1)}, f32[21,8,128]{2,1,0:T(8,128)S(1)}, u32[]{:S(2)}, u32[]{:S(2)}) collective-permute-start(f32[21,8,128]{2,1,0:T(8,128)S(1)} %get-tuple-element.54), channel_id=1, source_target_pairs={{255,63},{0,64},{1,65},{2,66},{3,67},{4,68},{5,69},{6,70},{7,71},{... | collective-permute-start | bytes 258056 | tf_op jit(solution)/shard_map/ppermute | solution.py:649
  25.0 5.9 %collective-permute-start.8 = (f32[21,8,128]{2,1,0:T(8,128)S(1)}, f32[21,8,128]{2,1,0:T(8,128)S(1)}, u32[]{:S(2)}, u32[]{:S(2)}) collective-permute-start(f32[21,8,128]{2,1,0:T(8,128)S(1)} %get-tuple-element.55), channel_id=1, source_target_pairs={{255,191},{0,192},{1,193},{2,194},{3,195},{4,196},{5,197},{6,198},... | collective-permute-start | bytes 258056 | tf_op jit(solution)/shard_map/ppermute | solution.py:649
  33.3 7.2 %collective-permute-start.9 = (f32[24,8,128]{2,1,0:T(8,128)S(1)}, f32[24,8,128]{2,1,0:T(8,128)S(1)}, u32[]{:S(2)}, u32[]{:S(2)}) collective-permute-start(f32[24,8,128]{2,1,0:T(8,128)S(1)} %get-tuple-element.62), channel_id=1, source_target_pairs={{255,62},{0,1},{1,0},{2,3},{3,2},{4,5},{5,4},{6,7},{7,6},{8,9},{9,... | collective-permute-start | bytes 294920 | tf_op jit(solution)/shard_map/ppermute | solution.py:662
  33.4 7.1 %collective-permute-start.10 = (f32[24,8,128]{2,1,0:T(8,128)S(1)}, f32[24,8,128]{2,1,0:T(8,128)S(1)}, u32[]{:S(2)}, u32[]{:S(2)}) collective-permute-start(f32[24,8,128]{2,1,0:T(8,128)S(1)} %get-tuple-element.63), channel_id=1, source_target_pairs={{255,63},{0,64},{1,65},{2,66},{3,67},{4,68},{5,69},{6,70},{7,71},{... | collective-permute-start | bytes 294920 | tf_op jit(solution)/shard_map/ppermute | solution.py:649
  33.5 7.7 %collective-permute-start.11 = (f32[24,8,128]{2,1,0:T(8,128)S(1)}, f32[24,8,128]{2,1,0:T(8,128)S(1)}, u32[]{:S(2)}, u32[]{:S(2)}) collective-permute-start(f32[24,8,128]{2,1,0:T(8,128)S(1)} %get-tuple-element.64), channel_id=1, source_target_pairs={{255,191},{0,192},{1,193},{2,194},{3,195},{4,196},{5,197},{6,198},... | collective-permute-start | bytes 294920 | tf_op jit(solution)/shard_map/ppermute | solution.py:649

commit v4 on v3

--- a/solution.py
+++ b/solution.py
@@ -149,10 +149,12 @@
             wet_rows[j, 8 * i : 8 * i + 8] = floor[:, 128 * j : 128 * j + 128]
 
 
-def side_columns(section, from_left, from_right):
-    even = lanes(from_left.shape[0]) % 2 == 0
-    east = jnp.where(section < 2, roll_lanes(from_right, -1), 0.0)
-    west = jnp.where(section > 0, roll_lanes(from_left, 1), 0.0)
+def side_columns(section, inner, outer):
+    even = lanes(inner.shape[0]) % 2 == 0
+    east = roll_lanes(jnp.where(section == 0, inner, outer), -1)
+    west = roll_lanes(jnp.where(section == 1, inner, outer), 1)
+    east = jnp.where(section < 2, east, 0.0)
+    west = jnp.where(section > 0, west, 0.0)
     return jnp.where(even, east, west)
 
 
@@ -424,7 +426,7 @@
 
 
 def sides_kernel(
-    from_left, from_right, send_a, send_b, send_c, partial, rim_edges, rim_wet, wet_rows,
+    inner, outer, send_a, send_b, send_c, partial, rim_edges, rim_wet, wet_rows,
     out_a, out_b, out_c,
 ):
     section, _, _ = place()
@@ -444,13 +446,13 @@
         row = lax.broadcasted_iota(jnp.int32, (16, 128), 0)
         inside = (row > 0) & (row < 15)
         for l in range(levels):
-            sides = side_columns(section, from_left[l], from_right[l])
+            sides = side_columns(section, inner[l], outer[l])
             wet_rim = rim & (floor > l)
             pair = [
                 partial[a, l] + jnp.where(wet_rim, roll_lanes(sides, -2 * a - 1), 0.0)
                 for a in range(2)
             ]
-            own = side_columns(section, from_left[l, 4:12], from_right[l, 4:12])
+            own = side_columns(section, inner[l, 4:12], outer[l, 4:12])
             edge = rim_edges[l] + jnp.where(rim_wet[l] > 0.0, own, 0.0)
             shade = jnp.where(inside, pigment_of(pair[0], pair[1]), 0.0)
             for out in outs:
@@ -471,7 +473,7 @@
     return [buffer.at[f] for f in range(4)]
 
 
-def early_kernel(flow_next, wet_rows, partial, from_left, from_right, early, tracers_next):
+def early_kernel(flow_next, wet_rows, partial, inner, outer, early, tracers_next):
     section, _, _ = place()
     nt, levels = partial.shape[0], partial.shape[1]
 
@@ -482,7 +484,7 @@
         rim = (lane == 0) | (lane == 127)
 
         def level(l, carry):
-            sides = side_columns(section, from_left[l], from_right[l])
+            sides = side_columns(section, inner[l], outer[l])
             wet_rim = rim & (floor > l)
             for a in range(nt):
                 side = jnp.where(wet_rim, roll_lanes(sides, -2 * a - 1), 0.0)
@@ -506,7 +508,7 @@
 
     @pl.when(section == 3)
     def _():
-        shades = (from_c, from_b, from_a)
+        shades = (from_a, from_b, from_c)
 
         def load(l, tile, j):
             return shades[j][2 * l + tile]
@@ -557,7 +559,7 @@
                 lane == 127, roll_lanes(edge_v, 126 - 2 * l), roll_lanes(v, 127)
             )
             winds[36 + l] = jnp.where(lane == 0, roll_lanes(edge_v, -2 * l), roll_lanes(v, 1))
-            winds[42 + l] = side_columns(section, from_a[12 + l], from_c[12 + l])
+            winds[42 + l] = side_columns(section, from_c[12 + l], from_a[12 + l])
         floor = wet_rows[section, 8:16]
 
         def level(l, carry):
@@ -610,7 +612,7 @@
     levels = light_out.shape[0]
     is_dynamics = section == 3
     for l in range(levels):
-        for j, shade in enumerate((from_c, from_b, from_a)):
+        for j, shade in enumerate((from_a, from_b, from_c)):
             light_out[l, :, 128 * j : 128 * j + 128] = jnp.where(is_dynamics, shade[l], 0.0)
         for f in range(4):
             i = 6 * f + l
@@ -645,19 +647,19 @@
     return pairs
 
 
-def across(value, by):
-    return lax.ppermute(value, AXES, route(lambda k, s, g: ((k + by) % SECTIONS, s)))
-
-
 def partner(strip, group):
     if strip in (0, group - 1):
         return group - 1 - strip
     return strip + 1 if strip % 2 == 1 else strip - 1
 
 
-def opposite(value):
+def trade(value, *pairs):
+    other = {}
+    for a, b in pairs:
+        other[a], other[b] = b, a
+
     def target(k, s, g):
-        return ((k + 2) % SECTIONS, s) if k % 2 == 1 else (k, partner(s, g))
+        return (other[k], s) if k in other else (k, partner(s, g))
 
     return lax.ppermute(value, AXES, route(target))
 
@@ -665,13 +667,6 @@
 def along_dynamics(value, by):
     def target(k, s, g):
         return (k, (s + by) % g) if k == 3 else (k, partner(s, g))
-
-    return lax.ppermute(value, AXES, route(target))
-
-
-def beside(value, by):
-    def target(k, s, g):
-        return ((k + by) % 3, s) if k < 3 else (k, partner(s, g))
 
     return lax.ppermute(value, AXES, route(target))
 
@@ -719,8 +714,8 @@
         (tracers, forcing, above, below, wet_rows),
         (vmem,) * 5,
     )
-    from_left = beside(border, 1)
-    from_right = beside(border, -1)
+    inner = trade(border, (0, 1))
+    outer = trade(border, (1, 2))
     exchange = ((21, 8, 128), F32)
     *sends, flow_next, partial, rim_edges, rim_wet = call(
         first_kernel,
@@ -742,16 +737,16 @@
     sent = call(
         sides_kernel,
         [exchange, exchange, exchange],
-        (from_left, from_right, *sends, partial, rim_edges, rim_wet, wet_rows),
+        (inner, outer, *sends, partial, rim_edges, rim_wet, wet_rows),
         (vmem,) * 9,
     )
-    from_b = opposite(sent[1])
-    from_a = across(sent[0], 1)
-    from_c = across(sent[2], -1)
+    from_b = trade(sent[1], (3, 1))
+    from_a = trade(sent[0], (3, 0), (1, 2))
+    from_c = trade(sent[2], (3, 2), (0, 1))
     early, tracers_next = call(
         early_kernel,
         [((4, levels, 3, 32, 128), F32), ((nt, levels, 16, 128), F32)],
-        (flow_next, wet_rows, partial, from_left, from_right),
+        (flow_next, wet_rows, partial, inner, outer),
         (vmem,) * 5,
     )
     exchange = ((24, 8, 128), F32)
@@ -770,9 +765,9 @@
             pltpu.VMEM((48, 8, 128), F32),
         ),
     )
-    final_b = opposite(last[1])
-    final_a = across(last[0], 1)
-    final_c = across(last[2], -1)
+    final_b = trade(last[1], (3, 1))
+    final_a = trade(last[0], (3, 0))
+    final_c = trade(last[2], (3, 2))
     flow_out, tracers_out = call(
         store_kernel,
         [(flow_fields.shape, F32), (tracers.shape, F32)],

time: 42.2 us -> 39.8 us (0.943)
  waiting for transfers between devices: 10.8 us -> 9.29 us
  starting transfers between devices: 20 us -> 19.3 us
    ppermute x8, waiting for transfers between devices: 9.73 us -> 8.24 us  [trade(): return lax.ppermute(value, AXES, route(target))]
    ppermute x8, starting transfers between devices: 5.9 us -> 5.17 us  [trade(): return lax.ppermute(value, AXES, route(target))]
  transfers between devices with their start and end apart: 12 -> 12, of which waited for: 5 -> 5; matrix products, arithmetic and copies ran while one was open for 0% -> 0% of each run, Pallas kernels for 14% -> 15%
where the time goes in v4:
time: 39.8 us; the launch traced here: 39.6 us
  starting transfers between devices  19.3 us (48%)
  Pallas kernels  10.2 us (26%)
  waiting for transfers between devices  9.29 us (23%)
  between operations  0.75 us (2%)
    pallas_call x9, Pallas kernels, call(): pl.pallas_call(kernel, out_shape=[jax.ShapeDtypeStruct(shape, dtype) for...  10.2 us
    ppermute x8, waiting for transfers between devices, trade(): return lax.ppermute(value, AXES, route(target))  8.24 us
    ppermute x2, starting transfers between devices, along(): lax.ppermute(value, AXES, route(lambda k, s, g: divmod((k * g + s + by) %...  8.17 us
    ppermute x2, starting transfers between devices, along_dynamics(): return lax.ppermute(value, AXES, route(target))  5.96 us
    ppermute x8, starting transfers between devices, trade(): return lax.ppermute(value, AXES, route(target))  5.17 us
    ppermute x2, waiting for transfers between devices, along_dynamics(): return lax.ppermute(value, AXES, route(target))  1.04 us
  transfers between devices with their start and end apart: 12, of which 5 were waited for; matrix products, arithmetic and copies ran while one was open for 0% of the time, Pallas kernels for 15%

profile of v4, /device:TPU:6, one launch (start us, length us, event | category | flops | bytes accessed | tf_op | source)
XLA Modules:
  0.0 39.6 jit_solution(14720284593304213858)
XLA Ops:
  0.6 1.2 %shard_map.102 = (f32[10,6,8,128]{3,2,1,0:T(8,128)S(1)}, f32[10,6,8,128]{3,2,1,0:T(8,128)S(1)}, f32[5,6,8,128]{3,2,1,0:T(8,128)S(1)}, f32[5,6,8,128]{3,2,1,0:T(8...) custom-call(f32[4,6,8,384]{3,2,1,0:T(8,128)} %flow.1, ...), custom_call_target="tpu_custom_call" | custom-call | tf_op jit(solution)/shard_map/pallas_call | solution.py:630
  1.9 0.1 collective-permute-start
  1.9 8.1 %collective-permute-start.1 = (f32[10,6,8,128]{3,2,1,0:T(8,128)S(1)}, f32[10,6,8,128]{3,2,1,0:T(8,128)S(1)}, u32[]{:S(2)}, u32[]{:S(2)}) collective-permute-start(f32[10,6,8,128]{3,2,1,0:T(8,128)S(1)} %get-tuple-element.39), channel_id=1, source_target_pairs={{255,254},{0,255},{1,0},{2,1},{3,2},{4,3},{5,4},{6,5},{7,6},{8,7},... | collective-permute-start | bytes 737288 | tf_op jit(solution)/shard_map/ppermute | solution.py:675
  10.0 0.0 collective-permute-start.4
  10.0 6.0 %collective-permute-start.5 = (f32[5,6,8,128]{3,2,1,0:T(8,128)S(1)}, f32[5,6,8,128]{3,2,1,0:T(8,128)S(1)}, u32[]{:S(2)}, u32[]{:S(2)}) collective-permute-start(f32[5,6,8,128]{3,2,1,0:T(8,128)S(1)} %get-tuple-element.44), channel_id=1, source_target_pairs={{255,62},{0,1},{1,0},{2,3},{3,2},{4,5},{5,4},{6,7},{7,6},{8,9},{9,... | collective-permute-start | bytes 368648 | tf_op jit(solution)/shard_map/ppermute | solution.py:671
  16.0 0.8 %shard_map.103.wet_rows = s32[3,24,128]{2,1,0:T(8,128)S(1)} custom-call(s32[512,384]{1,0:T(8,128)} %ocean.1, s32[512,384]{1,0:T(8,128)} %bottom.1), custom_call_target="tpu_custom_call" | custom-call | tf_op jit(solution)/shard_map/pallas_call | solution.py:630
  16.9 0.0 collective-permute-done.above
  16.9 0.0 collective-permute-done.1.below
  16.9 0.1 collective-permute-start.3
  17.0 0.5 %collective-permute-start.2 = (f32[6,16,128]{2,1,0:T(8,128)S(1)}, f32[6,16,128]{2,1,0:T(8,128)S(1)}, u32[]{:S(2)}, u32[]{:S(2)}) collective-permute-start(f32[6,16,128]{2,1,0:T(8,128)S(1)} %get-tuple-element.40), channel_id=1, source_target_pairs={{255,63},{0,64},{1,65},{2,66},{3,67},{4,68},{5,69},{6,70},{7,71},{... | collective-permute-start | bytes 147464 | tf_op jit(solution)/shard_map/ppermute | solution.py:664
  17.5 1.0 %collective-permute-done.4.more_above = f32[5,6,8,128]{3,2,1,0:T(8,128)S(1)} collective-permute-done((f32[5,6,8,128]{3,2,1,0:T(8,128)S(1)}, f32[5,6,8,128]{3,2,1,0:T(8,128)S(1)}, u32[]{:S(2)}, u32[]{:S(2)}) %collective-permute-start.4) | collective-permute-done | bytes 122912 | tf_op jit(solution)/shard_map/ppermute | solution.py:671
  18.6 0.0 collective-permute-done.5.more_below
  18.6 0.0 copy-done
  18.6 3.6 %shard_map.105 = (f32[21,8,128]{2,1,0:T(8,128)S(1)}, f32[21,8,128]{2,1,0:T(8,128)S(1)}, f32[21,8,128]{2,1,0:T(8,128)S(1)}, f32[4,6,3,32,128]{4,3,2,1,0:T(8,128)S...) custom-call(f32[4,6,3,8,128]{4,3,2,1,0:T(8,128)S(1)} %get-tuple-element.41.flow, ...), custom_call_target="tpu_custom_call" | custom-call | tf_op jit(solution)/shard_map/pallas_call | solution.py:630
  22.2 0.0 collective-permute-done.3.outer
  22.2 0.0 collective-permute-done.2.inner
  22.3 0.6 %collective-permute-start.6 = (f32[21,8,128]{2,1,0:T(8,128)S(1)}, f32[21,8,128]{2,1,0:T(8,128)S(1)}, u32[]{:S(2)}, u32[]{:S(2)}) collective-permute-start(f32[21,8,128]{2,1,0:T(8,128)S(1)} %get-tuple-element.53), channel_id=1, source_target_pairs={{255,62},{0,1},{1,0},{2,3},{3,2},{4,5},{5,4},{6,7},{7,6},{8,9},{9,... | collective-permute-start | bytes 258056 | tf_op jit(solution)/shard_map/ppermute | solution.py:664
  22.9 0.0 collective-permute-start.7
  22.9 3.0 %collective-permute-start.8 = (f32[21,8,128]{2,1,0:T(8,128)S(1)}, f32[21,8,128]{2,1,0:T(8,128)S(1)}, u32[]{:S(2)}, u32[]{:S(2)}) collective-permute-start(f32[21,8,128]{2,1,0:T(8,128)S(1)} %get-tuple-element.55), channel_id=1, source_target_pairs={{255,63},{0,64},{1,65},{2,66},{3,67},{4,68},{5,69},{6,70},{7,71},{... | collective-permute-start | bytes 258056 | tf_op jit(solution)/shard_map/ppermute | solution.py:664
  25.9 0.6 %shard_map.107 = (f32[4,6,3,32,128]{4,3,2,1,0:T(8,128)S(1)}, f32[16,6,16,128]{3,2,1,0:T(8,128)S(1)}) custom-call(f32[4,6,3,32,128]{4,3,2,1,0:T(8,128)S(1)} %get-tuple-element.56.flow_next, s32[3,24,128]{2,1,0:T(8,128)S(1)} %shard_map.103.wet_rows, f32[16,6,16,128]{3,2,1,0:T(8,128)S(1)} %get-tuple-element.50.partial, ...), custom_call_target="tpu_custom_call" | custom-call | tf_op jit(solution)/shard_map/pallas_call | solution.py:630
  26.4 2.0 %collective-permute-done.6.from_b = f32[21,8,128]{2,1,0:T(8,128)S(1)} collective-permute-done((f32[21,8,128]{2,1,0:T(8,128)S(1)}, f32[21,8,128]{2,1,0:T(8,128)S(1)}, u32[]{:S(2)}, u32[]{:S(2)}) %collective-permute-start.6) | collective-permute-done | bytes 86048 | tf_op jit(solution)/shard_map/ppermute | solution.py:664
  28.4 0.9 %collective-permute-done.7.from_a = f32[21,8,128]{2,1,0:T(8,128)S(1)} collective-permute-done((f32[21,8,128]{2,1,0:T(8,128)S(1)}, f32[21,8,128]{2,1,0:T(8,128)S(1)}, u32[]{:S(2)}, u32[]{:S(2)}) %collective-permute-start.7) | collective-permute-done | bytes 86048 | tf_op jit(solution)/shard_map/ppermute | solution.py:664
  29.3 0.0 collective-permute-done.8.from_c
  29.3 2.3 %shard_map.108 = (f32[24,8,128]{2,1,0:T(8,128)S(1)}, f32[24,8,128]{2,1,0:T(8,128)S(1)}, f32[24,8,128]{2,1,0:T(8,128)S(1)}, f32[4,6,3,8,128]{4,3,2,1,0:T(8,128)S(1)}, f32[16,6,8,128]{3,2,1,0:T(8,128)S(1)}) custom-call(f32[21,8,128]{2,1,0:T(8,128)S(1)} %collective-permute-done.6.from_b, f32[21,8,128]{2,1,0:T(8,128)S(1)} %collective-permute-done.7.from_a, ...), custom_call_target="tpu_custom_call" | custom-call | tf_op jit(solution)/shard_map/pallas_call | solution.py:630
  31.6 0.5 %collective-permute-start.9 = (f32[24,8,128]{2,1,0:T(8,128)S(1)}, f32[24,8,128]{2,1,0:T(8,128)S(1)}, u32[]{:S(2)}, u32[]{:S(2)}) collective-permute-start(f32[24,8,128]{2,1,0:T(8,128)S(1)} %get-tuple-element.62), channel_id=1, source_target_pairs={{255,62},{0,1},{1,0},{2,3},{3,2},{4,5},{5,4},{6,7},{7,6},{8,9},{9,... | collective-permute-start | bytes 294920 | tf_op jit(solution)/shard_map/ppermute | solution.py:664
  32.2 0.3 collective-permute-start.10
  32.4 0.2 collective-permute-start.11
  32.6 0.9 %shard_map.109 = (f32[4,6,8,384]{3,2,1,0:T(8,128)}, f32[16,6,8,128]{3,2,1,0:T(8,128)}) custom-call(f32[4,6,3,8,128]{4,3,2,1,0:T(8,128)S(1)} %get-tuple-element.59.flow_last, f32[16,6,8,128]{3,2,1,0:T(8,128)S(1)} %get-tuple-element.60.tracers_last), custom_call_target="tpu_custom_call" | custom-call | tf_op jit(solution)/shard_map/pallas_call | solution.py:630
  33.5 4.4 %collective-permute-done.9.from_b = f32[24,8,128]{2,1,0:T(8,128)S(1)} collective-permute-done((f32[24,8,128]{2,1,0:T(8,128)S(1)}, f32[24,8,128]{2,1,0:T(8,128)S(1)}, u32[]{:S(2)}, u32[]{:S(2)}) %collective-permute-start.9) | collective-permute-done | bytes 98336 | tf_op jit(solution)/shard_map/ppermute | solution.py:664
  37.9 1.0 %collective-permute-done.10.from_a = f32[24,8,128]{2,1,0:T(8,128)S(1)} collective-permute-done((f32[24,8,128]{2,1,0:T(8,128)S(1)}, f32[24,8,128]{2,1,0:T(8,128)S(1)}, u32[]{:S(2)}, u32[]{:S(2)}) %collective-permute-start.10) | collective-permute-done | bytes 98336 | tf_op jit(solution)/shard_map/ppermute | solution.py:664
  38.9 0.0 collective-permute-done.11.from_c
  38.9 0.7 %shard_map.110 = (f32[6,8,384]{2,1,0:T(8,128)}, f32[4,6,8,128]{3,2,1,0:T(8,128)}) custom-call(f32[24,8,128]{2,1,0:T(8,128)S(1)} %collective-permute-done.9.from_b, f32[24,8,128]{2,1,0:T(8,128)S(1)} %collective-permute-done.10.from_a, f32[24,8,128]{2,1,0:T(8,128)S(1)} %collective-permute-done.11.from_c), custom_call_target="tpu_custom_call" | custom-call | tf_op jit(solution)/shard_map/pallas_call | solution.py:630
  (3 shorter events, 0.1 us)
Async XLA Ops:
  1.9 15.0 %collective-permute-start = (f32[10,6,8,128]{3,2,1,0:T(8,128)S(1)}, f32[10,6,8,128]{3,2,1,0:T(8,128)S(1)}, u32[]{:S(2)}, u32[]{:S(2)}) collective-permute-start(f32[10,6,8,128]{3,2,1,0:T(8,128)S(1)} %get-tuple-element.38), channel_id=1, source_target_pairs={{255,0},{0,1},{1,2},{2,3},{3,4},{4,5},{5,6},{6,7},{7,8},{8,9},{9,1... | collective-permute-start | bytes 737288 | tf_op jit(solution)/shard_map/ppermute | solution.py:675
  1.9 14.9 %collective-permute-start.1 = (f32[10,6,8,128]{3,2,1,0:T(8,128)S(1)}, f32[10,6,8,128]{3,2,1,0:T(8,128)S(1)}, u32[]{:S(2)}, u32[]{:S(2)}) collective-permute-start(f32[10,6,8,128]{3,2,1,0:T(8,128)S(1)} %get-tuple-element.39), channel_id=1, source_target_pairs={{255,254},{0,255},{1,0},{2,1},{3,2},{4,3},{5,4},{6,5},{7,6},{8,7},... | collective-permute-start | bytes 737288 | tf_op jit(solution)/shard_map/ppermute | solution.py:675
  10.0 8.5 %collective-permute-start.4 = (f32[5,6,8,128]{3,2,1,0:T(8,128)S(1)}, f32[5,6,8,128]{3,2,1,0:T(8,128)S(1)}, u32[]{:S(2)}, u32[]{:S(2)}) collective-permute-start(f32[5,6,8,128]{3,2,1,0:T(8,128)S(1)} %get-tuple-element.43), channel_id=1, source_target_pairs={{255,62},{0,1},{1,0},{2,3},{3,2},{4,5},{5,4},{6,7},{7,6},{8,9},{9,... | collective-permute-start | bytes 368648 | tf_op jit(solution)/shard_map/ppermute | solution.py:671
  10.0 8.5 %copy-start = (f32[16,16]{1,0:T(8,128)S(1)}, f32[16,16]{1,0:T(8,128)}, u32[]{:S(2)}) copy-start(f32[16,16]{1,0:T(8,128)} %reaction.3) | copy-start | bytes 3076
  10.0 8.5 %collective-permute-start.5 = (f32[5,6,8,128]{3,2,1,0:T(8,128)S(1)}, f32[5,6,8,128]{3,2,1,0:T(8,128)S(1)}, u32[]{:S(2)}, u32[]{:S(2)}) collective-permute-start(f32[5,6,8,128]{3,2,1,0:T(8,128)S(1)} %get-tuple-element.44), channel_id=1, source_target_pairs={{255,62},{0,1},{1,0},{2,3},{3,2},{4,5},{5,4},{6,7},{7,6},{8,9},{9,... | collective-permute-start | bytes 368648 | tf_op jit(solution)/shard_map/ppermute | solution.py:671
  16.9 5.3 %collective-permute-start.3 = (f32[6,16,128]{2,1,0:T(8,128)S(1)}, f32[6,16,128]{2,1,0:T(8,128)S(1)}, u32[]{:S(2)}, u32[]{:S(2)}) collective-permute-start(f32[6,16,128]{2,1,0:T(8,128)S(1)} %get-tuple-element.40), channel_id=1, source_target_pairs={{255,62},{0,1},{1,0},{2,3},{3,2},{4,5},{5,4},{6,7},{7,6},{8,9},{9,... | collective-permute-start | bytes 147464 | tf_op jit(solution)/shard_map/ppermute | solution.py:664
  17.0 5.2 %collective-permute-start.2 = (f32[6,16,128]{2,1,0:T(8,128)S(1)}, f32[6,16,128]{2,1,0:T(8,128)S(1)}, u32[]{:S(2)}, u32[]{:S(2)}) collective-permute-start(f32[6,16,128]{2,1,0:T(8,128)S(1)} %get-tuple-element.40), channel_id=1, source_target_pairs={{255,63},{0,64},{1,65},{2,66},{3,67},{4,68},{5,69},{6,70},{7,71},{... | collective-permute-start | bytes 147464 | tf_op jit(solution)/shard_map/ppermute | solution.py:664
  22.3 6.2 %collective-permute-start.6 = (f32[21,8,128]{2,1,0:T(8,128)S(1)}, f32[21,8,128]{2,1,0:T(8,128)S(1)}, u32[]{:S(2)}, u32[]{:S(2)}) collective-permute-start(f32[21,8,128]{2,1,0:T(8,128)S(1)} %get-tuple-element.53), channel_id=1, source_target_pairs={{255,62},{0,1},{1,0},{2,3},{3,2},{4,5},{5,4},{6,7},{7,6},{8,9},{9,... | collective-permute-start | bytes 258056 | tf_op jit(solution)/shard_map/ppermute | solution.py:664
  22.9 6.5 %collective-permute-start.7 = (f32[21,8,128]{2,1,0:T(8,128)S(1)}, f32[21,8,128]{2,1,0:T(8,128)S(1)}, u32[]{:S(2)}, u32[]{:S(2)}) collective-permute-start(f32[21,8,128]{2,1,0:T(8,128)S(1)} %get-tuple-element.54), channel_id=1, source_target_pairs={{255,191},{0,192},{1,193},{2,194},{3,195},{4,196},{5,197},{6,198},... | collective-permute-start | bytes 258056 | tf_op jit(solution)/shard_map/ppermute | solution.py:664
  22.9 6.5 %collective-permute-start.8 = (f32[21,8,128]{2,1,0:T(8,128)S(1)}, f32[21,8,128]{2,1,0:T(8,128)S(1)}, u32[]{:S(2)}, u32[]{:S(2)}) collective-permute-start(f32[21,8,128]{2,1,0:T(8,128)S(1)} %get-tuple-element.55), channel_id=1, source_target_pairs={{255,63},{0,64},{1,65},{2,66},{3,67},{4,68},{5,69},{6,70},{7,71},{... | collective-permute-start | bytes 258056 | tf_op jit(solution)/shard_map/ppermute | solution.py:664
  31.6 6.3 %collective-permute-start.9 = (f32[24,8,128]{2,1,0:T(8,128)S(1)}, f32[24,8,128]{2,1,0:T(8,128)S(1)}, u32[]{:S(2)}, u32[]{:S(2)}) collective-permute-start(f32[24,8,128]{2,1,0:T(8,128)S(1)} %get-tuple-element.62), channel_id=1, source_target_pairs={{255,62},{0,1},{1,0},{2,3},{3,2},{4,5},{5,4},{6,7},{7,6},{8,9},{9,... | collective-permute-start | bytes 294920 | tf_op jit(solution)/shard_map/ppermute | solution.py:664
  32.2 6.7 %collective-permute-start.10 = (f32[24,8,128]{2,1,0:T(8,128)S(1)}, f32[24,8,128]{2,1,0:T(8,128)S(1)}, u32[]{:S(2)}, u32[]{:S(2)}) collective-permute-start(f32[24,8,128]{2,1,0:T(8,128)S(1)} %get-tuple-element.63), channel_id=1, source_target_pairs={{255,191},{0,192},{1,193},{2,194},{3,195},{4,196},{5,197},{6,198},... | collective-permute-start | bytes 294920 | tf_op jit(solution)/shard_map/ppermute | solution.py:664
  32.4 6.5 %collective-permute-start.11 = (f32[24,8,128]{2,1,0:T(8,128)S(1)}, f32[24,8,128]{2,1,0:T(8,128)S(1)}, u32[]{:S(2)}, u32[]{:S(2)}) collective-permute-start(f32[24,8,128]{2,1,0:T(8,128)S(1)} %get-tuple-element.64), channel_id=1, source_target_pairs={{255,62},{0,1},{1,0},{2,3},{3,2},{4,5},{5,4},{6,7},{7,6},{8,9},{9,... | collective-permute-start | bytes 294920 | tf_op jit(solution)/shard_map/ppermute | solution.py:664

commit v5 on v4

--- a/solution.py
+++ b/solution.py
@@ -11,7 +11,7 @@
 DT = 0.1
 F32 = jnp.float32
 UNROLL = 2
-VMEM_LIMIT = 48 * 1024 * 1024
+VMEM_LIMIT = 24 * 1024 * 1024
 
 
 def place():
@@ -130,7 +130,7 @@
         more_prev[...] = jnp.zeros_like(more_prev)
 
 
-def mask_kernel(ocean, bottom, wet_rows, ocean_rows, bottom_rows, mask_sems):
+def mask_kernel(ocean, bottom, reaction, wet_rows, rates, ocean_rows, bottom_rows, mask_sems):
     _, strip, group = place()
     starts = [jnp.maximum(strip - 1, 0), strip, jnp.minimum(strip + 1, group - 1)]
     masks = []
@@ -140,6 +140,9 @@
         masks.append(pltpu.make_async_copy(bottom.at[rows], bottom_rows.at[i], mask_sems.at[3 + i]))
     for copy in masks:
         copy.start()
+    nt = reaction.shape[0]
+    for k in range(nt):
+        rates[k] = jnp.broadcast_to(reaction[:, k : k + 1], (nt, 128))
     for copy in masks:
         copy.wait()
     inside = [(strip > 0).astype(jnp.int32), 1, (strip < group - 1).astype(jnp.int32)]
@@ -259,13 +262,17 @@
     lane = lanes(centre[0].shape[0])
     a, b, c, d, keep, grow = weights
     results = []
+
+    def rate(k, i):
+        return jnp.broadcast_to(reaction[k, i : i + 1], centre[0].shape)
+
     for i in range(nt):
         side = 0.0 if sides is None else roll_lanes(sides, -2 * i - 1)
         east = jnp.where(lane == 127, side, roll_lanes(centre[i], 127))
         west = jnp.where(lane == 0, side, roll_lanes(centre[i], 1))
-        mixed = reaction[i, 0] * centre[0]
+        mixed = rate(0, i) * centre[0]
         for k in range(1, nt):
-            mixed = mixed + reaction[i, k] * centre[k]
+            mixed = mixed + rate(k, i) * centre[k]
         results.append(
             (keep * centre[i] + grow * mixed)
             + ((down[i] * a + up[i] * b) + (east * c + west * d))
@@ -679,7 +686,7 @@
     levels = chlorophyll_lag.shape[0]
     nt = tracers.shape[0]
     breadth = flow_fields.shape[3]
-    vmem, smem, hbm = pltpu.VMEM, pltpu.SMEM, pltpu.HBM
+    vmem, hbm = pltpu.VMEM, pltpu.HBM
     message = (SHARED, levels, 8, 128)
     more = (15 - SHARED, levels, 8, 128)
     to_next, to_prev, more_next, more_prev, flow, pigment, tracers, forcing = call(
@@ -697,11 +704,11 @@
     below = along(to_prev, -1)
     more_above = along_dynamics(more_next, 1)
     more_below = along_dynamics(more_prev, -1)
-    (wet_rows,) = call(
+    wet_rows, rates = call(
         mask_kernel,
-        [((3, 24, 128), jnp.int32)],
-        (ocean_mask, bottom),
-        (hbm,) * 2,
+        [((3, 24, 128), jnp.int32), ((nt, nt, 128), F32)],
+        (ocean_mask, bottom, reaction),
+        (hbm, hbm, vmem),
         (
             pltpu.VMEM((3, 8, breadth), jnp.int32),
             pltpu.VMEM((3, 8, breadth), jnp.int32),
@@ -726,9 +733,9 @@
         ],
         (
             flow, pigment, above, below, more_above, more_below, cells, winds, wet_rows,
-            reaction,
+            rates,
         ),
-        (vmem,) * 9 + (smem,),
+        (vmem,) * 10,
         (
             *[pltpu.VMEM((4, levels, 3, 40, 128), F32) for _ in range(4)],
             pltpu.VMEM((levels, 3, 24, 128), F32),
@@ -756,8 +763,8 @@
             exchange, exchange, exchange,
             ((4, levels, 3, 8, 128), F32), ((nt, levels, 8, 128), F32),
         ],
-        (from_b, from_a, from_c, early, tracers_next, wet_rows, reaction),
-        (vmem,) * 6 + (smem,),
+        (from_b, from_a, from_c, early, tracers_next, wet_rows, rates),
+        (vmem,) * 7,
         (
             pltpu.VMEM((levels, 3, 32, 128), F32),
             *[pltpu.VMEM((4, levels, 3, 32, 128), F32) for _ in range(2)],

time: 39.8 us -> 39.2 us (0.985)
  Pallas kernels: 10.2 us -> 8.94 us
  local copies, waits for them, and re-layouts: 0.01 us -> 0.7 us
    pallas_call x9, Pallas kernels: 10.2 us -> 8.94 us  [call(): pl.pallas_call(kernel, out_shape=[jax.ShapeDtypeStruct(shape, dtype) for...]
    ppermute x2, waiting for transfers between devices: 1.04 us -> 0.32 us  [along_dynamics(): return lax.ppermute(value, AXES, route(target))]
    unnamed x2, local copies, waits for them, and re-layouts: 0.01 us -> 0.7 us
    ppermute x8, waiting for transfers between devices: 8.24 us -> 8.69 us  [trade(): return lax.ppermute(value, AXES, route(target))]
  transfers between devices with their start and end apart: 12 -> 12, of which waited for: 5 -> 5; matrix products, arithmetic and copies ran while one was open for 0% -> 0% of each run, Pallas kernels for 15% -> 14%
where the time goes in v5:
time: 39.2 us; the launch traced here: 38.7 us
  starting transfers between devices  19.3 us (49%)
  waiting for transfers between devices  9.02 us (23%)
  Pallas kernels  8.94 us (23%)
  between operations  0.75 us (2%)
  local copies, waits for them, and re-layouts  0.7 us (2%)
    pallas_call x9, Pallas kernels, call(): pl.pallas_call(kernel, out_shape=[jax.ShapeDtypeStruct(shape, dtype) for...  8.94 us
    ppermute x8, waiting for transfers between devices, trade(): return lax.ppermute(value, AXES, route(target))  8.69 us
    ppermute x2, starting transfers between devices, along(): lax.ppermute(value, AXES, route(lambda k, s, g: divmod((k * g + s + by) %...  8.17 us
    ppermute x2, starting transfers between devices, along_dynamics(): return lax.ppermute(value, AXES, route(target))  5.96 us
    ppermute x8, starting transfers between devices, trade(): return lax.ppermute(value, AXES, route(target))  5.16 us
  transfers between devices with their start and end apart: 12, of which 5 were waited for; matrix products, arithmetic and copies ran while one was open for 0% of the time, Pallas kernels for 14%

profile of v5, /device:TPU:6, one launch (start us, length us, event | category | flops | bytes accessed | tf_op | source)
XLA Modules:
  0.0 38.7 jit_solution(10687400923261482904)
XLA Ops:
  0.6 1.2 %shard_map.102 = (f32[10,6,8,128]{3,2,1,0:T(8,128)S(1)}, f32[10,6,8,128]{3,2,1,0:T(8,128)S(1)}, f32[5,6,8,128]{3,2,1,0:T(8,128)S(1)}, f32[5,6,8,128]{3,2,1,0:T(8...) custom-call(f32[4,6,8,384]{3,2,1,0:T(8,128)} %flow.1, ...), custom_call_target="tpu_custom_call" | custom-call | tf_op jit(solution)/shard_map/pallas_call | solution.py:637
  1.9 0.1 collective-permute-start
  1.9 8.1 %collective-permute-start.1 = (f32[10,6,8,128]{3,2,1,0:T(8,128)S(1)}, f32[10,6,8,128]{3,2,1,0:T(8,128)S(1)}, u32[]{:S(2)}, u32[]{:S(2)}) collective-permute-start(f32[10,6,8,128]{3,2,1,0:T(8,128)S(1)} %get-tuple-element.41), channel_id=1, source_target_pairs={{255,254},{0,255},{1,0},{2,1},{3,2},{4,3},{5,4},{6,5},{7,6},{8,7},... | collective-permute-start | bytes 737288 | tf_op jit(solution)/shard_map/ppermute | solution.py:682
  10.0 0.0 collective-permute-start.4
  10.0 6.0 %collective-permute-start.5 = (f32[5,6,8,128]{3,2,1,0:T(8,128)S(1)}, f32[5,6,8,128]{3,2,1,0:T(8,128)S(1)}, u32[]{:S(2)}, u32[]{:S(2)}) collective-permute-start(f32[5,6,8,128]{3,2,1,0:T(8,128)S(1)} %get-tuple-element.47), channel_id=1, source_target_pairs={{255,62},{0,1},{1,0},{2,3},{3,2},{4,5},{5,4},{6,7},{7,6},{8,9},{9,... | collective-permute-start | bytes 368648 | tf_op jit(solution)/shard_map/ppermute | solution.py:678
  16.0 0.7 %copy-done = f32[16,16]{1,0:T(8,128)S(1)} copy-done((f32[16,16]{1,0:T(8,128)S(1)}, f32[16,16]{1,0:T(8,128)}, u32[]{:S(2)}) %copy-start) | copy-done | bytes 1048
  16.7 0.9 %shard_map.103 = (s32[3,24,128]{2,1,0:T(8,128)S(1)}, f32[16,16,128]{2,1,0:T(8,128)S(1)}) custom-call(s32[512,384]{1,0:T(8,128)} %ocean.1, s32[512,384]{1,0:T(8,128)} %bottom.1, f32[16,16]{1,0:T(8,128)S(1)} %copy-done), custom_call_target="tpu_custom_call" | custom-call | tf_op jit(solution)/shard_map/pallas_call | solution.py:637
  17.6 0.0 collective-permute-done.above
  17.6 0.0 collective-permute-done.1.below
  17.6 0.1 collective-permute-start.3
  17.7 0.5 %collective-permute-start.2 = (f32[6,16,128]{2,1,0:T(8,128)S(1)}, f32[6,16,128]{2,1,0:T(8,128)S(1)}, u32[]{:S(2)}, u32[]{:S(2)}) collective-permute-start(f32[6,16,128]{2,1,0:T(8,128)S(1)} %get-tuple-element.43), channel_id=1, source_target_pairs={{255,63},{0,64},{1,65},{2,66},{3,67},{4,68},{5,69},{6,70},{7,71},{... | collective-permute-start | bytes 147464 | tf_op jit(solution)/shard_map/ppermute | solution.py:671
  18.2 0.3 collective-permute-done.4.more_above
  18.6 0.0 collective-permute-done.5.more_below
  18.6 3.0 %shard_map.105 = (f32[21,8,128]{2,1,0:T(8,128)S(1)}, f32[21,8,128]{2,1,0:T(8,128)S(1)}, f32[21,8,128]{2,1,0:T(8,128)S(1)}, f32[4,6,3,32,128]{4,3,2,1,0:T(8,128)S...) custom-call(f32[4,6,3,8,128]{4,3,2,1,0:T(8,128)S(1)} %get-tuple-element.44.flow, ...), custom_call_target="tpu_custom_call" | custom-call | tf_op jit(solution)/shard_map/pallas_call | solution.py:637
  21.6 0.0 collective-permute-done.3.outer
  21.6 0.0 collective-permute-done.2.inner
  21.6 1.2 %collective-permute-start.6 = (f32[21,8,128]{2,1,0:T(8,128)S(1)}, f32[21,8,128]{2,1,0:T(8,128)S(1)}, u32[]{:S(2)}, u32[]{:S(2)}) collective-permute-start(f32[21,8,128]{2,1,0:T(8,128)S(1)} %get-tuple-element.57), channel_id=1, source_target_pairs={{255,62},{0,1},{1,0},{2,3},{3,2},{4,5},{5,4},{6,7},{7,6},{8,9},{9,... | collective-permute-start | bytes 258056 | tf_op jit(solution)/shard_map/ppermute | solution.py:671
  22.8 0.0 collective-permute-start.7
  22.9 2.4 %collective-permute-start.8 = (f32[21,8,128]{2,1,0:T(8,128)S(1)}, f32[21,8,128]{2,1,0:T(8,128)S(1)}, u32[]{:S(2)}, u32[]{:S(2)}) collective-permute-start(f32[21,8,128]{2,1,0:T(8,128)S(1)} %get-tuple-element.59), channel_id=1, source_target_pairs={{255,63},{0,64},{1,65},{2,66},{3,67},{4,68},{5,69},{6,70},{7,71},{... | collective-permute-start | bytes 258056 | tf_op jit(solution)/shard_map/ppermute | solution.py:671
  25.2 0.6 %shard_map.107 = (f32[4,6,3,32,128]{4,3,2,1,0:T(8,128)S(1)}, f32[16,6,16,128]{3,2,1,0:T(8,128)S(1)}) custom-call(f32[4,6,3,32,128]{4,3,2,1,0:T(8,128)S(1)} %get-tuple-element.60.flow_next, s32[3,24,128]{2,1,0:T(8,128)S(1)} %get-tuple-element.42.wet_rows, f32[16,6,16,128]{3,2,1,0:T(8,128)S(1)} %get-tuple-element.54.partial, ...), custom_call_target="tpu_custom_call" | custom-call | tf_op jit(solution)/shard_map/pallas_call | solution.py:637
  25.8 2.7 %collective-permute-done.6.from_b = f32[21,8,128]{2,1,0:T(8,128)S(1)} collective-permute-done((f32[21,8,128]{2,1,0:T(8,128)S(1)}, f32[21,8,128]{2,1,0:T(8,128)S(1)}, u32[]{:S(2)}, u32[]{:S(2)}) %collective-permute-start.6) | collective-permute-done | bytes 86048 | tf_op jit(solution)/shard_map/ppermute | solution.py:671
  28.5 0.6 %collective-permute-done.7.from_a = f32[21,8,128]{2,1,0:T(8,128)S(1)} collective-permute-done((f32[21,8,128]{2,1,0:T(8,128)S(1)}, f32[21,8,128]{2,1,0:T(8,128)S(1)}, u32[]{:S(2)}, u32[]{:S(2)}) %collective-permute-start.7) | collective-permute-done | bytes 86048 | tf_op jit(solution)/shard_map/ppermute | solution.py:671
  29.1 0.0 collective-permute-done.8.from_c
  29.1 1.6 %shard_map.108 = (f32[24,8,128]{2,1,0:T(8,128)S(1)}, f32[24,8,128]{2,1,0:T(8,128)S(1)}, f32[24,8,128]{2,1,0:T(8,128)S(1)}, f32[4,6,3,8,128]{4,3,2,1,0:T(8,128)S(1)}, f32[16,6,8,128]{3,2,1,0:T(8,128)S(1)}) custom-call(f32[21,8,128]{2,1,0:T(8,128)S(1)} %collective-permute-done.6.from_b, f32[21,8,128]{2,1,0:T(8,128)S(1)} %collective-permute-done.7.from_a, ...), custom_call_target="tpu_custom_call" | custom-call | tf_op jit(solution)/shard_map/pallas_call | solution.py:637
  30.7 0.4 %collective-permute-start.9 = (f32[24,8,128]{2,1,0:T(8,128)S(1)}, f32[24,8,128]{2,1,0:T(8,128)S(1)}, u32[]{:S(2)}, u32[]{:S(2)}) collective-permute-start(f32[24,8,128]{2,1,0:T(8,128)S(1)} %get-tuple-element.66), channel_id=1, source_target_pairs={{255,62},{0,1},{1,0},{2,3},{3,2},{4,5},{5,4},{6,7},{7,6},{8,9},{9,... | collective-permute-start | bytes 294920 | tf_op jit(solution)/shard_map/ppermute | solution.py:671
  31.2 0.6 %collective-permute-start.10 = (f32[24,8,128]{2,1,0:T(8,128)S(1)}, f32[24,8,128]{2,1,0:T(8,128)S(1)}, u32[]{:S(2)}, u32[]{:S(2)}) collective-permute-start(f32[24,8,128]{2,1,0:T(8,128)S(1)} %get-tuple-element.67), channel_id=1, source_target_pairs={{255,191},{0,192},{1,193},{2,194},{3,195},{4,196},{5,197},{6,198},... | collective-permute-start | bytes 294920 | tf_op jit(solution)/shard_map/ppermute | solution.py:671
  31.7 0.0 collective-permute-start.11
  31.7 0.9 %shard_map.109 = (f32[4,6,8,384]{3,2,1,0:T(8,128)}, f32[16,6,8,128]{3,2,1,0:T(8,128)}) custom-call(f32[4,6,3,8,128]{4,3,2,1,0:T(8,128)S(1)} %get-tuple-element.63.flow_last, f32[16,6,8,128]{3,2,1,0:T(8,128)S(1)} %get-tuple-element.64.tracers_last), custom_call_target="tpu_custom_call" | custom-call | tf_op jit(solution)/shard_map/pallas_call | solution.py:637
  32.6 4.4 %collective-permute-done.9.from_b = f32[24,8,128]{2,1,0:T(8,128)S(1)} collective-permute-done((f32[24,8,128]{2,1,0:T(8,128)S(1)}, f32[24,8,128]{2,1,0:T(8,128)S(1)}, u32[]{:S(2)}, u32[]{:S(2)}) %collective-permute-start.9) | collective-permute-done | bytes 98336 | tf_op jit(solution)/shard_map/ppermute | solution.py:671
  37.1 0.9 %collective-permute-done.10.from_a = f32[24,8,128]{2,1,0:T(8,128)S(1)} collective-permute-done((f32[24,8,128]{2,1,0:T(8,128)S(1)}, f32[24,8,128]{2,1,0:T(8,128)S(1)}, u32[]{:S(2)}, u32[]{:S(2)}) %collective-permute-start.10) | collective-permute-done | bytes 98336 | tf_op jit(solution)/shard_map/ppermute | solution.py:671
  38.0 0.0 collective-permute-done.11.from_c
  38.0 0.7 %shard_map.110 = (f32[6,8,384]{2,1,0:T(8,128)}, f32[4,6,8,128]{3,2,1,0:T(8,128)}) custom-call(f32[24,8,128]{2,1,0:T(8,128)S(1)} %collective-permute-done.9.from_b, f32[24,8,128]{2,1,0:T(8,128)S(1)} %collective-permute-done.10.from_a, f32[24,8,128]{2,1,0:T(8,128)S(1)} %collective-permute-done.11.from_c), custom_call_target="tpu_custom_call" | custom-call | tf_op jit(solution)/shard_map/pallas_call | solution.py:637
  (3 shorter events, 0.1 us)
Async XLA Ops:
  1.9 15.7 %collective-permute-start = (f32[10,6,8,128]{3,2,1,0:T(8,128)S(1)}, f32[10,6,8,128]{3,2,1,0:T(8,128)S(1)}, u32[]{:S(2)}, u32[]{:S(2)}) collective-permute-start(f32[10,6,8,128]{3,2,1,0:T(8,128)S(1)} %get-tuple-element.40), channel_id=1, source_target_pairs={{255,0},{0,1},{1,2},{2,3},{3,4},{4,5},{5,6},{6,7},{7,8},{8,9},{9,1... | collective-permute-start | bytes 737288 | tf_op jit(solution)/shard_map/ppermute | solution.py:682
  1.9 15.6 %collective-permute-start.1 = (f32[10,6,8,128]{3,2,1,0:T(8,128)S(1)}, f32[10,6,8,128]{3,2,1,0:T(8,128)S(1)}, u32[]{:S(2)}, u32[]{:S(2)}) collective-permute-start(f32[10,6,8,128]{3,2,1,0:T(8,128)S(1)} %get-tuple-element.41), channel_id=1, source_target_pairs={{255,254},{0,255},{1,0},{2,1},{3,2},{4,3},{5,4},{6,5},{7,6},{8,7},... | collective-permute-start | bytes 737288 | tf_op jit(solution)/shard_map/ppermute | solution.py:682
  10.0 8.5 %collective-permute-start.4 = (f32[5,6,8,128]{3,2,1,0:T(8,128)S(1)}, f32[5,6,8,128]{3,2,1,0:T(8,128)S(1)}, u32[]{:S(2)}, u32[]{:S(2)}) collective-permute-start(f32[5,6,8,128]{3,2,1,0:T(8,128)S(1)} %get-tuple-element.46), channel_id=1, source_target_pairs={{255,62},{0,1},{1,0},{2,3},{3,2},{4,5},{5,4},{6,7},{7,6},{8,9},{9,... | collective-permute-start | bytes 368648 | tf_op jit(solution)/shard_map/ppermute | solution.py:678
  10.0 8.5 %collective-permute-start.5 = (f32[5,6,8,128]{3,2,1,0:T(8,128)S(1)}, f32[5,6,8,128]{3,2,1,0:T(8,128)S(1)}, u32[]{:S(2)}, u32[]{:S(2)}) collective-permute-start(f32[5,6,8,128]{3,2,1,0:T(8,128)S(1)} %get-tuple-element.47), channel_id=1, source_target_pairs={{255,62},{0,1},{1,0},{2,3},{3,2},{4,5},{5,4},{6,7},{7,6},{8,9},{9,... | collective-permute-start | bytes 368648 | tf_op jit(solution)/shard_map/ppermute | solution.py:678
  16.0 0.7 %copy-start = (f32[16,16]{1,0:T(8,128)S(1)}, f32[16,16]{1,0:T(8,128)}, u32[]{:S(2)}) copy-start(f32[16,16]{1,0:T(8,128)} %reaction.1) | copy-start | bytes 3076
  17.6 3.9 %collective-permute-start.3 = (f32[6,16,128]{2,1,0:T(8,128)S(1)}, f32[6,16,128]{2,1,0:T(8,128)S(1)}, u32[]{:S(2)}, u32[]{:S(2)}) collective-permute-start(f32[6,16,128]{2,1,0:T(8,128)S(1)} %get-tuple-element.43), channel_id=1, source_target_pairs={{255,62},{0,1},{1,0},{2,3},{3,2},{4,5},{5,4},{6,7},{7,6},{8,9},{9,... | collective-permute-start | bytes 147464 | tf_op jit(solution)/shard_map/ppermute | solution.py:671
  17.7 3.8 %collective-permute-start.2 = (f32[6,16,128]{2,1,0:T(8,128)S(1)}, f32[6,16,128]{2,1,0:T(8,128)S(1)}, u32[]{:S(2)}, u32[]{:S(2)}) collective-permute-start(f32[6,16,128]{2,1,0:T(8,128)S(1)} %get-tuple-element.43), channel_id=1, source_target_pairs={{255,63},{0,64},{1,65},{2,66},{3,67},{4,68},{5,69},{6,70},{7,71},{... | collective-permute-start | bytes 147464 | tf_op jit(solution)/shard_map/ppermute | solution.py:671
  21.6 6.8 %collective-permute-start.6 = (f32[21,8,128]{2,1,0:T(8,128)S(1)}, f32[21,8,128]{2,1,0:T(8,128)S(1)}, u32[]{:S(2)}, u32[]{:S(2)}) collective-permute-start(f32[21,8,128]{2,1,0:T(8,128)S(1)} %get-tuple-element.57), channel_id=1, source_target_pairs={{255,62},{0,1},{1,0},{2,3},{3,2},{4,5},{5,4},{6,7},{7,6},{8,9},{9,... | collective-permute-start | bytes 258056 | tf_op jit(solution)/shard_map/ppermute | solution.py:671
  22.8 6.2 %collective-permute-start.7 = (f32[21,8,128]{2,1,0:T(8,128)S(1)}, f32[21,8,128]{2,1,0:T(8,128)S(1)}, u32[]{:S(2)}, u32[]{:S(2)}) collective-permute-start(f32[21,8,128]{2,1,0:T(8,128)S(1)} %get-tuple-element.58), channel_id=1, source_target_pairs={{255,191},{0,192},{1,193},{2,194},{3,195},{4,196},{5,197},{6,198},... | collective-permute-start | bytes 258056 | tf_op jit(solution)/shard_map/ppermute | solution.py:671
  22.9 6.2 %collective-permute-start.8 = (f32[21,8,128]{2,1,0:T(8,128)S(1)}, f32[21,8,128]{2,1,0:T(8,128)S(1)}, u32[]{:S(2)}, u32[]{:S(2)}) collective-permute-start(f32[21,8,128]{2,1,0:T(8,128)S(1)} %get-tuple-element.59), channel_id=1, source_target_pairs={{255,63},{0,64},{1,65},{2,66},{3,67},{4,68},{5,69},{6,70},{7,71},{... | collective-permute-start | bytes 258056 | tf_op jit(solution)/shard_map/ppermute | solution.py:671
  30.7 6.3 %collective-permute-start.9 = (f32[24,8,128]{2,1,0:T(8,128)S(1)}, f32[24,8,128]{2,1,0:T(8,128)S(1)}, u32[]{:S(2)}, u32[]{:S(2)}) collective-permute-start(f32[24,8,128]{2,1,0:T(8,128)S(1)} %get-tuple-element.66), channel_id=1, source_target_pairs={{255,62},{0,1},{1,0},{2,3},{3,2},{4,5},{5,4},{6,7},{7,6},{8,9},{9,... | collective-permute-start | bytes 294920 | tf_op jit(solution)/shard_map/ppermute | solution.py:671
  31.2 6.8 %collective-permute-start.10 = (f32[24,8,128]{2,1,0:T(8,128)S(1)}, f32[24,8,128]{2,1,0:T(8,128)S(1)}, u32[]{:S(2)}, u32[]{:S(2)}) collective-permute-start(f32[24,8,128]{2,1,0:T(8,128)S(1)} %get-tuple-element.67), channel_id=1, source_target_pairs={{255,191},{0,192},{1,193},{2,194},{3,195},{4,196},{5,197},{6,198},... | collective-permute-start | bytes 294920 | tf_op jit(solution)/shard_map/ppermute | solution.py:671
  31.7 6.3 %collective-permute-start.11 = (f32[24,8,128]{2,1,0:T(8,128)S(1)}, f32[24,8,128]{2,1,0:T(8,128)S(1)}, u32[]{:S(2)}, u32[]{:S(2)}) collective-permute-start(f32[24,8,128]{2,1,0:T(8,128)S(1)} %get-tuple-element.68), channel_id=1, source_target_pairs={{255,62},{0,1},{1,0},{2,3},{3,2},{4,5},{5,4},{6,7},{7,6},{8,9},{9,... | collective-permute-start | bytes 294920 | tf_op jit(solution)/shard_map/ppermute | solution.py:671

commit v6 on v5

--- a/solution.py
+++ b/solution.py
@@ -10,7 +10,7 @@
 SHARED = 10
 DT = 0.1
 F32 = jnp.float32
-UNROLL = 2
+UNROLL = 6
 VMEM_LIMIT = 24 * 1024 * 1024
 
 
@@ -433,7 +433,7 @@
 
 
 def sides_kernel(
-    inner, outer, send_a, send_b, send_c, partial, rim_edges, rim_wet, wet_rows,
+    outer, inner, send_a, send_b, send_c, partial, rim_edges, rim_wet, wet_rows,
     out_a, out_b, out_c,
 ):
     section, _, _ = place()
@@ -480,7 +480,7 @@
     return [buffer.at[f] for f in range(4)]
 
 
-def early_kernel(flow_next, wet_rows, partial, inner, outer, early, tracers_next):
+def early_kernel(flow_next, wet_rows, partial, outer, inner, early, tracers_next):
     section, _, _ = place()
     nt, levels = partial.shape[0], partial.shape[1]
 
@@ -744,7 +744,7 @@
     sent = call(
         sides_kernel,
         [exchange, exchange, exchange],
-        (inner, outer, *sends, partial, rim_edges, rim_wet, wet_rows),
+        (outer, inner, *sends, partial, rim_edges, rim_wet, wet_rows),
         (vmem,) * 9,
     )
     from_b = trade(sent[1], (3, 1))
@@ -753,7 +753,7 @@
     early, tracers_next = call(
         early_kernel,
         [((4, levels, 3, 32, 128), F32), ((nt, levels, 16, 128), F32)],
-        (flow_next, wet_rows, partial, inner, outer),
+        (flow_next, wet_rows, partial, outer, inner),
         (vmem,) * 5,
     )
     exchange = ((24, 8, 128), F32)

time: 39.2 us -> 38.8 us (0.990)
  the two profiles are of different devices: /device:TPU:6 before, /device:TPU:127 now
where the time goes in v6:
time: 38.8 us; the launch traced here: 38.6 us
  waiting for transfers between devices  15.6 us (40%)
  starting transfers between devices  13.8 us (36%)
  Pallas kernels  7.77 us (20%)
  between operations  0.72 us (2%)
  local copies, waits for them, and re-layouts  0.7 us (2%)
    ppermute x8, waiting for transfers between devices, trade(): return lax.ppermute(value, AXES, route(target))  9.77 us
    pallas_call x9, Pallas kernels, call(): pl.pallas_call(kernel, out_shape=[jax.ShapeDtypeStruct(shape, dtype) for...  7.77 us
    ppermute x2, starting transfers between devices, along_dynamics(): return lax.ppermute(value, AXES, route(target))  5.36 us
    ppermute x8, starting transfers between devices, trade(): return lax.ppermute(value, AXES, route(target))  4.28 us
    ppermute x2, starting transfers between devices, along(): lax.ppermute(value, AXES, route(lambda k, s, g: divmod((k * g + s + by) %...  4.16 us
    ppermute x2, waiting for transfers between devices, along_dynamics(): return lax.ppermute(value, AXES, route(target))  3.53 us
    ppermute x2, waiting for transfers between devices, along(): lax.ppermute(value, AXES, route(lambda k, s, g: divmod((k * g + s + by) %...  2.29 us
  transfers between devices with their start and end apart: 12, of which 6 were waited for; matrix products, arithmetic and copies ran while one was open for 0% of the time, Pallas kernels for 12%

profile of v6, /device:TPU:127, one launch (start us, length us, event | category | flops | bytes accessed | tf_op | source)
XLA Modules:
  0.0 38.6 jit_solution(15840999449612862881)
XLA Ops:
  0.6 1.2 %shard_map.102 = (f32[10,6,8,128]{3,2,1,0:T(8,128)S(1)}, f32[10,6,8,128]{3,2,1,0:T(8,128)S(1)}, f32[5,6,8,128]{3,2,1,0:T(8,128)S(1)}, f32[5,6,8,128]{3,2,1,0:T(8...) custom-call(f32[4,6,8,384]{3,2,1,0:T(8,128)} %flow.1, ...), custom_call_target="tpu_custom_call" | custom-call | tf_op jit(solution)/shard_map/pallas_call | solution.py:637
  1.9 4.2 %collective-permute-start = (f32[10,6,8,128]{3,2,1,0:T(8,128)S(1)}, f32[10,6,8,128]{3,2,1,0:T(8,128)S(1)}, u32[]{:S(2)}, u32[]{:S(2)}) collective-permute-start(f32[10,6,8,128]{3,2,1,0:T(8,128)S(1)} %get-tuple-element.40), channel_id=1, source_target_pairs={{255,0},{0,1},{1,2},{2,3},{3,4},{4,5},{5,6},{6,7},{7,8},{8,9},{9,1... | collective-permute-start | bytes 737288 | tf_op jit(solution)/shard_map/ppermute | solution.py:682
  6.0 0.0 collective-permute-start.1
  6.0 5.4 %collective-permute-start.4 = (f32[5,6,8,128]{3,2,1,0:T(8,128)S(1)}, f32[5,6,8,128]{3,2,1,0:T(8,128)S(1)}, u32[]{:S(2)}, u32[]{:S(2)}) collective-permute-start(f32[5,6,8,128]{3,2,1,0:T(8,128)S(1)} %get-tuple-element.46), channel_id=1, source_target_pairs={{255,62},{0,1},{1,0},{2,3},{3,2},{4,5},{5,4},{6,7},{7,6},{8,9},{9,... | collective-permute-start | bytes 368648 | tf_op jit(solution)/shard_map/ppermute | solution.py:678
  11.4 0.0 collective-permute-start.5
  11.4 0.7 %copy-done = f32[16,16]{1,0:T(8,128)S(1)} copy-done((f32[16,16]{1,0:T(8,128)S(1)}, f32[16,16]{1,0:T(8,128)}, u32[]{:S(2)}) %copy-start) | copy-done | bytes 1048
  12.1 0.9 %shard_map.103 = (s32[3,24,128]{2,1,0:T(8,128)S(1)}, f32[16,16,128]{2,1,0:T(8,128)S(1)}) custom-call(s32[512,384]{1,0:T(8,128)} %ocean.1, s32[512,384]{1,0:T(8,128)} %bottom.1, f32[16,16]{1,0:T(8,128)S(1)} %copy-done), custom_call_target="tpu_custom_call" | custom-call | tf_op jit(solution)/shard_map/pallas_call | solution.py:637
  13.0 0.0 collective-permute-done.above
  13.0 2.3 %collective-permute-done.1.below = f32[10,6,8,128]{3,2,1,0:T(8,128)S(1)} collective-permute-done((f32[10,6,8,128]{3,2,1,0:T(8,128)S(1)}, f32[10,6,8,128]{3,2,1,0:T(8,128)S(1)}, u32[]{:S(2)}, u32[]{:S(2)}) %collective-permute-start.1) | collective-permute-done | bytes 245792 | tf_op jit(solution)/shard_map/ppermute | solution.py:682
  15.3 0.0 collective-permute-start.3
  15.3 0.5 %collective-permute-start.2 = (f32[6,16,128]{2,1,0:T(8,128)S(1)}, f32[6,16,128]{2,1,0:T(8,128)S(1)}, u32[]{:S(2)}, u32[]{:S(2)}) collective-permute-start(f32[6,16,128]{2,1,0:T(8,128)S(1)} %get-tuple-element.43), channel_id=1, source_target_pairs={{255,62},{0,1},{1,0},{2,3},{3,2},{4,5},{5,4},{6,7},{7,6},{8,9},{9,... | collective-permute-start | bytes 147464 | tf_op jit(solution)/shard_map/ppermute | solution.py:671
  15.8 0.0 collective-permute-done.4.more_above
  15.8 3.5 %collective-permute-done.5.more_below = f32[5,6,8,128]{3,2,1,0:T(8,128)S(1)} collective-permute-done((f32[5,6,8,128]{3,2,1,0:T(8,128)S(1)}, f32[5,6,8,128]{3,2,1,0:T(8,128)S(1)}, u32[]{:S(2)}, u32[]{:S(2)}) %collective-permute-start.5) | collective-permute-done | bytes 122912 | tf_op jit(solution)/shard_map/ppermute | solution.py:678
  19.3 2.5 %shard_map.105 = (f32[21,8,128]{2,1,0:T(8,128)S(1)}, f32[21,8,128]{2,1,0:T(8,128)S(1)}, f32[21,8,128]{2,1,0:T(8,128)S(1)}, f32[4,6,3,32,128]{4,3,2,1,0:T(8,128)S...) custom-call(f32[4,6,3,8,128]{4,3,2,1,0:T(8,128)S(1)} %get-tuple-element.44.flow, ...), custom_call_target="tpu_custom_call" | custom-call | tf_op jit(solution)/shard_map/pallas_call | solution.py:637
  21.7 0.0 collective-permute-done.3.inner
  21.7 0.0 collective-permute-done.2.outer
  21.8 0.1 collective-permute-start.6
  21.9 0.1 collective-permute-start.7
  22.0 2.5 %collective-permute-start.8 = (f32[21,8,128]{2,1,0:T(8,128)S(1)}, f32[21,8,128]{2,1,0:T(8,128)S(1)}, u32[]{:S(2)}, u32[]{:S(2)}) collective-permute-start(f32[21,8,128]{2,1,0:T(8,128)S(1)} %get-tuple-element.59), channel_id=1, source_target_pairs={{255,63},{0,64},{1,65},{2,66},{3,67},{4,68},{5,69},{6,70},{7,71},{... | collective-permute-start | bytes 258056 | tf_op jit(solution)/shard_map/ppermute | solution.py:671
  24.5 0.4 %shard_map.107 = (f32[4,6,3,32,128]{4,3,2,1,0:T(8,128)S(1)}, f32[16,6,16,128]{3,2,1,0:T(8,128)S(1)}) custom-call(f32[4,6,3,32,128]{4,3,2,1,0:T(8,128)S(1)} %get-tuple-element.60.flow_next, s32[3,24,128]{2,1,0:T(8,128)S(1)} %get-tuple-element.42.wet_rows, f32[16,6,16,128]{3,2,1,0:T(8,128)S(1)} %get-tuple-element.54.partial, ...), custom_call_target="tpu_custom_call" | custom-call | tf_op jit(solution)/shard_map/pallas_call | solution.py:637
  25.0 1.8 %collective-permute-done.6.from_b = f32[21,8,128]{2,1,0:T(8,128)S(1)} collective-permute-done((f32[21,8,128]{2,1,0:T(8,128)S(1)}, f32[21,8,128]{2,1,0:T(8,128)S(1)}, u32[]{:S(2)}, u32[]{:S(2)}) %collective-permute-start.6) | collective-permute-done | bytes 86048 | tf_op jit(solution)/shard_map/ppermute | solution.py:671
  26.8 1.6 %collective-permute-done.7.from_a = f32[21,8,128]{2,1,0:T(8,128)S(1)} collective-permute-done((f32[21,8,128]{2,1,0:T(8,128)S(1)}, f32[21,8,128]{2,1,0:T(8,128)S(1)}, u32[]{:S(2)}, u32[]{:S(2)}) %collective-permute-start.7) | collective-permute-done | bytes 86048 | tf_op jit(solution)/shard_map/ppermute | solution.py:671
  28.5 0.0 collective-permute-done.8.from_c
  28.5 1.2 %shard_map.108 = (f32[24,8,128]{2,1,0:T(8,128)S(1)}, f32[24,8,128]{2,1,0:T(8,128)S(1)}, f32[24,8,128]{2,1,0:T(8,128)S(1)}, f32[4,6,3,8,128]{4,3,2,1,0:T(8,128)S(1)}, f32[16,6,8,128]{3,2,1,0:T(8,128)S(1)}) custom-call(f32[21,8,128]{2,1,0:T(8,128)S(1)} %collective-permute-done.6.from_b, f32[21,8,128]{2,1,0:T(8,128)S(1)} %collective-permute-done.7.from_a, ...), custom_call_target="tpu_custom_call" | custom-call | tf_op jit(solution)/shard_map/pallas_call | solution.py:637
  29.6 0.3 collective-permute-start.9
  29.9 0.8 %collective-permute-start.10 = (f32[24,8,128]{2,1,0:T(8,128)S(1)}, f32[24,8,128]{2,1,0:T(8,128)S(1)}, u32[]{:S(2)}, u32[]{:S(2)}) collective-permute-start(f32[24,8,128]{2,1,0:T(8,128)S(1)} %get-tuple-element.67), channel_id=1, source_target_pairs={{255,191},{0,192},{1,193},{2,194},{3,195},{4,196},{5,197},{6,198},... | collective-permute-start | bytes 294920 | tf_op jit(solution)/shard_map/ppermute | solution.py:671
  30.7 0.0 collective-permute-start.11
  30.7 0.9 %shard_map.109 = (f32[4,6,8,384]{3,2,1,0:T(8,128)}, f32[16,6,8,128]{3,2,1,0:T(8,128)}) custom-call(f32[4,6,3,8,128]{4,3,2,1,0:T(8,128)S(1)} %get-tuple-element.63.flow_last, f32[16,6,8,128]{3,2,1,0:T(8,128)S(1)} %get-tuple-element.64.tracers_last), custom_call_target="tpu_custom_call" | custom-call | tf_op jit(solution)/shard_map/pallas_call | solution.py:637
  31.6 3.5 %collective-permute-done.9.from_b = f32[24,8,128]{2,1,0:T(8,128)S(1)} collective-permute-done((f32[24,8,128]{2,1,0:T(8,128)S(1)}, f32[24,8,128]{2,1,0:T(8,128)S(1)}, u32[]{:S(2)}, u32[]{:S(2)}) %collective-permute-start.9) | collective-permute-done | bytes 98336 | tf_op jit(solution)/shard_map/ppermute | solution.py:671
  35.1 2.8 %collective-permute-done.10.from_a = f32[24,8,128]{2,1,0:T(8,128)S(1)} collective-permute-done((f32[24,8,128]{2,1,0:T(8,128)S(1)}, f32[24,8,128]{2,1,0:T(8,128)S(1)}, u32[]{:S(2)}, u32[]{:S(2)}) %collective-permute-start.10) | collective-permute-done | bytes 98336 | tf_op jit(solution)/shard_map/ppermute | solution.py:671
  37.9 0.0 collective-permute-done.11.from_c
  37.9 0.7 %shard_map.110 = (f32[6,8,384]{2,1,0:T(8,128)}, f32[4,6,8,128]{3,2,1,0:T(8,128)}) custom-call(f32[24,8,128]{2,1,0:T(8,128)S(1)} %collective-permute-done.9.from_b, f32[24,8,128]{2,1,0:T(8,128)S(1)} %collective-permute-done.10.from_a, f32[24,8,128]{2,1,0:T(8,128)S(1)} %collective-permute-done.11.from_c), custom_call_target="tpu_custom_call" | custom-call | tf_op jit(solution)/shard_map/pallas_call | solution.py:637
  (3 shorter events, 0.1 us)
Async XLA Ops:
  1.9 11.1 %collective-permute-start = (f32[10,6,8,128]{3,2,1,0:T(8,128)S(1)}, f32[10,6,8,128]{3,2,1,0:T(8,128)S(1)}, u32[]{:S(2)}, u32[]{:S(2)}) collective-permute-start(f32[10,6,8,128]{3,2,1,0:T(8,128)S(1)} %get-tuple-element.40), channel_id=1, source_target_pairs={{255,0},{0,1},{1,2},{2,3},{3,4},{4,5},{5,6},{6,7},{7,8},{8,9},{9,1... | collective-permute-start | bytes 737288 | tf_op jit(solution)/shard_map/ppermute | solution.py:682
  6.0 9.2 %collective-permute-start.1 = (f32[10,6,8,128]{3,2,1,0:T(8,128)S(1)}, f32[10,6,8,128]{3,2,1,0:T(8,128)S(1)}, u32[]{:S(2)}, u32[]{:S(2)}) collective-permute-start(f32[10,6,8,128]{3,2,1,0:T(8,128)S(1)} %get-tuple-element.41), channel_id=1, source_target_pairs={{255,254},{0,255},{1,0},{2,1},{3,2},{4,3},{5,4},{6,5},{7,6},{8,7},... | collective-permute-start | bytes 737288 | tf_op jit(solution)/shard_map/ppermute | solution.py:682
  6.0 9.8 %collective-permute-start.4 = (f32[5,6,8,128]{3,2,1,0:T(8,128)S(1)}, f32[5,6,8,128]{3,2,1,0:T(8,128)S(1)}, u32[]{:S(2)}, u32[]{:S(2)}) collective-permute-start(f32[5,6,8,128]{3,2,1,0:T(8,128)S(1)} %get-tuple-element.46), channel_id=1, source_target_pairs={{255,62},{0,1},{1,0},{2,3},{3,2},{4,5},{5,4},{6,7},{7,6},{8,9},{9,... | collective-permute-start | bytes 368648 | tf_op jit(solution)/shard_map/ppermute | solution.py:678
  11.4 7.9 %collective-permute-start.5 = (f32[5,6,8,128]{3,2,1,0:T(8,128)S(1)}, f32[5,6,8,128]{3,2,1,0:T(8,128)S(1)}, u32[]{:S(2)}, u32[]{:S(2)}) collective-permute-start(f32[5,6,8,128]{3,2,1,0:T(8,128)S(1)} %get-tuple-element.47), channel_id=1, source_target_pairs={{255,62},{0,1},{1,0},{2,3},{3,2},{4,5},{5,4},{6,7},{7,6},{8,9},{9,... | collective-permute-start | bytes 368648 | tf_op jit(solution)/shard_map/ppermute | solution.py:678
  11.4 0.7 %copy-start = (f32[16,16]{1,0:T(8,128)S(1)}, f32[16,16]{1,0:T(8,128)}, u32[]{:S(2)}) copy-start(f32[16,16]{1,0:T(8,128)} %reaction.1) | copy-start | bytes 3076
  15.3 6.5 %collective-permute-start.3 = (f32[6,16,128]{2,1,0:T(8,128)S(1)}, f32[6,16,128]{2,1,0:T(8,128)S(1)}, u32[]{:S(2)}, u32[]{:S(2)}) collective-permute-start(f32[6,16,128]{2,1,0:T(8,128)S(1)} %get-tuple-element.43), channel_id=1, source_target_pairs={{255,63},{0,64},{1,65},{2,66},{3,67},{4,68},{5,69},{6,70},{7,71},{... | collective-permute-start | bytes 147464 | tf_op jit(solution)/shard_map/ppermute | solution.py:671
  15.3 6.5 %collective-permute-start.2 = (f32[6,16,128]{2,1,0:T(8,128)S(1)}, f32[6,16,128]{2,1,0:T(8,128)S(1)}, u32[]{:S(2)}, u32[]{:S(2)}) collective-permute-start(f32[6,16,128]{2,1,0:T(8,128)S(1)} %get-tuple-element.43), channel_id=1, source_target_pairs={{255,62},{0,1},{1,0},{2,3},{3,2},{4,5},{5,4},{6,7},{7,6},{8,9},{9,... | collective-permute-start | bytes 147464 | tf_op jit(solution)/shard_map/ppermute | solution.py:671
  21.8 5.0 %collective-permute-start.6 = (f32[21,8,128]{2,1,0:T(8,128)S(1)}, f32[21,8,128]{2,1,0:T(8,128)S(1)}, u32[]{:S(2)}, u32[]{:S(2)}) collective-permute-start(f32[21,8,128]{2,1,0:T(8,128)S(1)} %get-tuple-element.57), channel_id=1, source_target_pairs={{255,62},{0,1},{1,0},{2,3},{3,2},{4,5},{5,4},{6,7},{7,6},{8,9},{9,... | collective-permute-start | bytes 258056 | tf_op jit(solution)/shard_map/ppermute | solution.py:671
  21.9 6.6 %collective-permute-start.7 = (f32[21,8,128]{2,1,0:T(8,128)S(1)}, f32[21,8,128]{2,1,0:T(8,128)S(1)}, u32[]{:S(2)}, u32[]{:S(2)}) collective-permute-start(f32[21,8,128]{2,1,0:T(8,128)S(1)} %get-tuple-element.58), channel_id=1, source_target_pairs={{255,191},{0,192},{1,193},{2,194},{3,195},{4,196},{5,197},{6,198},... | collective-permute-start | bytes 258056 | tf_op jit(solution)/shard_map/ppermute | solution.py:671
  22.0 6.5 %collective-permute-start.8 = (f32[21,8,128]{2,1,0:T(8,128)S(1)}, f32[21,8,128]{2,1,0:T(8,128)S(1)}, u32[]{:S(2)}, u32[]{:S(2)}) collective-permute-start(f32[21,8,128]{2,1,0:T(8,128)S(1)} %get-tuple-element.59), channel_id=1, source_target_pairs={{255,63},{0,64},{1,65},{2,66},{3,67},{4,68},{5,69},{6,70},{7,71},{... | collective-permute-start | bytes 258056 | tf_op jit(solution)/shard_map/ppermute | solution.py:671
  29.6 5.4 %collective-permute-start.9 = (f32[24,8,128]{2,1,0:T(8,128)S(1)}, f32[24,8,128]{2,1,0:T(8,128)S(1)}, u32[]{:S(2)}, u32[]{:S(2)}) collective-permute-start(f32[24,8,128]{2,1,0:T(8,128)S(1)} %get-tuple-element.66), channel_id=1, source_target_pairs={{255,62},{0,1},{1,0},{2,3},{3,2},{4,5},{5,4},{6,7},{7,6},{8,9},{9,... | collective-permute-start | bytes 294920 | tf_op jit(solution)/shard_map/ppermute | solution.py:671
  29.9 7.9 %collective-permute-start.10 = (f32[24,8,128]{2,1,0:T(8,128)S(1)}, f32[24,8,128]{2,1,0:T(8,128)S(1)}, u32[]{:S(2)}, u32[]{:S(2)}) collective-permute-start(f32[24,8,128]{2,1,0:T(8,128)S(1)} %get-tuple-element.67), channel_id=1, source_target_pairs={{255,191},{0,192},{1,193},{2,194},{3,195},{4,196},{5,197},{6,198},... | collective-permute-start | bytes 294920 | tf_op jit(solution)/shard_map/ppermute | solution.py:671
  30.7 7.2 %collective-permute-start.11 = (f32[24,8,128]{2,1,0:T(8,128)S(1)}, f32[24,8,128]{2,1,0:T(8,128)S(1)}, u32[]{:S(2)}, u32[]{:S(2)}) collective-permute-start(f32[24,8,128]{2,1,0:T(8,128)S(1)} %get-tuple-element.68), channel_id=1, source_target_pairs={{255,62},{0,1},{1,0},{2,3},{3,2},{4,5},{5,4},{6,7},{7,6},{8,9},{9,... | collective-permute-start | bytes 294920 | tf_op jit(solution)/shard_map/ppermute | solution.py:671

commit v7 on v6

--- a/solution.py
+++ b/solution.py
@@ -614,7 +614,7 @@
         put(lambda j: blank.at[0:4], tracers_last)
 
 
-def last_kernel(from_b, from_a, from_c, light_out, forcing_out):
+def last_kernel(from_a, from_b, from_c, light_out, forcing_out):
     section, _, _ = place()
     levels = light_out.shape[0]
     is_dynamics = section == 3
@@ -786,7 +786,7 @@
     light_out, forcing_out = call(
         last_kernel,
         [((levels, 8, breadth), F32), ((4, levels, 8, 128), F32)],
-        (final_b, final_a, final_c),
+        (final_a, final_b, final_c),
         (vmem,) * 3,
     )
     return flow_out, light_out, tracers_out, forcing_out

time: 38.8 us -> 38.5 us (level)
  the two profiles are of different devices: /device:TPU:127 before, /device:TPU:6 now
where the time goes in v7:
time: 38.5 us; the launch traced here: 38.1 us
  starting transfers between devices  19.8 us (51%)
  waiting for transfers between devices  9.02 us (23%)
  Pallas kernels  7.8 us (20%)
  between operations  0.73 us (2%)
  local copies, waits for them, and re-layouts  0.7 us (2%)
    ppermute x8, waiting for transfers between devices, trade(): return lax.ppermute(value, AXES, route(target))  8.69 us
    ppermute x2, starting transfers between devices, along(): lax.ppermute(value, AXES, route(lambda k, s, g: divmod((k * g + s + by) %...  8.17 us
    pallas_call x9, Pallas kernels, call(): pl.pallas_call(kernel, out_shape=[jax.ShapeDtypeStruct(shape, dtype) for...  7.8 us
    ppermute x2, starting transfers between devices, along_dynamics(): return lax.ppermute(value, AXES, route(target))  5.96 us
    ppermute x8, starting transfers between devices, trade(): return lax.ppermute(value, AXES, route(target))  5.67 us
  transfers between devices with their start and end apart: 12, of which 5 were waited for; matrix products, arithmetic and copies ran while one was open for 0% of the time, Pallas kernels for 12%

profile of v7, /device:TPU:6, one launch (start us, length us, event | category | flops | bytes accessed | tf_op | source)
XLA Modules:
  0.0 38.1 jit_solution(9307666849341363910)
XLA Ops:
  0.6 1.2 %shard_map.102 = (f32[10,6,8,128]{3,2,1,0:T(8,128)S(1)}, f32[10,6,8,128]{3,2,1,0:T(8,128)S(1)}, f32[5,6,8,128]{3,2,1,0:T(8,128)S(1)}, f32[5,6,8,128]{3,2,1,0:T(8...) custom-call(f32[4,6,8,384]{3,2,1,0:T(8,128)} %flow.1, ...), custom_call_target="tpu_custom_call" | custom-call | tf_op jit(solution)/shard_map/pallas_call | solution.py:637
  1.9 0.1 collective-permute-start
  1.9 8.1 %collective-permute-start.1 = (f32[10,6,8,128]{3,2,1,0:T(8,128)S(1)}, f32[10,6,8,128]{3,2,1,0:T(8,128)S(1)}, u32[]{:S(2)}, u32[]{:S(2)}) collective-permute-start(f32[10,6,8,128]{3,2,1,0:T(8,128)S(1)} %get-tuple-element.41), channel_id=1, source_target_pairs={{255,254},{0,255},{1,0},{2,1},{3,2},{4,3},{5,4},{6,5},{7,6},{8,7},... | collective-permute-start | bytes 737288 | tf_op jit(solution)/shard_map/ppermute | solution.py:682
  10.0 0.0 collective-permute-start.4
  10.0 6.0 %collective-permute-start.5 = (f32[5,6,8,128]{3,2,1,0:T(8,128)S(1)}, f32[5,6,8,128]{3,2,1,0:T(8,128)S(1)}, u32[]{:S(2)}, u32[]{:S(2)}) collective-permute-start(f32[5,6,8,128]{3,2,1,0:T(8,128)S(1)} %get-tuple-element.47), channel_id=1, source_target_pairs={{255,62},{0,1},{1,0},{2,3},{3,2},{4,5},{5,4},{6,7},{7,6},{8,9},{9,... | collective-permute-start | bytes 368648 | tf_op jit(solution)/shard_map/ppermute | solution.py:678
  16.0 0.7 %copy-done = f32[16,16]{1,0:T(8,128)S(1)} copy-done((f32[16,16]{1,0:T(8,128)S(1)}, f32[16,16]{1,0:T(8,128)}, u32[]{:S(2)}) %copy-start) | copy-done | bytes 1048
  16.7 0.9 %shard_map.103 = (s32[3,24,128]{2,1,0:T(8,128)S(1)}, f32[16,16,128]{2,1,0:T(8,128)S(1)}) custom-call(s32[512,384]{1,0:T(8,128)} %ocean.1, s32[512,384]{1,0:T(8,128)} %bottom.1, f32[16,16]{1,0:T(8,128)S(1)} %copy-done), custom_call_target="tpu_custom_call" | custom-call | tf_op jit(solution)/shard_map/pallas_call | solution.py:637
  17.6 0.0 collective-permute-done.above
  17.6 0.0 collective-permute-done.1.below
  17.6 0.1 collective-permute-start.3
  17.7 0.5 %collective-permute-start.2 = (f32[6,16,128]{2,1,0:T(8,128)S(1)}, f32[6,16,128]{2,1,0:T(8,128)S(1)}, u32[]{:S(2)}, u32[]{:S(2)}) collective-permute-start(f32[6,16,128]{2,1,0:T(8,128)S(1)} %get-tuple-element.43), channel_id=1, source_target_pairs={{255,62},{0,1},{1,0},{2,3},{3,2},{4,5},{5,4},{6,7},{7,6},{8,9},{9,... | collective-permute-start | bytes 147464 | tf_op jit(solution)/shard_map/ppermute | solution.py:671
  18.2 0.3 collective-permute-done.4.more_above
  18.6 0.0 collective-permute-done.5.more_below
  18.6 2.5 %shard_map.105 = (f32[21,8,128]{2,1,0:T(8,128)S(1)}, f32[21,8,128]{2,1,0:T(8,128)S(1)}, f32[21,8,128]{2,1,0:T(8,128)S(1)}, f32[4,6,3,32,128]{4,3,2,1,0:T(8,128)S...) custom-call(f32[4,6,3,8,128]{4,3,2,1,0:T(8,128)S(1)} %get-tuple-element.44.flow, ...), custom_call_target="tpu_custom_call" | custom-call | tf_op jit(solution)/shard_map/pallas_call | solution.py:637
  21.0 0.0 collective-permute-done.3.inner
  21.0 0.0 collective-permute-done.2.outer
  21.1 1.4 %collective-permute-start.6 = (f32[21,8,128]{2,1,0:T(8,128)S(1)}, f32[21,8,128]{2,1,0:T(8,128)S(1)}, u32[]{:S(2)}, u32[]{:S(2)}) collective-permute-start(f32[21,8,128]{2,1,0:T(8,128)S(1)} %get-tuple-element.57), channel_id=1, source_target_pairs={{255,62},{0,1},{1,0},{2,3},{3,2},{4,5},{5,4},{6,7},{7,6},{8,9},{9,... | collective-permute-start | bytes 258056 | tf_op jit(solution)/shard_map/ppermute | solution.py:671
  22.5 0.0 collective-permute-start.7
  22.5 2.2 %collective-permute-start.8 = (f32[21,8,128]{2,1,0:T(8,128)S(1)}, f32[21,8,128]{2,1,0:T(8,128)S(1)}, u32[]{:S(2)}, u32[]{:S(2)}) collective-permute-start(f32[21,8,128]{2,1,0:T(8,128)S(1)} %get-tuple-element.59), channel_id=1, source_target_pairs={{255,63},{0,64},{1,65},{2,66},{3,67},{4,68},{5,69},{6,70},{7,71},{... | collective-permute-start | bytes 258056 | tf_op jit(solution)/shard_map/ppermute | solution.py:671
  24.7 0.4 %shard_map.107 = (f32[4,6,3,32,128]{4,3,2,1,0:T(8,128)S(1)}, f32[16,6,16,128]{3,2,1,0:T(8,128)S(1)}) custom-call(f32[4,6,3,32,128]{4,3,2,1,0:T(8,128)S(1)} %get-tuple-element.60.flow_next, s32[3,24,128]{2,1,0:T(8,128)S(1)} %get-tuple-element.42.wet_rows, f32[16,6,16,128]{3,2,1,0:T(8,128)S(1)} %get-tuple-element.54.partial, ...), custom_call_target="tpu_custom_call" | custom-call | tf_op jit(solution)/shard_map/pallas_call | solution.py:637
  25.1 2.8 %collective-permute-done.6.from_b = f32[21,8,128]{2,1,0:T(8,128)S(1)} collective-permute-done((f32[21,8,128]{2,1,0:T(8,128)S(1)}, f32[21,8,128]{2,1,0:T(8,128)S(1)}, u32[]{:S(2)}, u32[]{:S(2)}) %collective-permute-start.6) | collective-permute-done | bytes 86048 | tf_op jit(solution)/shard_map/ppermute | solution.py:671
  27.9 0.7 %collective-permute-done.7.from_a = f32[21,8,128]{2,1,0:T(8,128)S(1)} collective-permute-done((f32[21,8,128]{2,1,0:T(8,128)S(1)}, f32[21,8,128]{2,1,0:T(8,128)S(1)}, u32[]{:S(2)}, u32[]{:S(2)}) %collective-permute-start.7) | collective-permute-done | bytes 86048 | tf_op jit(solution)/shard_map/ppermute | solution.py:671
  28.6 0.0 collective-permute-done.8.from_c
  28.6 1.2 %shard_map.108 = (f32[24,8,128]{2,1,0:T(8,128)S(1)}, f32[24,8,128]{2,1,0:T(8,128)S(1)}, f32[24,8,128]{2,1,0:T(8,128)S(1)}, f32[4,6,3,8,128]{4,3,2,1,0:T(8,128)S(1)}, f32[16,6,8,128]{3,2,1,0:T(8,128)S(1)}) custom-call(f32[21,8,128]{2,1,0:T(8,128)S(1)} %collective-permute-done.6.from_b, f32[21,8,128]{2,1,0:T(8,128)S(1)} %collective-permute-done.7.from_a, ...), custom_call_target="tpu_custom_call" | custom-call | tf_op jit(solution)/shard_map/pallas_call | solution.py:637
  29.7 1.5 %collective-permute-start.9 = (f32[24,8,128]{2,1,0:T(8,128)S(1)}, f32[24,8,128]{2,1,0:T(8,128)S(1)}, u32[]{:S(2)}, u32[]{:S(2)}) collective-permute-start(f32[24,8,128]{2,1,0:T(8,128)S(1)} %get-tuple-element.66), channel_id=1, source_target_pairs={{255,191},{0,192},{1,193},{2,194},{3,195},{4,196},{5,197},{6,198},... | collective-permute-start | bytes 294920 | tf_op jit(solution)/shard_map/ppermute | solution.py:671
  31.2 0.0 collective-permute-start.10
  31.2 0.0 collective-permute-start.11
  31.2 0.9 %shard_map.109 = (f32[4,6,8,384]{3,2,1,0:T(8,128)}, f32[16,6,8,128]{3,2,1,0:T(8,128)}) custom-call(f32[4,6,3,8,128]{4,3,2,1,0:T(8,128)S(1)} %get-tuple-element.63.flow_last, f32[16,6,8,128]{3,2,1,0:T(8,128)S(1)} %get-tuple-element.64.tracers_last), custom_call_target="tpu_custom_call" | custom-call | tf_op jit(solution)/shard_map/pallas_call | solution.py:637
  32.2 3.5 %collective-permute-done.9.from_a = f32[24,8,128]{2,1,0:T(8,128)S(1)} collective-permute-done((f32[24,8,128]{2,1,0:T(8,128)S(1)}, f32[24,8,128]{2,1,0:T(8,128)S(1)}, u32[]{:S(2)}, u32[]{:S(2)}) %collective-permute-start.9) | collective-permute-done | bytes 98336 | tf_op jit(solution)/shard_map/ppermute | solution.py:671
  35.7 1.7 %collective-permute-done.10.from_b = f32[24,8,128]{2,1,0:T(8,128)S(1)} collective-permute-done((f32[24,8,128]{2,1,0:T(8,128)S(1)}, f32[24,8,128]{2,1,0:T(8,128)S(1)}, u32[]{:S(2)}, u32[]{:S(2)}) %collective-permute-start.10) | collective-permute-done | bytes 98336 | tf_op jit(solution)/shard_map/ppermute | solution.py:671
  37.4 0.0 collective-permute-done.11.from_c
  37.4 0.7 %shard_map.110 = (f32[6,8,384]{2,1,0:T(8,128)}, f32[4,6,8,128]{3,2,1,0:T(8,128)}) custom-call(f32[24,8,128]{2,1,0:T(8,128)S(1)} %collective-permute-done.9.from_a, f32[24,8,128]{2,1,0:T(8,128)S(1)} %collective-permute-done.10.from_b, f32[24,8,128]{2,1,0:T(8,128)S(1)} %collective-permute-done.11.from_c), custom_call_target="tpu_custom_call" | custom-call | tf_op jit(solution)/shard_map/pallas_call | solution.py:637
  (3 shorter events, 0.1 us)
Async XLA Ops:
  1.9 15.7 %collective-permute-start = (f32[10,6,8,128]{3,2,1,0:T(8,128)S(1)}, f32[10,6,8,128]{3,2,1,0:T(8,128)S(1)}, u32[]{:S(2)}, u32[]{:S(2)}) collective-permute-start(f32[10,6,8,128]{3,2,1,0:T(8,128)S(1)} %get-tuple-element.40), channel_id=1, source_target_pairs={{255,0},{0,1},{1,2},{2,3},{3,4},{4,5},{5,6},{6,7},{7,8},{8,9},{9,1... | collective-permute-start | bytes 737288 | tf_op jit(solution)/shard_map/ppermute | solution.py:682
  1.9 15.6 %collective-permute-start.1 = (f32[10,6,8,128]{3,2,1,0:T(8,128)S(1)}, f32[10,6,8,128]{3,2,1,0:T(8,128)S(1)}, u32[]{:S(2)}, u32[]{:S(2)}) collective-permute-start(f32[10,6,8,128]{3,2,1,0:T(8,128)S(1)} %get-tuple-element.41), channel_id=1, source_target_pairs={{255,254},{0,255},{1,0},{2,1},{3,2},{4,3},{5,4},{6,5},{7,6},{8,7},... | collective-permute-start | bytes 737288 | tf_op jit(solution)/shard_map/ppermute | solution.py:682
  10.0 8.5 %collective-permute-start.4 = (f32[5,6,8,128]{3,2,1,0:T(8,128)S(1)}, f32[5,6,8,128]{3,2,1,0:T(8,128)S(1)}, u32[]{:S(2)}, u32[]{:S(2)}) collective-permute-start(f32[5,6,8,128]{3,2,1,0:T(8,128)S(1)} %get-tuple-element.46), channel_id=1, source_target_pairs={{255,62},{0,1},{1,0},{2,3},{3,2},{4,5},{5,4},{6,7},{7,6},{8,9},{9,... | collective-permute-start | bytes 368648 | tf_op jit(solution)/shard_map/ppermute | solution.py:678
  10.0 8.5 %collective-permute-start.5 = (f32[5,6,8,128]{3,2,1,0:T(8,128)S(1)}, f32[5,6,8,128]{3,2,1,0:T(8,128)S(1)}, u32[]{:S(2)}, u32[]{:S(2)}) collective-permute-start(f32[5,6,8,128]{3,2,1,0:T(8,128)S(1)} %get-tuple-element.47), channel_id=1, source_target_pairs={{255,62},{0,1},{1,0},{2,3},{3,2},{4,5},{5,4},{6,7},{7,6},{8,9},{9,... | collective-permute-start | bytes 368648 | tf_op jit(solution)/shard_map/ppermute | solution.py:678
  16.0 0.7 %copy-start = (f32[16,16]{1,0:T(8,128)S(1)}, f32[16,16]{1,0:T(8,128)}, u32[]{:S(2)}) copy-start(f32[16,16]{1,0:T(8,128)} %reaction.1) | copy-start | bytes 3076
  17.6 3.4 %collective-permute-start.3 = (f32[6,16,128]{2,1,0:T(8,128)S(1)}, f32[6,16,128]{2,1,0:T(8,128)S(1)}, u32[]{:S(2)}, u32[]{:S(2)}) collective-permute-start(f32[6,16,128]{2,1,0:T(8,128)S(1)} %get-tuple-element.43), channel_id=1, source_target_pairs={{255,63},{0,64},{1,65},{2,66},{3,67},{4,68},{5,69},{6,70},{7,71},{... | collective-permute-start | bytes 147464 | tf_op jit(solution)/shard_map/ppermute | solution.py:671
  17.7 3.3 %collective-permute-start.2 = (f32[6,16,128]{2,1,0:T(8,128)S(1)}, f32[6,16,128]{2,1,0:T(8,128)S(1)}, u32[]{:S(2)}, u32[]{:S(2)}) collective-permute-start(f32[6,16,128]{2,1,0:T(8,128)S(1)} %get-tuple-element.43), channel_id=1, source_target_pairs={{255,62},{0,1},{1,0},{2,3},{3,2},{4,5},{5,4},{6,7},{7,6},{8,9},{9,... | collective-permute-start | bytes 147464 | tf_op jit(solution)/shard_map/ppermute | solution.py:671
  21.1 6.8 %collective-permute-start.6 = (f32[21,8,128]{2,1,0:T(8,128)S(1)}, f32[21,8,128]{2,1,0:T(8,128)S(1)}, u32[]{:S(2)}, u32[]{:S(2)}) collective-permute-start(f32[21,8,128]{2,1,0:T(8,128)S(1)} %get-tuple-element.57), channel_id=1, source_target_pairs={{255,62},{0,1},{1,0},{2,3},{3,2},{4,5},{5,4},{6,7},{7,6},{8,9},{9,... | collective-permute-start | bytes 258056 | tf_op jit(solution)/shard_map/ppermute | solution.py:671
  22.5 6.1 %collective-permute-start.7 = (f32[21,8,128]{2,1,0:T(8,128)S(1)}, f32[21,8,128]{2,1,0:T(8,128)S(1)}, u32[]{:S(2)}, u32[]{:S(2)}) collective-permute-start(f32[21,8,128]{2,1,0:T(8,128)S(1)} %get-tuple-element.58), channel_id=1, source_target_pairs={{255,191},{0,192},{1,193},{2,194},{3,195},{4,196},{5,197},{6,198},... | collective-permute-start | bytes 258056 | tf_op jit(solution)/shard_map/ppermute | solution.py:671
  22.5 6.1 %collective-permute-start.8 = (f32[21,8,128]{2,1,0:T(8,128)S(1)}, f32[21,8,128]{2,1,0:T(8,128)S(1)}, u32[]{:S(2)}, u32[]{:S(2)}) collective-permute-start(f32[21,8,128]{2,1,0:T(8,128)S(1)} %get-tuple-element.59), channel_id=1, source_target_pairs={{255,63},{0,64},{1,65},{2,66},{3,67},{4,68},{5,69},{6,70},{7,71},{... | collective-permute-start | bytes 258056 | tf_op jit(solution)/shard_map/ppermute | solution.py:671
  29.7 5.9 %collective-permute-start.9 = (f32[24,8,128]{2,1,0:T(8,128)S(1)}, f32[24,8,128]{2,1,0:T(8,128)S(1)}, u32[]{:S(2)}, u32[]{:S(2)}) collective-permute-start(f32[24,8,128]{2,1,0:T(8,128)S(1)} %get-tuple-element.66), channel_id=1, source_target_pairs={{255,191},{0,192},{1,193},{2,194},{3,195},{4,196},{5,197},{6,198},... | collective-permute-start | bytes 294920 | tf_op jit(solution)/shard_map/ppermute | solution.py:671
  31.2 6.1 %collective-permute-start.10 = (f32[24,8,128]{2,1,0:T(8,128)S(1)}, f32[24,8,128]{2,1,0:T(8,128)S(1)}, u32[]{:S(2)}, u32[]{:S(2)}) collective-permute-start(f32[24,8,128]{2,1,0:T(8,128)S(1)} %get-tuple-element.67), channel_id=1, source_target_pairs={{255,62},{0,1},{1,0},{2,3},{3,2},{4,5},{5,4},{6,7},{7,6},{8,9},{9,... | collective-permute-start | bytes 294920 | tf_op jit(solution)/shard_map/ppermute | solution.py:671
  31.2 6.1 %collective-permute-start.11 = (f32[24,8,128]{2,1,0:T(8,128)S(1)}, f32[24,8,128]{2,1,0:T(8,128)S(1)}, u32[]{:S(2)}, u32[]{:S(2)}) collective-permute-start(f32[24,8,128]{2,1,0:T(8,128)S(1)} %get-tuple-element.68), channel_id=1, source_target_pairs={{255,62},{0,1},{1,0},{2,3},{3,2},{4,5},{5,4},{6,7},{7,6},{8,9},{9,... | collective-permute-start | bytes 294920 | tf_op jit(solution)/shard_map/ppermute | solution.py:671

commit v8 on v7

--- a/solution.py
+++ b/solution.py
@@ -506,7 +506,7 @@
 
 
 def second_kernel(
-    from_b, from_a, from_c, early, tracers_next, wet_rows, reaction,
+    from_a, from_b, from_c, early, tracers_next, wet_rows, reaction,
     out_a, out_b, out_c, flow_last, tracers_last, warm, field_1, field_2, heat, winds,
 ):
     section, _, _ = place()
@@ -614,7 +614,7 @@
         put(lambda j: blank.at[0:4], tracers_last)
 
 
-def last_kernel(from_a, from_b, from_c, light_out, forcing_out):
+def last_kernel(from_a, from_c, from_b, light_out, forcing_out):
     section, _, _ = place()
     levels = light_out.shape[0]
     is_dynamics = section == 3
@@ -763,7 +763,7 @@
             exchange, exchange, exchange,
             ((4, levels, 3, 8, 128), F32), ((nt, levels, 8, 128), F32),
         ],
-        (from_b, from_a, from_c, early, tracers_next, wet_rows, rates),
+        (from_a, from_b, from_c, early, tracers_next, wet_rows, rates),
         (vmem,) * 7,
         (
             pltpu.VMEM((levels, 3, 32, 128), F32),
@@ -786,7 +786,7 @@
     light_out, forcing_out = call(
         last_kernel,
         [((levels, 8, breadth), F32), ((4, levels, 8, 128), F32)],
-        (final_a, final_b, final_c),
+        (final_a, final_c, final_b),
         (vmem,) * 3,
     )
     return flow_out, light_out, tracers_out, forcing_out

time: 38.5 us -> 38.4 us (level)
  waiting for transfers between devices: 9.02 us -> 11.1 us
  starting transfers between devices: 19.8 us -> 17.8 us
    ppermute x8, waiting for transfers between devices: 8.69 us -> 10.7 us  [trade(): return lax.ppermute(value, AXES, route(target))]
    ppermute x8, starting transfers between devices: 5.67 us -> 3.7 us  [trade(): return lax.ppermute(value, AXES, route(target))]
  transfers between devices with their start and end apart: 12 -> 12, of which waited for: 5 -> 3; matrix products, arithmetic and copies ran while one was open for 0% -> 0% of each run, Pallas kernels for 12% -> 12%
where the time goes in v8:
time: 38.4 us; the launch traced here: 38.1 us
  starting transfers between devices  17.8 us (46%)
  waiting for transfers between devices  11.1 us (29%)
  Pallas kernels  7.81 us (20%)
  between operations  0.74 us (2%)
  local copies, waits for them, and re-layouts  0.7 us (2%)
    ppermute x8, waiting for transfers between devices, trade(): return lax.ppermute(value, AXES, route(target))  10.7 us
    ppermute x2, starting transfers between devices, along(): lax.ppermute(value, AXES, route(lambda k, s, g: divmod((k * g + s + by) %...  8.17 us
    pallas_call x9, Pallas kernels, call(): pl.pallas_call(kernel, out_shape=[jax.ShapeDtypeStruct(shape, dtype) for...  7.81 us
    ppermute x2, starting transfers between devices, along_dynamics(): return lax.ppermute(value, AXES, route(target))  5.96 us
    ppermute x8, starting transfers between devices, trade(): return lax.ppermute(value, AXES, route(target))  3.7 us
  transfers between devices with their start and end apart: 12, of which 3 were waited for; matrix products, arithmetic and copies ran while one was open for 0% of the time, Pallas kernels for 12%

profile of v8, /device:TPU:6, one launch (start us, length us, event | category | flops | bytes accessed | tf_op | source)
XLA Modules:
  0.0 38.1 jit_solution(139358922870281327)
XLA Ops:
  0.6 1.2 %shard_map.102 = (f32[10,6,8,128]{3,2,1,0:T(8,128)S(1)}, f32[10,6,8,128]{3,2,1,0:T(8,128)S(1)}, f32[5,6,8,128]{3,2,1,0:T(8,128)S(1)}, f32[5,6,8,128]{3,2,1,0:T(8...) custom-call(f32[4,6,8,384]{3,2,1,0:T(8,128)} %flow.1, ...), custom_call_target="tpu_custom_call" | custom-call | tf_op jit(solution)/shard_map/pallas_call | solution.py:637
  1.9 0.1 collective-permute-start
  1.9 8.1 %collective-permute-start.1 = (f32[10,6,8,128]{3,2,1,0:T(8,128)S(1)}, f32[10,6,8,128]{3,2,1,0:T(8,128)S(1)}, u32[]{:S(2)}, u32[]{:S(2)}) collective-permute-start(f32[10,6,8,128]{3,2,1,0:T(8,128)S(1)} %get-tuple-element.41), channel_id=1, source_target_pairs={{255,254},{0,255},{1,0},{2,1},{3,2},{4,3},{5,4},{6,5},{7,6},{8,7},... | collective-permute-start | bytes 737288 | tf_op jit(solution)/shard_map/ppermute | solution.py:682
  10.0 0.0 collective-permute-start.4
  10.0 6.0 %collective-permute-start.5 = (f32[5,6,8,128]{3,2,1,0:T(8,128)S(1)}, f32[5,6,8,128]{3,2,1,0:T(8,128)S(1)}, u32[]{:S(2)}, u32[]{:S(2)}) collective-permute-start(f32[5,6,8,128]{3,2,1,0:T(8,128)S(1)} %get-tuple-element.47), channel_id=1, source_target_pairs={{255,62},{0,1},{1,0},{2,3},{3,2},{4,5},{5,4},{6,7},{7,6},{8,9},{9,... | collective-permute-start | bytes 368648 | tf_op jit(solution)/shard_map/ppermute | solution.py:678
  16.0 0.7 %copy-done = f32[16,16]{1,0:T(8,128)S(1)} copy-done((f32[16,16]{1,0:T(8,128)S(1)}, f32[16,16]{1,0:T(8,128)}, u32[]{:S(2)}) %copy-start) | copy-done | bytes 1048
  16.7 0.9 %shard_map.103 = (s32[3,24,128]{2,1,0:T(8,128)S(1)}, f32[16,16,128]{2,1,0:T(8,128)S(1)}) custom-call(s32[512,384]{1,0:T(8,128)} %ocean.1, s32[512,384]{1,0:T(8,128)} %bottom.1, f32[16,16]{1,0:T(8,128)S(1)} %copy-done), custom_call_target="tpu_custom_call" | custom-call | tf_op jit(solution)/shard_map/pallas_call | solution.py:637
  17.6 0.0 collective-permute-done.above
  17.6 0.0 collective-permute-done.1.below
  17.6 0.1 collective-permute-start.3
  17.7 0.5 %collective-permute-start.2 = (f32[6,16,128]{2,1,0:T(8,128)S(1)}, f32[6,16,128]{2,1,0:T(8,128)S(1)}, u32[]{:S(2)}, u32[]{:S(2)}) collective-permute-start(f32[6,16,128]{2,1,0:T(8,128)S(1)} %get-tuple-element.43), channel_id=1, source_target_pairs={{255,62},{0,1},{1,0},{2,3},{3,2},{4,5},{5,4},{6,7},{7,6},{8,9},{9,... | collective-permute-start | bytes 147464 | tf_op jit(solution)/shard_map/ppermute | solution.py:671
  18.2 0.3 collective-permute-done.4.more_above
  18.6 0.0 collective-permute-done.5.more_below
  18.6 2.5 %shard_map.105 = (f32[21,8,128]{2,1,0:T(8,128)S(1)}, f32[21,8,128]{2,1,0:T(8,128)S(1)}, f32[21,8,128]{2,1,0:T(8,128)S(1)}, f32[4,6,3,32,128]{4,3,2,1,0:T(8,128)S...) custom-call(f32[4,6,3,8,128]{4,3,2,1,0:T(8,128)S(1)} %get-tuple-element.44.flow, ...), custom_call_target="tpu_custom_call" | custom-call | tf_op jit(solution)/shard_map/pallas_call | solution.py:637
  21.0 0.0 collective-permute-done.3.inner
  21.0 0.0 collective-permute-done.2.outer
  21.1 0.1 collective-permute-start.6
  21.2 1.8 %collective-permute-start.7 = (f32[21,8,128]{2,1,0:T(8,128)S(1)}, f32[21,8,128]{2,1,0:T(8,128)S(1)}, u32[]{:S(2)}, u32[]{:S(2)}) collective-permute-start(f32[21,8,128]{2,1,0:T(8,128)S(1)} %get-tuple-element.58), channel_id=1, source_target_pairs={{255,62},{0,1},{1,0},{2,3},{3,2},{4,5},{5,4},{6,7},{7,6},{8,9},{9,... | collective-permute-start | bytes 258056 | tf_op jit(solution)/shard_map/ppermute | solution.py:671
  22.9 0.0 collective-permute-start.8
  23.0 0.4 %shard_map.107 = (f32[4,6,3,32,128]{4,3,2,1,0:T(8,128)S(1)}, f32[16,6,16,128]{3,2,1,0:T(8,128)S(1)}) custom-call(f32[4,6,3,32,128]{4,3,2,1,0:T(8,128)S(1)} %get-tuple-element.60.flow_next, s32[3,24,128]{2,1,0:T(8,128)S(1)} %get-tuple-element.42.wet_rows, f32[16,6,16,128]{3,2,1,0:T(8,128)S(1)} %get-tuple-element.54.partial, ...), custom_call_target="tpu_custom_call" | custom-call | tf_op jit(solution)/shard_map/pallas_call | solution.py:637
  23.4 5.0 %collective-permute-done.6.from_a = f32[21,8,128]{2,1,0:T(8,128)S(1)} collective-permute-done((f32[21,8,128]{2,1,0:T(8,128)S(1)}, f32[21,8,128]{2,1,0:T(8,128)S(1)}, u32[]{:S(2)}, u32[]{:S(2)}) %collective-permute-start.6) | collective-permute-done | bytes 86048 | tf_op jit(solution)/shard_map/ppermute | solution.py:671
  28.4 0.0 collective-permute-done.7.from_b
  28.4 0.0 collective-permute-done.8.from_c
  28.4 1.2 %shard_map.108 = (f32[24,8,128]{2,1,0:T(8,128)S(1)}, f32[24,8,128]{2,1,0:T(8,128)S(1)}, f32[24,8,128]{2,1,0:T(8,128)S(1)}, f32[4,6,3,8,128]{4,3,2,1,0:T(8,128)S(1)}, f32[16,6,8,128]{3,2,1,0:T(8,128)S(1)}) custom-call(f32[21,8,128]{2,1,0:T(8,128)S(1)} %collective-permute-done.6.from_a, f32[21,8,128]{2,1,0:T(8,128)S(1)} %collective-permute-done.7.from_b, ...), custom_call_target="tpu_custom_call" | custom-call | tf_op jit(solution)/shard_map/pallas_call | solution.py:637
  29.6 1.1 %collective-permute-start.9 = (f32[24,8,128]{2,1,0:T(8,128)S(1)}, f32[24,8,128]{2,1,0:T(8,128)S(1)}, u32[]{:S(2)}, u32[]{:S(2)}) collective-permute-start(f32[24,8,128]{2,1,0:T(8,128)S(1)} %get-tuple-element.66), channel_id=1, source_target_pairs={{255,191},{0,192},{1,193},{2,194},{3,195},{4,196},{5,197},{6,198},... | collective-permute-start | bytes 294920 | tf_op jit(solution)/shard_map/ppermute | solution.py:671
  30.7 0.0 collective-permute-start.10
  30.7 0.1 collective-permute-start.11
  30.8 0.9 %shard_map.109 = (f32[4,6,8,384]{3,2,1,0:T(8,128)}, f32[16,6,8,128]{3,2,1,0:T(8,128)}) custom-call(f32[4,6,3,8,128]{4,3,2,1,0:T(8,128)S(1)} %get-tuple-element.63.flow_last, f32[16,6,8,128]{3,2,1,0:T(8,128)S(1)} %get-tuple-element.64.tracers_last), custom_call_target="tpu_custom_call" | custom-call | tf_op jit(solution)/shard_map/pallas_call | solution.py:637
  31.7 5.7 %collective-permute-done.9.from_a = f32[24,8,128]{2,1,0:T(8,128)S(1)} collective-permute-done((f32[24,8,128]{2,1,0:T(8,128)S(1)}, f32[24,8,128]{2,1,0:T(8,128)S(1)}, u32[]{:S(2)}, u32[]{:S(2)}) %collective-permute-start.9) | collective-permute-done | bytes 98336 | tf_op jit(solution)/shard_map/ppermute | solution.py:671
  37.4 0.0 collective-permute-done.10.from_c
  37.4 0.0 collective-permute-done.11.from_b
  37.4 0.7 %shard_map.110 = (f32[6,8,384]{2,1,0:T(8,128)}, f32[4,6,8,128]{3,2,1,0:T(8,128)}) custom-call(f32[24,8,128]{2,1,0:T(8,128)S(1)} %collective-permute-done.9.from_a, f32[24,8,128]{2,1,0:T(8,128)S(1)} %collective-permute-done.10.from_c, f32[24,8,128]{2,1,0:T(8,128)S(1)} %collective-permute-done.11.from_b), custom_call_target="tpu_custom_call" | custom-call | tf_op jit(solution)/shard_map/pallas_call | solution.py:637
  (3 shorter events, 0.1 us)
Async XLA Ops:
  1.9 15.7 %collective-permute-start = (f32[10,6,8,128]{3,2,1,0:T(8,128)S(1)}, f32[10,6,8,128]{3,2,1,0:T(8,128)S(1)}, u32[]{:S(2)}, u32[]{:S(2)}) collective-permute-start(f32[10,6,8,128]{3,2,1,0:T(8,128)S(1)} %get-tuple-element.40), channel_id=1, source_target_pairs={{255,0},{0,1},{1,2},{2,3},{3,4},{4,5},{5,6},{6,7},{7,8},{8,9},{9,1... | collective-permute-start | bytes 737288 | tf_op jit(solution)/shard_map/ppermute | solution.py:682
  1.9 15.6 %collective-permute-start.1 = (f32[10,6,8,128]{3,2,1,0:T(8,128)S(1)}, f32[10,6,8,128]{3,2,1,0:T(8,128)S(1)}, u32[]{:S(2)}, u32[]{:S(2)}) collective-permute-start(f32[10,6,8,128]{3,2,1,0:T(8,128)S(1)} %get-tuple-element.41), channel_id=1, source_target_pairs={{255,254},{0,255},{1,0},{2,1},{3,2},{4,3},{5,4},{6,5},{7,6},{8,7},... | collective-permute-start | bytes 737288 | tf_op jit(solution)/shard_map/ppermute | solution.py:682
  10.0 8.5 %collective-permute-start.4 = (f32[5,6,8,128]{3,2,1,0:T(8,128)S(1)}, f32[5,6,8,128]{3,2,1,0:T(8,128)S(1)}, u32[]{:S(2)}, u32[]{:S(2)}) collective-permute-start(f32[5,6,8,128]{3,2,1,0:T(8,128)S(1)} %get-tuple-element.46), channel_id=1, source_target_pairs={{255,62},{0,1},{1,0},{2,3},{3,2},{4,5},{5,4},{6,7},{7,6},{8,9},{9,... | collective-permute-start | bytes 368648 | tf_op jit(solution)/shard_map/ppermute | solution.py:678
  10.0 8.5 %collective-permute-start.5 = (f32[5,6,8,128]{3,2,1,0:T(8,128)S(1)}, f32[5,6,8,128]{3,2,1,0:T(8,128)S(1)}, u32[]{:S(2)}, u32[]{:S(2)}) collective-permute-start(f32[5,6,8,128]{3,2,1,0:T(8,128)S(1)} %get-tuple-element.47), channel_id=1, source_target_pairs={{255,62},{0,1},{1,0},{2,3},{3,2},{4,5},{5,4},{6,7},{7,6},{8,9},{9,... | collective-permute-start | bytes 368648 | tf_op jit(solution)/shard_map/ppermute | solution.py:678
  16.0 0.7 %copy-start = (f32[16,16]{1,0:T(8,128)S(1)}, f32[16,16]{1,0:T(8,128)}, u32[]{:S(2)}) copy-start(f32[16,16]{1,0:T(8,128)} %reaction.1) | copy-start | bytes 3076
  17.6 3.4 %collective-permute-start.3 = (f32[6,16,128]{2,1,0:T(8,128)S(1)}, f32[6,16,128]{2,1,0:T(8,128)S(1)}, u32[]{:S(2)}, u32[]{:S(2)}) collective-permute-start(f32[6,16,128]{2,1,0:T(8,128)S(1)} %get-tuple-element.43), channel_id=1, source_target_pairs={{255,63},{0,64},{1,65},{2,66},{3,67},{4,68},{5,69},{6,70},{7,71},{... | collective-permute-start | bytes 147464 | tf_op jit(solution)/shard_map/ppermute | solution.py:671
  17.7 3.3 %collective-permute-start.2 = (f32[6,16,128]{2,1,0:T(8,128)S(1)}, f32[6,16,128]{2,1,0:T(8,128)S(1)}, u32[]{:S(2)}, u32[]{:S(2)}) collective-permute-start(f32[6,16,128]{2,1,0:T(8,128)S(1)} %get-tuple-element.43), channel_id=1, source_target_pairs={{255,62},{0,1},{1,0},{2,3},{3,2},{4,5},{5,4},{6,7},{7,6},{8,9},{9,... | collective-permute-start | bytes 147464 | tf_op jit(solution)/shard_map/ppermute | solution.py:671
  21.1 7.4 %collective-permute-start.6 = (f32[21,8,128]{2,1,0:T(8,128)S(1)}, f32[21,8,128]{2,1,0:T(8,128)S(1)}, u32[]{:S(2)}, u32[]{:S(2)}) collective-permute-start(f32[21,8,128]{2,1,0:T(8,128)S(1)} %get-tuple-element.57), channel_id=1, source_target_pairs={{255,191},{0,192},{1,193},{2,194},{3,195},{4,196},{5,197},{6,198},... | collective-permute-start | bytes 258056 | tf_op jit(solution)/shard_map/ppermute | solution.py:671
  21.2 7.3 %collective-permute-start.7 = (f32[21,8,128]{2,1,0:T(8,128)S(1)}, f32[21,8,128]{2,1,0:T(8,128)S(1)}, u32[]{:S(2)}, u32[]{:S(2)}) collective-permute-start(f32[21,8,128]{2,1,0:T(8,128)S(1)} %get-tuple-element.58), channel_id=1, source_target_pairs={{255,62},{0,1},{1,0},{2,3},{3,2},{4,5},{5,4},{6,7},{7,6},{8,9},{9,... | collective-permute-start | bytes 258056 | tf_op jit(solution)/shard_map/ppermute | solution.py:671
  22.9 5.5 %collective-permute-start.8 = (f32[21,8,128]{2,1,0:T(8,128)S(1)}, f32[21,8,128]{2,1,0:T(8,128)S(1)}, u32[]{:S(2)}, u32[]{:S(2)}) collective-permute-start(f32[21,8,128]{2,1,0:T(8,128)S(1)} %get-tuple-element.59), channel_id=1, source_target_pairs={{255,63},{0,64},{1,65},{2,66},{3,67},{4,68},{5,69},{6,70},{7,71},{... | collective-permute-start | bytes 258056 | tf_op jit(solution)/shard_map/ppermute | solution.py:671
  29.6 7.8 %collective-permute-start.9 = (f32[24,8,128]{2,1,0:T(8,128)S(1)}, f32[24,8,128]{2,1,0:T(8,128)S(1)}, u32[]{:S(2)}, u32[]{:S(2)}) collective-permute-start(f32[24,8,128]{2,1,0:T(8,128)S(1)} %get-tuple-element.66), channel_id=1, source_target_pairs={{255,191},{0,192},{1,193},{2,194},{3,195},{4,196},{5,197},{6,198},... | collective-permute-start | bytes 294920 | tf_op jit(solution)/shard_map/ppermute | solution.py:671
  30.7 6.7 %collective-permute-start.10 = (f32[24,8,128]{2,1,0:T(8,128)S(1)}, f32[24,8,128]{2,1,0:T(8,128)S(1)}, u32[]{:S(2)}, u32[]{:S(2)}) collective-permute-start(f32[24,8,128]{2,1,0:T(8,128)S(1)} %get-tuple-element.67), channel_id=1, source_target_pairs={{255,62},{0,1},{1,0},{2,3},{3,2},{4,5},{5,4},{6,7},{7,6},{8,9},{9,... | collective-permute-start | bytes 294920 | tf_op jit(solution)/shard_map/ppermute | solution.py:671
  30.7 6.7 %collective-permute-start.11 = (f32[24,8,128]{2,1,0:T(8,128)S(1)}, f32[24,8,128]{2,1,0:T(8,128)S(1)}, u32[]{:S(2)}, u32[]{:S(2)}) collective-permute-start(f32[24,8,128]{2,1,0:T(8,128)S(1)} %get-tuple-element.68), channel_id=1, source_target_pairs={{255,62},{0,1},{1,0},{2,3},{3,2},{4,5},{5,4},{6,7},{7,6},{8,9},{9,... | collective-permute-start | bytes 294920 | tf_op jit(solution)/shard_map/ppermute | solution.py:671
